TPU v7x, 32 devices: a whole 2x2x4 slice. The times are simulated.
32 devices in a mesh: dp: 4 (over y, x), mp: 8 (over z, core).
Axes of the slice: x: 2, y: 2, z: 4, core: 2. Of those that a mesh axis runs over, the one named last changes fastest.
Arguments:
- tokens: bfloat16 [4096, 1024], P('dp'), may hold values from -6 to 6
- states: bfloat16 [8, 128, 1024], P('dp'), may hold values from -6 to 6
- cotangent: bfloat16 [4096, 1024], P('dp'), may hold values from -6 to 6
- self_weight: bfloat16 [3, 1024, 1024], P(None, None, 'mp'), may hold values from -0.1875 to 0.1875
- self_output: bfloat16 [1024, 1024], P('mp'), may hold values from -1 to 1
- cross_query: bfloat16 [1024, 1024], P(None, 'mp'), may hold values from -0.1875 to 0.1875
- cross_pair: bfloat16 [2, 1024, 1024], P(None, None, 'mp'), may hold values from -0.1875 to 0.1875
- cross_output: bfloat16 [1024, 1024], P('mp'), may hold values from -0.5 to 0.5
- hidden_weight: bfloat16 [1024, 4096], P(None, 'mp'), may hold values from -0.1875 to 0.1875
- hidden_bias: bfloat16 [4096], P('mp'), may hold values from -3 to 3
- output_weight: bfloat16 [4096, 1024], P('mp'), may hold values from -0.09375 to 0.09375
- output_bias: bfloat16 [1024], replicated, may hold values from -3 to 3
- norm_gain: bfloat16 [3, 1024], replicated, may hold values from 0.5 to 1.5
- norm_shift: bfloat16 [3, 1024], replicated, may hold values from -2 to 2
- state_row: int32 [4], P('dp'), may hold values from 0 to 1
- state_segment: int32 [8, 128], P('dp'), may hold values from 0 to 3, never falling along the last dimension, each value on 1 to 64 neighbouring positions
- caption: int32 [4], P('dp'), may hold values from 0 to 3
Outputs:
- block_output: bfloat16 [4096, 1024], P(('dp', 'mp'))
- grad_tokens: float32 [4096, 1024], P(('dp', 'mp'))
- grad_states: float32 [8, 128, 1024], P('dp')
- grad_self_weight: float32 [3, 1024, 1024], P(None, None, 'mp')
- grad_self_output: float32 [1024, 1024], P('mp')
- grad_cross_query: float32 [1024, 1024], P(None, 'mp')
- grad_cross_pair: float32 [2, 1024, 1024], P(None, None, 'mp')
- grad_cross_output: float32 [1024, 1024], P('mp')
- grad_hidden_weight: float32 [1024, 4096], P(None, 'mp')
- grad_hidden_bias: float32 [4096], P('mp')
- grad_output_weight: float32 [4096, 1024], P('mp')
- grad_output_bias: float32 [1024], replicated
- grad_norm_gain: float32 [3, 1024], replicated
- grad_norm_shift: float32 [3, 1024], replicated
Inputs may be any that keep to these rules, and one draw needn't show every extreme that they name: `state_segment`: in each encoder row the caption numbers never fall, and every caption 0 to 3 holds 1 to 64 states.
All inputs are finite; a program needn't handle non-finite values.
Results may differ from a plain program's by a relative error of at most 0.025.
Values may be sent and summed in bfloat16 or wider, within the bound.
No kernel may reach another device: no remote copies, remote signals or barrier semaphores. Data moves between devices by JAX's collectives and lax.ppermute only.
A program may use at most 128 MiB of HBM per device.

v0:
```python
import functools
import math

import jax
import jax.numpy as jnp
from jax import lax
from jax.experimental import pallas as pl
from jax.experimental.pallas import tpu as pltpu
from jax.sharding import PartitionSpec as P

HDIM = 64
SEEN = 64
QB = 256
PAD = 16
EPSILON = 1e-05
NEG_FILL = -1e30
SCALE = HDIM ** (-0.5)
F32 = jnp.float32
BF16 = jnp.bfloat16


def dot_nn(a, b):
    return lax.dot_general(a, b, (((1,), (0,)), ((), ())), preferred_element_type=F32)


def dot_nt(a, b):
    return lax.dot_general(a, b, (((1,), (1,)), ((), ())), preferred_element_type=F32)


def dot_tn(a, b):
    return lax.dot_general(a, b, (((0,), (0,)), ((), ())), preferred_element_type=F32)


def normalize(resid):
    center = resid - jnp.mean(resid, -1, keepdims=True)
    inverse = lax.rsqrt(jnp.mean(center * center, -1, keepdims=True) + EPSILON)
    return (center * inverse, inverse)


def norm_backward(standard, inverse, grad_normed, gain):
    scaled = grad_normed * gain
    return inverse * (
        scaled
        - jnp.mean(scaled, -1, keepdims=True)
        - standard * jnp.mean(scaled * standard, -1, keepdims=True)
    )


def at(index, size):
    return pl.ds(pl.multiple_of(index * size, size), size)


def staged(kernel, ins, outs, extra, *refs):
    count_in, count_out = len(ins), len(outs)
    idx, refs = refs[0], list(refs[1:])
    inner = refs[: count_in + count_out]
    own = refs[count_in + count_out : count_in + count_out + extra]
    rest = refs[count_in + count_out + extra :]
    sem_in, sem_out = rest[-2:]
    held = iter(rest[:-2])
    started, results = [], []
    for i, here in enumerate(ins):
        if here:
            local = next(held)
            started.append(pltpu.make_async_copy(inner[i], local, sem_in.at[len(started)]))
            inner[i] = local
    for i, here in enumerate(outs):
        if here:
            local = next(held)
            target = inner[count_in + i]
            results.append(pltpu.make_async_copy(local, target, sem_out.at[len(results)]))
            inner[count_in + i] = local
    for copy in started:
        copy.start()
    for copy in started:
        copy.wait()
    kernel(idx, *inner, *own)
    for copy in results:
        copy.start()
    for copy in results:
        copy.wait()


def call(
    kernel, outs, idx, *args, scratch=(), after=(), stage=False, tight=False, raw=(), cost=1, name=None, spill=8
):
    if after:
        idx = lax.optimization_barrier((idx, *after))[0]
    out_shape = [jax.ShapeDtypeStruct(s, t) for s, t in outs]
    big = lambda a: bool(stage) and a.size >= 1 << 15
    ins_far = [big(a) and i not in raw for i, a in enumerate(args)]
    outs_far = [big(a) for a in out_shape]
    vmem = pl.BlockSpec(memory_space=pltpu.VMEM)
    hbm = pl.BlockSpec(memory_space=pltpu.HBM)
    held = spill << 20
    for i, a in enumerate((*args, *out_shape)):
        if i not in raw:
            held += a.size * a.dtype.itemsize
    for a in scratch:
        if len(getattr(a, "shape", ())) > 1 and a.dtype in (F32, BF16):
            held += math.prod(a.shape) * jnp.dtype(a.dtype).itemsize
    scratch = list(scratch)
    if any(ins_far) or any(outs_far):
        kernel = functools.partial(staged, kernel, ins_far, outs_far, len(scratch))
        for a, far in zip((*args, *out_shape), ins_far + outs_far):
            if far:
                scratch.append(pltpu.VMEM(a.shape, a.dtype))
        scratch.append(pltpu.SemaphoreType.DMA((max(1, sum(ins_far)),)))
        scratch.append(pltpu.SemaphoreType.DMA((max(1, sum(outs_far)),)))
    return pl.pallas_call(
        kernel,
        out_shape=out_shape,
        in_specs=[pl.BlockSpec(memory_space=pltpu.SMEM)]
        + [hbm if far or i in raw else vmem for i, far in enumerate(ins_far)],
        out_specs=[hbm if far else vmem for far in outs_far],
        scratch_shapes=scratch,
        cost_estimate=pl.CostEstimate(flops=cost, bytes_accessed=1, transcendentals=0),
        compiler_params=pltpu.CompilerParams(
            vmem_limit_bytes=min(held, 60 << 20) if tight else 60 << 20
        ),
        name=name,
    )(idx, *args)


def head_select(parts, axis):
    if len(parts) == 1:
        return parts[0]
    head = lax.broadcasted_iota(jnp.int32, parts[0].shape, axis) // HDIM
    return jnp.where(head == 0, parts[0], parts[1])


def head_only(value, h, count):
    if count == 1:
        return value
    head = lax.broadcasted_iota(jnp.int32, value.shape, 1) // HDIM
    return jnp.where(head == h, value, jnp.zeros_like(value))


def self_kernel(
    chips, idx, tok, weight, gain, shift, states, pair, segment, normed, triple, probs, *rest
):
    att_out = rest[:chips]
    val_t, att, kv = rest[chips:]
    rows, width = tok.shape[0], weight.shape[2]
    heads = width // HDIM
    g = gain[0:1, :].astype(F32)
    s = shift[0:1, :].astype(F32)

    def project(i, carry):
        here = at(i, QB)
        standard, _ = normalize(tok[here, :].astype(F32))
        n = (standard * g + s).astype(BF16)
        normed[here, :] = n
        triple[0, here, :] = dot_nn(n, weight[0]).astype(BF16)
        triple[1, here, :] = dot_nn(n, weight[1]).astype(BF16)
        value = dot_nn(n, weight[2])
        triple[2, here, :] = value.astype(BF16)
        val_t[:, here] = value.T.astype(BF16)
        return carry

    lax.fori_loop(0, rows // QB, project, 0)
    for i in range(rows // QB):
        here = slice(i * QB, (i + 1) * QB)
        query = triple[0, here, :]
        seen = (i + 1) * QB
        outs = []
        for h in range(heads):
            scores = dot_nt(triple[1, 0:seen, :], head_only(query, h, heads)) * SCALE
            key_at = lax.broadcasted_iota(jnp.int32, scores.shape, 0)
            row_at = lax.broadcasted_iota(jnp.int32, scores.shape, 1) + i * QB
            scores = jnp.where(key_at <= row_at, scores, NEG_FILL)
            e = jnp.exp(scores - jnp.max(scores, 0, keepdims=True))
            p = (e * (1.0 / jnp.sum(e, 0, keepdims=True))).astype(BF16)
            probs[h, 0:seen, here] = p
            outs.append(dot_nn(val_t[:, 0:seen], p))
        att[here, :] = head_select(outs, 0).T.astype(BF16)
    own = (att_out[0].shape[0] - 2 * SEEN) // 2
    before = segment[pl.ds(idx[2], 1), :] < idx[3]
    begin = jnp.minimum(jnp.sum(before.astype(jnp.int32)), states.shape[1] - SEEN)
    for c in range(2):
        kv[...] = dot_nn(states[idx[2]], pair[c])
        for k in range(chips):
            where = slice(2 * own + c * SEEN, 2 * own + (c + 1) * SEEN)
            att_out[k][where, :] = kv[pl.ds(begin, SEEN), :].astype(BF16)
    for k in range(chips):
        for cc in range(2):
            att_out[k][cc * own : (cc + 1) * own, :] = att[at(idx[0] ^ (2 * k + cc), own), :]


def pair_tiles(block, heads):
    return jnp.concatenate([head_only(block, h, heads) for h in range(heads)], 0)


def half_reduce(op, value, heads, fill):
    if heads == 1:
        return op(value, -1, keepdims=True)
    half = lax.broadcasted_iota(jnp.int32, value.shape, 1) // SEEN
    first = op(jnp.where(half == 0, value, fill), -1, keepdims=True)
    other = op(jnp.where(half == 1, value, fill), -1, keepdims=True)
    return jnp.where(half == 0, first, other)


def fetch_weights(chips, dps, idx, weights, wf, sem):
    width = wf.shape[1] // (2 * chips)
    cut = wf.shape[2] // dps
    span = (chips - 1) * width
    half = chips * width
    lists = []
    for m in range(3):
        copies = []
        for cc in range(2):
            source = weights[cc * (dps + 1)]
            where = wf.at[m, cc * half : cc * half + width, :]
            copies.append((source.at[m * width : (m + 1) * width, :], where))
            for q in range(dps):
                source = weights[cc * (dps + 1) + 1 + q]
                cols = at(idx[1] ^ q, cut)
                where = wf.at[m, cc * half + width : (cc + 1) * half, cols]
                copies.append((source.at[m * span : (m + 1) * span, :], where))
        lists.append(
            [pltpu.make_async_copy(s, d, sem.at[m, i]) for i, (s, d) in enumerate(copies)]
        )
    return lists


def own_rows(idx, source, rows, sem):
    copy = pltpu.make_async_copy(source.at[at(idx[0], rows.shape[0]), :], rows, sem)
    copy.start()
    return copy


def cross_kernel(chips, dps, idx, tokens, gain, shift, seen, *rest):
    take = iter(rest)
    pull = lambda n: [next(take) for _ in range(n)]
    weights = pull(2 * dps + 2)
    att_in = [pull(chips), pull(chips)]
    first_o, pack_o, q_o, cp_o, second_o, n3_o = pull(6)
    wf, sem, tok, tok_sem = pull(4)
    fetch = own_rows(idx, tokens, tok, tok_sem)
    own, dim = tok.shape
    width = wf.shape[1] // (2 * chips)
    heads = width // HDIM
    half = chips * width
    copies = fetch_weights(chips, dps, idx, weights, wf, sem)
    for each in copies:
        for copy in each:
            copy.start()
    for k in range(chips):
        pack_o[0, :, k * width : (k + 1) * width] = att_in[0][k][0:own, :]
        pack_o[0, :, half + k * width : half + (k + 1) * width] = att_in[1][k][own : 2 * own, :]
    fetch.wait()
    for copy in copies[0]:
        copy.wait()
    resid = tok[...].astype(F32) + dot_nn(pack_o[0], wf[0])
    first_o[...] = resid
    n2 = (normalize(resid)[0] * gain[1:2, :].astype(F32) + shift[1:2, :].astype(F32)).astype(BF16)
    pack_o[1, :, :] = n2
    for copy in copies[1]:
        copy.wait()
    q_o[...] = dot_nt(n2, wf[1]).astype(BF16)
    allowed = seen[...] > 0
    for cc in range(2):
        for k in range(chips):
            b = cc * chips + k
            lanes = slice(b * width, (b + 1) * width)
            keys = pair_tiles(att_in[cc][k][2 * own : 2 * own + SEEN, :], heads)
            values = pair_tiles(att_in[cc][k][2 * own + SEEN :, :], heads)
            scores = dot_nt(q_o[:, lanes], keys) * SCALE
            scores = jnp.where(allowed, scores, NEG_FILL)
            e = jnp.exp(scores - half_reduce(jnp.max, scores, heads, NEG_FILL))
            p = (e * (1.0 / half_reduce(jnp.sum, e, heads, 0.0))).astype(BF16)
            cp_o[b] = p
            pack_o[2, :, lanes] = dot_nn(p, values).astype(BF16)
    for copy in copies[2]:
        copy.wait()
    resid = resid + dot_nn(pack_o[2], wf[2])
    second_o[...] = resid
    n3 = normalize(resid)[0] * gain[2:3, :].astype(F32) + shift[2:3, :].astype(F32)
    n3_o[...] = n3.astype(BF16)


def active_kernel(chips, idx, cot, weight, *rest):
    outs, part = rest[:chips], rest[chips]
    rows = outs[0].shape[0]

    def chip(k, carry):
        part[k] = dot_nt(cot[at((idx[0] // 2) ^ k, rows), :], weight[...])
        return carry

    lax.fori_loop(0, chips, chip, 0)
    for k in range(chips):
        outs[k][...] = part[k]


def hidden_kernel(idx, same, other, weight, bias, grad_active, n3_o, act_o, ghi_o, bs_o, bo_o, back):
    own = same.shape[0]
    core = lax.rem(idx[0], 2)
    n3_o[at(core, own), :] = same[...]
    n3_o[at(1 - core, own), :] = other[...]
    v = dot_nn(n3_o[...], weight[...]) + bias[...].astype(F32)
    root = 0.7978845608028654
    square = v * v
    t = jnp.tanh(root * v * (1.0 + 0.044715 * square))
    act_o[...] = (0.5 * v * (1.0 + t)).astype(BF16)
    slope = 0.5 * (1.0 + t) + 0.5 * v * (1.0 - t * t) * (root * (1.0 + 0.134145 * square))
    ghi = (grad_active[...] * slope).astype(BF16)
    ghi_o[...] = ghi
    back[...] = dot_nt(ghi, weight[...])
    bs_o[...] = back[at(core, own), :].astype(BF16)
    dim = back.shape[1]
    bo_o[:, 0:dim] = back[at(1 - core, own), :].astype(BF16)
    bo_o[:, dim:] = act_o[at(1 - core, own), :]


def mlp_out_kernel(chips, idx, weight, weight2, *rest):
    acts, others, outs = rest[:chips], rest[chips : 2 * chips], rest[2 * chips : 3 * chips]
    near, part, sem = rest[3 * chips :]
    own, dim = outs[0].shape
    hid = weight.shape[0]
    mine = at(lax.rem(idx[0], 2), own)
    copies = []
    for k in range(chips):
        sources = acts[k].at[mine, :], others[k].at[:, dim : dim + hid]
        for c, source in enumerate(sources):
            copies.append(pltpu.make_async_copy(source, near.at[c, k], sem.at[c, k]))
    for copy in copies:
        copy.start()
    for copy in copies:
        copy.wait()

    def chip(k, carry):
        value = dot_nn(near[0, k], weight[...]) + dot_nn(near[1, k], weight2[...])
        part[k] = value.astype(BF16)
        return carry

    lax.fori_loop(0, chips, chip, 0)
    for k in range(chips):
        outs[k][...] = part[k]


def mlp_grad_kernel(chips, idx, cot, *rest):
    acts = rest[:chips]
    ghis = rest[chips : 2 * chips]
    n3s = rest[2 * chips : 3 * chips]
    out, act, ghi, n3 = rest[3 * chips :]
    step = acts[0].shape[0]
    hid = acts[0].shape[1]
    dps, _, cut = out.shape
    total = jnp.zeros((1, hid), F32)
    for k in range(chips):
        rows = at((idx[0] // 2) ^ k, step)
        act[rows, :] = acts[k][...]
        ghi[rows, :] = ghis[k][...]
        n3[rows, :] = n3s[k][...]
        total += jnp.sum(ghis[k][...].astype(F32), 0, keepdims=True)
    row = lax.broadcasted_iota(jnp.int32, (PAD, cut), 0)
    bias = jnp.zeros((PAD, cut), F32)
    for j in range(hid // cut):
        bias = jnp.where(row == j, total[:, j * cut : (j + 1) * cut], bias)
    def columns(q, carry):
        cols = at(q, cut)
        out[q, 0:hid, :] = dot_tn(act[...], cot[:, cols]).astype(BF16)
        out[q, hid : 2 * hid, :] = dot_tn(ghi[...], n3[:, cols]).astype(BF16)
        out[q, 2 * hid : 2 * hid + PAD, :] = bias.astype(BF16)
        return carry

    lax.fori_loop(0, dps, columns, 0)


def cross_back_kernel(chips, dps, count, idx, cotangent, gain, second, first, cp, q, *rest):
    take = iter(rest)
    pull = lambda n: [next(take) for _ in range(n)]
    weights = pull(2 * dps + 2)
    parts = pull(count)
    kv = [pull(chips), pull(chips)]
    pack_o, gf_o, stat_o, same_o, other_o = pull(5)
    gt_o = pull(chips)
    gc, wf, sem, cot, cot_sem = pull(5)
    fetch = own_rows(idx, cotangent, cot, cot_sem)
    copies = fetch_weights(chips, dps, idx, weights, wf, sem)
    for each in reversed(copies):
        for copy in each:
            copy.start()
    dkv_o = (same_o, other_o)
    own = cot.shape[0]
    width = kv[0][0].shape[1]
    heads = width // HDIM
    grad_normed = parts[0][...].astype(F32)
    for part in parts[1:]:
        grad_normed += part[...].astype(F32)
    fetch.wait()
    c = cot[...].astype(F32)
    standard, inverse = normalize(second[...])
    grad = c + norm_backward(standard, inverse, grad_normed, gain[2:3, :].astype(F32))
    stat_o[0:1, :] = jnp.sum(grad_normed * standard, 0, keepdims=True)
    stat_o[1:2, :] = jnp.sum(grad_normed, 0, keepdims=True)
    stat_o[4:5, :] = jnp.sum(c, 0, keepdims=True)
    g2 = grad.astype(BF16)
    pack_o[2, :, :] = g2
    for copy in copies[2]:
        copy.wait()
    gc[...] = dot_nt(g2, wf[2]).astype(BF16)
    for cc in range(2):
        for k in range(chips):
            b = cc * chips + k
            lanes = slice(b * width, (b + 1) * width)
            keys = pair_tiles(kv[cc][k][2 * own : 2 * own + SEEN, :], heads)
            values = pair_tiles(kv[cc][k][2 * own + SEEN :, :], heads)
            gcb = gc[:, lanes]
            dp = dot_nt(gcb, values)
            low = cp[b]
            p = low.astype(F32)
            inner = half_reduce(jnp.sum, dp * p, heads, 0.0)
            ds = (p * (dp - inner) * SCALE).astype(BF16)
            pack_o[1, :, lanes] = dot_nn(ds, keys).astype(BF16)
            dk = dot_tn(ds, q[:, lanes])
            dv = dot_tn(low, gcb)
            for i, d in enumerate((dk, dv)):
                fold = head_select([d[h * SEEN : (h + 1) * SEEN, :] for h in range(heads)], 1)
                dkv_o[cc][k, i, :, :] = fold.astype(BF16)
    for copy in copies[1]:
        copy.wait()
    grad_normed = dot_nn(pack_o[1], wf[1])
    standard, inverse = normalize(first[...])
    grad = grad + norm_backward(standard, inverse, grad_normed, gain[1:2, :].astype(F32))
    stat_o[2:3, :] = jnp.sum(grad_normed * standard, 0, keepdims=True)
    stat_o[3:4, :] = jnp.sum(grad_normed, 0, keepdims=True)
    gf_o[...] = grad
    g1 = grad.astype(BF16)
    pack_o[0, :, :] = g1
    for copy in copies[0]:
        copy.wait()
    gatt = dot_nt(g1, wf[0]).astype(BF16)
    for cc in range(2):
        for k in range(chips):
            b = cc * chips + k
            gt_o[k][cc, :, :] = gatt[:, b * width : (b + 1) * width]


def row_grad_kernel(chips, idx, fwd, fwd2, bwd, bwd2, out, left, right):
    dps, height, cut = out.shape
    width = height // (3 * chips)
    own = fwd.shape[1]
    half = chips * width
    for m, (l, r) in enumerate((((fwd, fwd2), (bwd, bwd2)), ((bwd, bwd2), (fwd, fwd2)), ((fwd, fwd2), (bwd, bwd2)))):
        left[0:own, :] = l[0][m, :, 0:half]
        left[own : 2 * own, :] = l[1][m, :, half : 2 * half]
        right[0:own, :] = r[0][m]
        right[own : 2 * own, :] = r[1][m]
        for q in range(dps):
            part = dot_tn(left[...], right[:, q * cut : (q + 1) * cut]).astype(BF16)
            for k in range(chips):
                row = (3 * k + m) * width
                out[q, row : row + width, :] = part[k * width : (k + 1) * width, :]


def pack_kernel(idx, *refs):
    parts, out = refs[:-1], refs[-1]
    width = parts[0].shape[0] // 3
    for m in range(3):
        for k, part in enumerate(parts):
            row = (m * len(parts) + k) * width
            out[row : row + width, :] = part[m * width : (m + 1) * width, :]


def self_back_kernel(chips, idx, triple, probs, weight, *rest):
    take = iter(rest)
    pull = lambda n: [next(take) for _ in range(n)]
    grads = [pull(chips), pull(chips)]
    (gt_o,) = pull(1)
    bs_o, bo_o = pull(chips), pull(chips)
    gout, key_t, wcat, dq, dk, dv, back = pull(7)
    rows, width = triple.shape[1], triple.shape[2]
    heads = width // HDIM
    own = bs_o[0].shape[0]
    for k in range(chips):
        gout[at(idx[0] ^ (2 * k), own), :] = grads[0][k][0]
        gout[at(idx[0] ^ (2 * k + 1), own), :] = grads[1][k][1]
    for c in range(3):
        wcat[:, c * width : (c + 1) * width] = weight[c]
    count = rows // QB
    for i in range(count):
        here = slice(i * QB, (i + 1) * QB)
        key_t[:, here] = triple[1, here, :].astype(F32).T.astype(BF16)
    dk[...] = jnp.zeros(dk.shape, F32)
    dv[...] = jnp.zeros(dv.shape, F32)

    def one_head(h, carry):
        for i in reversed(range(count)):
            here = slice(i * QB, (i + 1) * QB)
            seen = (i + 1) * QB
            go = head_only(gout[here, :], h, heads)
            query = head_only(triple[0, here, :], h, heads)
            dp = dot_nt(triple[2, 0:seen, :], go)
            low = probs[h, 0:seen, here]
            p = low.astype(F32)
            inner = jnp.sum(dp * p, 0, keepdims=True)
            ds = (p * (dp - inner) * SCALE).astype(BF16)
            dk[0:seen, :] += dot_nn(ds, query)
            dv[0:seen, :] += dot_nn(low, go)
            new_q = dot_nn(key_t[:, 0:seen], ds)
            head = lax.broadcasted_iota(jnp.int32, new_q.shape, 0) // HDIM
            dq[:, here] = jnp.where(head == h, new_q, dq[:, here])
        return carry

    lax.fori_loop(0, heads, one_head, 0)
    for i in range(count):
        here = slice(i * QB, (i + 1) * QB)
        gt_o[here, 0:width] = dq[:, here].T.astype(BF16)
        gt_o[here, width : 2 * width] = dk[here, :].astype(BF16)
        gt_o[here, 2 * width : 3 * width] = dv[here, :].astype(BF16)

    def project(i, carry):
        back[at(i, QB), :] = dot_nt(gt_o[at(i, QB), :], wcat[...]).astype(BF16)
        return carry

    lax.fori_loop(0, count, project, 0)
    for k in range(chips):
        bs_o[k][...] = back[at(idx[0] ^ (2 * k), own), :]
        bo_o[k][...] = back[at(idx[0] ^ (2 * k + 1), own), :]


def self_grad_kernel(chips, dps, idx, tok, normed, gt, states, gp, stat, *rest):
    parts, (out, held, sem) = rest[: 2 * chips], rest[2 * chips :]
    cut = out.shape[2]
    width = gp.shape[2]
    own = held.shape[1]
    copies = []
    for k in range(chips):
        for cc in range(2):
            j = 2 * k + cc
            copies.append(pltpu.make_async_copy(parts[cc * chips + k], held.at[j], sem.at[j]))
    for copy in copies:
        copy.start()

    def columns(q, carry):
        cols = at(q, cut)
        out[q, 0 : 3 * width, :] = dot_tn(gt[...], normed[:, cols]).astype(BF16)
        for c in range(2):
            out[q, (3 + c) * width : (4 + c) * width, :] = dot_tn(
                gp[c], states[:, cols]
            ).astype(BF16)
        return carry

    lax.fori_loop(0, dps, columns, 0)
    for copy in copies:
        copy.wait()

    def add_rows(j, carry):
        g = held[j].astype(F32)
        standard, _ = normalize(tok[at(idx[0] ^ j, own), :].astype(F32))
        gain = carry[0] + jnp.sum(g * standard, 0, keepdims=True)
        return gain, carry[1] + jnp.sum(g, 0, keepdims=True)

    none = jnp.zeros((1, tok.shape[1]), F32)
    gain, shift = lax.fori_loop(0, 2 * chips, add_rows, (none, none))
    row = lax.broadcasted_iota(jnp.int32, (PAD, tok.shape[1]), 0)
    both = jnp.where(row == 0, gain, jnp.where(row == 1, shift, 0.0))
    for i in range(5):
        both = jnp.where(row == i + 2, stat[i : i + 1, :], both)
    both = both.astype(BF16)
    for q in range(dps):
        for c in range(dps):
            here = slice(5 * width + c * PAD, 5 * width + (c + 1) * PAD)
            out[q, here, :] = both[:, c * cut : (c + 1) * cut]


def add_kernel(idx, *refs):
    count = len(refs) // 3
    for k in range(count):
        total = refs[k][...].astype(F32) + refs[count + k][...].astype(F32)
        refs[2 * count + k][...] = total.astype(BF16)


def sum_kernel(idx, pieces, out):
    step = math.gcd(out.shape[0], 64)

    def add_rows(i, carry):
        here = at(i, step)
        out[here, :] = jnp.sum(pieces[:, here, :].astype(F32), 0).astype(BF16)
        return carry

    lax.fori_loop(0, out.shape[0] // step, add_rows, 0)


def token_kernel(idx, tokens, gain, grad, *rest):
    parts, (out, tok, sem) = rest[:-3], rest[-3:]
    own_rows(idx, tokens, tok, sem).wait()
    grad_normed = parts[0][...].astype(F32)
    for part in parts[1:]:
        grad_normed += part[...].astype(F32)
    standard, inverse = normalize(tok[...].astype(F32))
    out[...] = grad[...] + norm_backward(standard, inverse, grad_normed, gain[0:1, :].astype(F32))


def place_kernel(plan, idx, *refs):
    parts, outs = refs[: -len(plan)], refs[-len(plan) :]
    if len(parts) == 1:
        source = parts[0]
        count, _, cut = source.shape
        take = lambda q, rows: source[q, rows, :]
        where_of = lambda q: slice(q * cut, (q + 1) * cut)
    else:
        count, cut = len(parts), parts[0].shape[1]
        take = lambda q, rows: parts[q][rows, :]
        where_of = lambda q: at(idx[1] ^ q, cut)
    row = 0
    for out, (height, lead, flip) in zip(outs, plan):
        for q in range(count):
            where = where_of(q)
            piece = take(q, slice(row, row + height)).astype(F32)
            if not flip:
                out[:, where] = piece
            elif lead is None:
                out[where, :] = piece.T
            else:
                step = height // lead
                for c in range(lead):
                    out[c, where, :] = piece[c * step : (c + 1) * step, :].T
        row += height


def flip_bits(axis, bits, size):
    return functools.partial(
        lax.ppermute, axis_name=axis, perm=[(i, i ^ bits) for i in range(size)]
    )


def total(*parts):
    out = parts[0].astype(F32)
    for part in parts[1:]:
        out = out + part.astype(F32)
    return out


def body(
    tokens,
    states,
    cotangent,
    self_weight,
    self_output,
    cross_query,
    cross_pair,
    cross_output,
    hidden_weight,
    hidden_bias,
    output_weight,
    output_bias,
    norm_gain,
    norm_shift,
    state_row,
    state_segment,
    caption,
):
    rows, dim = tokens.shape
    width = cross_query.shape[1]
    heads = width // HDIM
    hid = hidden_bias.shape[0]
    cores = lax.axis_size("mp")
    chips = cores // 2
    dps = lax.axis_size("dp")
    own = rows // cores
    cut = dim // dps
    me = lax.axis_index("mp")
    dpi = lax.axis_index("dp")
    idx = jnp.stack([me, dpi, state_row[0], caption[0]]).astype(jnp.int32)
    to_z = [flip_bits("mp", 2 * k, cores) for k in range(chips)]
    to_core = flip_bits("mp", 1, cores)
    to_dp = [flip_bits("dp", q, dps) for q in range(dps)]
    far = range(1, chips)
    peers = range(1, dps)

    def share_dp(piece):
        return lax.all_to_all(jnp.broadcast_to(piece[None], (dps,) + piece.shape), "dp", 0, 0)

    def add_all(left, right, name):
        return list(
            call(
            add_kernel,
            [((own, dim), BF16)] * chips,
            idx,
            *left,
            *right,
            stage=True,
            name=name,
        ))

    def swap_dp(pieces):
        return lax.all_to_all(pieces, "dp", 0, 0)

    def sum_dp(pieces):
        return jnp.sum(pieces.astype(F32), 0).astype(BF16)

    labels = lax.dynamic_index_in_dim(state_segment, state_row[0], 0, False)
    begin = jnp.minimum(jnp.sum((labels < caption[0]).astype(jnp.int32)), labels.shape[0] - SEEN)
    labels = lax.dynamic_slice_in_dim(labels, begin, SEEN, 0)
    seen = jnp.tile((labels == caption[0]).astype(jnp.int32)[None, :], (1, heads))
    near = lax.dynamic_slice(states, (state_row[0], begin, 0), (1, SEEN, dim))[0]

    mine = jnp.concatenate([self_output, cross_query.T, cross_output], 0)
    piece = lax.dynamic_slice_in_dim(mine, dpi * cut, cut, 1)
    got = [to_z[k](piece) for k in far]
    output_weight2 = to_core(output_weight)

    outs = call(
        functools.partial(self_kernel, chips),
        [
            ((rows, dim), BF16),
            ((3, rows, width), BF16),
            ((heads, rows, rows), BF16),
        ]
        + [((2 * own + 2 * SEEN, width), BF16)] * chips,
        idx,
        tokens,
        self_weight,
        norm_gain,
        norm_shift,
        states,
        cross_pair,
        state_segment,
        scratch=[
            pltpu.VMEM((width, rows), BF16),
            pltpu.VMEM((rows, width), BF16),
            pltpu.VMEM((states.shape[1], width), F32),
        ],
        after=(piece,),
        stage=True,
        name="self_fwd",
    )
    normed_one, triple, probs = outs[:3]
    att = outs[3:]
    *got, output_weight2, _ = lax.optimization_barrier((*got, output_weight2, att[0]))
    (cat,) = call(pack_kernel, [((3 * width * (chips - 1), cut), BF16)], idx, *got, tight=True, name="pack")
    att = [att[0]] + [to_z[k](att[k]) for k in far]
    att2 = [to_core(x) for x in att]

    grad_active = call(
        functools.partial(active_kernel, chips),
        [((2 * own, hid), F32)] * chips,
        idx,
        cotangent,
        output_weight,
        scratch=[pltpu.VMEM((chips, 2 * own, hid), F32)],
        after=att[:1],
        stage=True,
        name="grad_active",
    )

    cats = [cat] + [to_dp[q](cat) for q in peers]
    cats, grad_active, seen = lax.optimization_barrier((cats, grad_active, seen))
    weights = [mine, *cats, to_core(mine), *[to_core(x) for x in cats]]

    sq = cores * width
    first, fwd, q, cp, second, n3 = call(
        functools.partial(cross_kernel, chips, dps),
        [
            ((own, dim), F32),
            ((3, own, dim), BF16),
            ((own, sq), BF16),
            ((cores, own, heads * SEEN), BF16),
            ((own, dim), F32),
            ((own, dim), BF16),
        ],
        idx,
        tokens,
        norm_gain,
        norm_shift,
        seen,
        *weights,
        *att,
        *att2,
        scratch=[
            pltpu.VMEM((3, sq, dim), BF16),
            pltpu.SemaphoreType.DMA((3, 2 * dps + 2)),
            pltpu.VMEM((own, dim), BF16),
            pltpu.SemaphoreType.DMA,
        ],
        raw=(0, *range(4, 4 + len(weights))),
        stage=True,
        name="cross_fwd",
    )

    relay = chips == 4
    order = (0, 1, 3, 2) if relay else range(chips)
    n3s = [n3] + [None if relay and k == 2 else to_z[k](n3) for k in far]
    fwd2 = to_core(fwd)
    bias_row = hidden_bias[None, :]
    acts, ghis, chunks, sent, others = ([None] * chips for _ in range(5))
    done = ()
    for k in order:
        arrived = n3s[k]
        chunk, act, ghi, bs, bo = call(
            hidden_kernel,
            [
                ((2 * own, dim), BF16),
                ((2 * own, hid), BF16),
                ((2 * own, hid), BF16),
                ((own, dim), BF16),
                ((own, dim + hid), BF16),
            ],
            idx,
            arrived,
            to_core(arrived),
            hidden_weight,
            bias_row,
            grad_active[k],
            scratch=[pltpu.VMEM((2 * own, dim), F32)],
            after=done,
            tight=True,
            name="hidden",
        )
        done = (act,)
        acts[k], ghis[k], chunks[k] = act, ghi, chunk
        others[k] = to_core(bo)
        sent[k] = total(bs, others[k][:, :dim]).astype(BF16)
        if k == 0:
            *n3s, _ = lax.optimization_barrier((*n3s, act))
            if relay:
                n3s[2] = to_z[1](n3s[3])
    backs = sent[:1] + [to_z[k](sent[k]) for k in range(1, 2 if relay else chips)]
    if relay:
        sent[2] = total(sent[2], to_z[1](sent[3])).astype(BF16)
        backs.append(to_z[2](sent[2]))
    (mlp_grad,) = call(
        functools.partial(mlp_grad_kernel, chips),
        [((dps, 2 * hid + PAD, cut), BF16)],
        idx,
        cotangent,
        *acts,
        *ghis,
        *chunks,
        scratch=[
            pltpu.VMEM((rows, hid), BF16),
            pltpu.VMEM((rows, hid), BF16),
            pltpu.VMEM((rows, dim), BF16),
        ],
        after=sent,
        stage=True,
        name="mlp_grad",
    )
    mlp_grad, backs[1] = lax.optimization_barrier((mlp_grad, backs[1]))
    mlp_swap = swap_dp(mlp_grad)
    mlp_part = call(
        functools.partial(mlp_out_kernel, chips),
        [((own, dim), BF16)] * chips,
        idx,
        output_weight,
        output_weight2,
        *acts,
        *others,
        scratch=[
            pltpu.VMEM((2, chips, own, hid), BF16),
            pltpu.VMEM((chips, own, dim), BF16),
            pltpu.SemaphoreType.DMA((2, chips)),
        ],
        raw=tuple(range(2, 2 + 2 * chips)),
        after=(mlp_grad,),
        stage=True,
        name="mlp_out",
    )
    *backs, mlp_part = lax.optimization_barrier((*backs, list(mlp_part)))
    mlp_parts = mlp_part[:1] + [to_z[k](mlp_part[k]) for k in far[:2]]

    outs = call(
        functools.partial(cross_back_kernel, chips, dps, len(backs)),
        [
            ((3, own, dim), BF16),
            ((own, dim), F32),
            ((8, dim), F32),
            ((chips, 2, SEEN, width), BF16),
            ((chips, 2, SEEN, width), BF16),
        ]
        + [((2, own, width), BF16)] * chips,
        idx,
        cotangent,
        norm_gain,
        second,
        first,
        cp,
        q,
        *weights,
        *backs,
        *att,
        *att2,
        scratch=[
            pltpu.VMEM((own, sq), BF16),
            pltpu.VMEM((3, sq, dim), BF16),
            pltpu.SemaphoreType.DMA((3, 2 * dps + 2)),
            pltpu.VMEM((own, dim), BF16),
            pltpu.SemaphoreType.DMA,
        ],
        raw=(0, *range(6, 6 + len(weights))),
        cost=10**12,
        stage=True,
        name="cross_bwd",
    )
    outs, mlp_parts, mlp_swap = lax.optimization_barrier((outs, mlp_parts, mlp_swap))
    mlp_piece = call(
        sum_kernel, [((2 * hid, cut), BF16)], idx, mlp_swap, stage=True, name="sum_mlp"
    )[0]
    mlp_all = [mlp_piece] + [to_dp[q](mlp_piece) for q in (1, 2)]
    bwd, gf, stat_a, dkv, dkv_other = outs[:5]
    gatt = outs[5:]
    gatt = [gatt[0]] + [to_z[k](gatt[k]) for k in far]

    (row_grad,) = call(
        functools.partial(row_grad_kernel, chips),
        [((dps, chips * 3 * width, cut), BF16)],
        idx,
        fwd,
        fwd2,
        bwd,
        to_core(bwd),
        scratch=[pltpu.VMEM((2 * own, chips * width), BF16), pltpu.VMEM((2 * own, dim), BF16)],
        stage=True,
        name="row_grad",
    )
    gatt, row_grad, mlp_all, mlp_part = lax.optimization_barrier(
        (gatt, row_grad, mlp_all, mlp_part)
    )
    mlp_all += [to_dp[q](mlp_all[0]) for q in range(3, dps)]
    gatt2 = [to_core(x) for x in gatt]
    row_swap = swap_dp(row_grad)
    mlp_parts += [to_z[k](mlp_part[k]) for k in far[2:]]

    outs = call(
        functools.partial(self_back_kernel, chips),
        [((rows, 3 * width), BF16)] + [((own, dim), BF16)] * (2 * chips),
        idx,
        triple,
        probs,
        self_weight,
        *gatt,
        *gatt2,
        scratch=[
            pltpu.VMEM((rows, width), BF16),
            pltpu.VMEM((width, rows), BF16),
            pltpu.VMEM((dim, 3 * width), BF16),
            pltpu.VMEM((width, rows), F32),
            pltpu.VMEM((rows, width), F32),
            pltpu.VMEM((rows, width), F32),
            pltpu.VMEM((rows, dim), BF16),
        ],
        cost=10**12,
        stage=True,
        name="self_bwd",
    )
    outs, mlp_parts = lax.optimization_barrier((outs, mlp_parts))
    gt, bs, bo = outs[0], outs[1 : 1 + chips], outs[1 + chips :]
    bos = [to_core(x) for x in bo]

    dkv = total(dkv, to_core(dkv_other)).astype(BF16)
    gp = total(dkv[0], *[to_z[k](dkv[k]) for k in far]).astype(BF16)

    *bos, gp = lax.optimization_barrier((*bos, gp))
    sent = add_all(bs, bos, "self_add")
    parts = sent[:1] + [to_z[k](sent[k]) for k in far]

    (self_part,) = call(
        functools.partial(self_grad_kernel, chips, dps),
        [((dps, 5 * width + dps * PAD, cut), BF16)],
        idx,
        tokens,
        normed_one,
        gt,
        near,
        gp,
        stat_a,
        *bs,
        *bo,
        scratch=[
            pltpu.VMEM((cores, own, dim), BF16),
            pltpu.SemaphoreType.DMA((cores,)),
        ],
        raw=tuple(range(6, 6 + cores)),
        after=sent[:1],
        stage=True,
        name="self_grad",
    )
    self_part, row_swap, mlp_all, parts[1:3] = lax.optimization_barrier(
        (self_part, row_swap, mlp_all, parts[1:3])
    )
    self_swap = swap_dp(self_part)
    row_piece = sum_dp(row_swap).reshape(chips, 3 * width, cut)
    row_parts = [row_piece[0]] + [to_z[k](row_piece[k]) for k in far]
    row_parts, self_swap = lax.optimization_barrier((row_parts, self_swap))
    row_piece = total(*row_parts).astype(BF16)
    self_sum = sum_dp(self_swap)
    piece = jnp.concatenate([row_piece, self_sum[: 5 * width]], 0)
    swapped = share_dp(piece)
    (grad_tokens,) = call(
        token_kernel,
        [((own, dim), F32)],
        idx,
        tokens,
        norm_gain,
        gf,
        *parts,
        scratch=[pltpu.VMEM((own, dim), BF16), pltpu.SemaphoreType.DMA],
        raw=(0,),
        stage=True,
        name="tokens",
    )
    state_part = jnp.einsum("cse,cde->sd", gp, cross_pair, preferred_element_type=F32)
    held = self_sum[5 * width :].reshape(dps, PAD, cut)
    held = jnp.concatenate([held[c] for c in range(dps)], 1)
    state_part = jnp.concatenate([state_part.astype(BF16), held], 0)
    core = lax.rem(me, 2)
    half_of = lambda c: lax.dynamic_slice_in_dim(state_part, c * (dim // 2), dim // 2, 1)
    state_half = total(half_of(core), to_core(half_of(1 - core))).astype(BF16)
    state_half = total(state_half, *[to_z[k](state_half) for k in far])
    state_sum = jnp.zeros((state_part.shape[0], dim), F32)
    for c, part in ((core, state_half), (1 - core, to_core(state_half))):
        state_sum = lax.dynamic_update_slice(state_sum, part, (0, c * (dim // 2)))
    grad_states = lax.dynamic_update_slice(
        jnp.zeros(states.shape, F32), state_sum[None, :SEEN], (state_row[0], begin, 0)
    )
    stats = state_sum[SEEN:]

    def place(pieces, plan, shapes, name):
        return call(
            functools.partial(place_kernel, plan),
            [(s, F32) for s in shapes],
            idx,
            *pieces,
            stage=True,
            name=name,
        )

    block_output = (second + total(*mlp_parts) + output_bias.astype(F32)).astype(BF16)
    grad_output_weight, grad_hidden_weight = place(
        mlp_all, ((hid, None, False), (hid, None, True)), ((hid, dim), (dim, hid)), "place_mlp"
    )
    swapped, block_output, grad_output_weight, grad_tokens, state_sum = lax.optimization_barrier(
        (swapped, block_output, grad_output_weight, grad_tokens, state_sum)
    )
    (
        grad_self_output,
        grad_cross_query,
        grad_cross_output,
        grad_self_weight,
        grad_cross_pair,
    ) = place(
        [swapped],
        (
            (width, None, False),
            (width, None, True),
            (width, None, False),
            (3 * width, 3, True),
            (2 * width, 2, True),
        ),
        (
            (width, dim),
            (dim, width),
            (width, dim),
            (3, dim, width),
            (2, dim, width),
        ),
        "place",
    )
    grad_norm_gain = jnp.stack([stats[0], stats[4], stats[2]])
    grad_norm_shift = jnp.stack([stats[1], stats[5], stats[3]])
    grad_output_bias = stats[6]
    grad_hidden_bias = jnp.sum(mlp_swap[:, 2 * hid : 2 * hid + hid // cut].astype(F32), 0).reshape(hid)
    return (
        block_output,
        grad_tokens,
        grad_states,
        grad_self_weight,
        grad_self_output,
        grad_cross_query,
        grad_cross_pair,
        grad_cross_output,
        grad_hidden_weight,
        grad_hidden_bias,
        grad_output_weight,
        grad_output_bias,
        grad_norm_gain,
        grad_norm_shift,
    )


def solution(mesh):
    placed = (
        P("dp", None),
        P("dp", None, None),
        P("dp", None),
        P(None, None, "mp"),
        P("mp", None),
        P(None, "mp"),
        P(None, None, "mp"),
        P("mp", None),
        P(None, "mp"),
        P("mp"),
        P("mp", None),
        P(),
        P(),
        P(),
        P("dp"),
        P("dp", None),
        P("dp"),
    )
    return jax.shard_map(
        body,
        mesh=mesh,
        in_specs=placed,
        out_specs=(
            P(("dp", "mp"), None),
            P(("dp", "mp"), None),
            P("dp", None, None),
            P(None, None, "mp"),
            P("mp", None),
            P(None, "mp"),
            P(None, None, "mp"),
            P("mp", None),
            P(None, "mp"),
            P("mp"),
            P("mp", None),
            P(),
            P(),
            P(),
        ),
        check_vma=False,
    )
```

profile of v0, /device:TPU:11, one launch (start us, length us, event | category | flops | bytes accessed | tf_op | source)
XLA Modules:
  0.0 301.2 jit_solution(8908500147547294759)
XLA Ops:
  3.9 2.3 collective-permute-start.1
  8.2 13.3 %self_fwd.1 = (bf16[1024,1024]{1,0:T(8,128)(2,1)}, bf16[3,1024,128]{2,1,0:T(8,128)(2,1)}, bf16[2,1024,1024]{2,1,0:T(8,128)(2,1)}, bf16[384,128]{1,0:T(8,128)(2,1...) custom-call(s32[4]{0:T(128)} %pad_add_fusion.refs_0_.idx, ...), custom_call_target="tpu_custom_call" | custom-call | flops 1 | bytes 1 | tf_op jit(solution)/shard_map/self_fwd/pallas_call | solution.py:110
  21.5 2.2 collective-permute-done.2.refs_2_
  24.7 1.2 collective-permute-start.5
  27.1 2.5 collective-permute-start.13
  29.5 1.6 collective-permute-done.12.refs_16_.refs_21_
  31.1 1.3 collective-permute-start.14
  32.9 4.3 %collective-permute-start.7 = (bf16[384,1024]{1,0:T(8,128)(2,1)S(1)}, bf16[384,1024]{1,0:T(8,128)(2,1)}, u32[]{:S(2)}, u32[]{:S(2)}) collective-permute-start(bf16[384,1024]{1,0:T(8,128)(2,1)S(1)} %pad_maximum_fusion.refs_5_.refs_7_), channel_id=1, source_target_pairs={{0,1},{1,0},{2,3},{3,2},{4,5},{5,4},{6,7},{7,6},{8,9},{9,8},{10,11... | collective-permute-start | bytes 2359304 | tf_op jit(solution)/shard_map/ppermute | solution.py:751
  37.2 6.0 %grad_active.1 = (f32[256,512]{1,0:T(8,128)}, f32[256,512]{1,0:T(8,128)}, f32[256,512]{1,0:T(8,128)}, f32[256,512]{1,0:T(8,128)}) custom-call(s32[4]{0:T(128)} %pad_add_fusion.refs_0_.idx, bf16[1024,1024]{1,0:T(8,128)(2,1)} %refs_1_.13, bf16[512,1024]{1,0:T(8,128)(2,1)} %refs_1_.12), custom_call_target="tpu_custom_call" | custom-call | flops 1 | bytes 1 | tf_op jit(solution)/shard_map/grad_active/pallas_call | solution.py:110
  45.1 7.0 %collective-permute-start.17 = (bf16[384,128]{1,0:T(8,128)(2,1)S(1)}, bf16[384,128]{1,0:T(8,128)(2,1)}, u32[]{:S(2)}, u32[]{:S(2)}) collective-permute-start(bf16[384,128]{1,0:T(8,128)(2,1)S(1)} %collective-permute-done.13.refs_17_.refs_22_), channel_id=1, source_target_pairs={{0,1},{1,0},{2,3},{3,2},{4,5},{5,4},{6,7},{7,6},{8,9},{9,8},{10,11... | collective-permute-start | bytes 294920 | tf_op jit(solution)/shard_map/ppermute | solution.py:735
  52.1 1.7 collective-permute-start.18
  59.6 10.6 %cross_fwd.1 = (f32[128,1024]{1,0:T(8,128)}, bf16[3,128,1024]{2,1,0:T(8,128)(2,1)}, bf16[128,1024]{1,0:T(8,128)(2,1)}, bf16[8,128,128]{2,1,0:T(8,128)(2,1)}, f32...) custom-call(s32[4]{0:T(128)} %pad_add_fusion.refs_0_.idx, bf16[1024,1024]{1,0:T(8,128)(2,1)} %refs_1_.15, ...), custom_call_target="tpu_custom_call" | custom-call | flops 1 | bytes 1 | tf_op jit(solution)/shard_map/cross_fwd/pallas_call | solution.py:110
  70.4 1.4 collective-permute-start.22
  73.0 1.7 hidden.4
  78.1 2.0 collective-permute-start.23
  80.2 6.9 %collective-permute-start.26 = (bf16[128,1024]{1,0:T(8,128)(2,1)S(1)}, bf16[128,1024]{1,0:T(8,128)(2,1)S(1)}, u32[]{:S(2)}, u32[]{:S(2)}) collective-permute-start(bf16[128,1024]{1,0:T(8,128)(2,1)S(1)} %collective-permute-done.22.same), channel_id=1, source_target_pairs={{0,2},{1,3},{2,0},{3,1},{4,6},{5,7},{6,4},{7,5},{8,10},{9,11},{10,... | collective-permute-start | bytes 786440 | tf_op jit(solution)/shard_map/ppermute | solution.py:819
  87.1 1.7 hidden.5
  90.4 1.7 hidden.6
  95.7 1.2 collective-permute-done.27.other
  96.9 1.7 hidden.7
  102.7 5.7 %collective-permute-done.30 = bf16[128,1024]{1,0:T(8,128)(2,1)S(1)} collective-permute-done((bf16[128,1024]{1,0:T(8,128)(2,1)S(1)}, bf16[128,1024]{1,0:T(8,128)(2,1)S(1)}, u32[]{:S(2)}, u32[]{:S(2)}) %collective-permute-start.30) | collective-permute-done | bytes 262176 | tf_op jit(solution)/shard_map/ppermute | solution.py:822
  109.3 1.8 collective-permute-start.38
  112.0 8.4 %mlp_grad.1 = bf16[4,1040,256]{2,1,0:T(8,128)(2,1)} custom-call(s32[4]{0:T(128)} %pad_add_fusion.refs_0_.idx, bf16[1024,1024]{1,0:T(8,128)(2,1)} %refs_1_.13, bf16[256,512]{1,0:T(8,128)(2,1)} %copy-done.2, bf16[256,512]{1,0:T(8,128)(2,1)} %copy-done.3, bf16[256,512]{1,0:T(8,128)(2,1)} %copy-done.5, bf16[256,512]{1,0:T(8,128)(2,1)} %copy-done.4, ...), custom_call_target="tpu_custom_call" | custom-call | flops 1 | bytes 1 | tf_op jit(solution)/shard_map/mlp_grad/pallas_call | solution.py:110
  121.2 5.3 %all-to-all-start = ((bf16[4,1040,256]{2,1,0:T(8,128)(2,1)}), bf16[4,1040,256]{2,1,0:T(8,128)(2,1)}, u32[]{:S(2)}, u32[]{:S(2)}) async-start(bf16[4,1040,256]{2,1,0:T(8,128)(2,1)} %mlp_grad.1), calls=%async_computation | async-start | bytes 4259840 | tf_op jit(solution)/shard_map/all_to_all | solution.py:689
  126.5 6.4 %mlp_out.1 = (bf16[128,1024]{1,0:T(8,128)(2,1)}, bf16[128,1024]{1,0:T(8,128)(2,1)}, bf16[128,1024]{1,0:T(8,128)(2,1)}, bf16[128,1024]{1,0:T(8,128)(2,1)}) custom-call(s32[4]{0:T(128)} %pad_add_fusion.refs_0_.idx, bf16[512,1024]{1,0:T(8,128)(2,1)} %refs_1_.12, bf16[512,1024]{1,0:T(8,128)(2,1)} %copy-done.29, bf16[256,512]{1,0:T(8,128)(2,1)} %copy-done.2, ...), custom_call_target="tpu_custom_call" | custom-call | flops 1 | bytes 1 | tf_op jit(solution)/shard_map/mlp_out/pallas_call | solution.py:110
  133.8 1.6 collective-permute-start.34
  135.4 12.5 %cross_bwd.1 = (bf16[3,128,1024]{2,1,0:T(8,128)(2,1)}, f32[128,1024]{1,0:T(8,128)}, f32[8,1024]{1,0:T(8,128)}, bf16[4,2,64,128]{3,2,1,0:T(8,128)(2,1)}, bf16[4,2...) custom-call(s32[4]{0:T(128)} %pad_add_fusion.refs_0_.idx, ...), custom_call_target="tpu_custom_call" | custom-call | flops 999999995904 | bytes 1 | tf_op jit(solution)/shard_map/cross_bwd/pallas_call | solution.py:110
  148.0 3.7 %all-to-all-done.refs_1_ = bf16[4,1040,256]{2,1,0:T(8,128)(2,1)} async-done(((bf16[4,1040,256]{2,1,0:T(8,128)(2,1)}), bf16[4,1040,256]{2,1,0:T(8,128)(2,1)}, u32[]{:S(2)}, u32[]{:S(2)}) %all-to-all-start) | async-done | bytes 2129952 | tf_op jit(solution)/shard_map/all_to_all | solution.py:689
  152.5 3.4 %sum_mlp.1.refs_1_ = bf16[1024,256]{1,0:T(8,128)(2,1)} custom-call(s32[4]{0:T(128)} %pad_add_fusion.refs_0_.idx, bf16[4,1040,256]{2,1,0:T(8,128)(2,1)} %all-to-all-done.refs_1_), custom_call_target="tpu_custom_call" | custom-call | flops 1 | bytes 1 | tf_op jit(solution)/shard_map/sum_mlp/pallas_call | solution.py:110
  156.3 1.2 collective-permute-start.41
  159.0 1.6 collective-permute-start.36
  161.6 5.4 %row_grad.1 = bf16[4,1536,256]{2,1,0:T(8,128)(2,1)} custom-call(s32[4]{0:T(128)} %pad_add_fusion.refs_0_.idx, bf16[3,128,1024]{2,1,0:T(8,128)(2,1)} %get-tuple-element.255.refs_1_, bf16[3,128,1024]{2,1,0:T(8,128)(2,1)} %collective-permute-done.38.refs_2_, bf16[3,128,1024]{2,1,0:T(8,128)(2,1)} %get-tuple-element.256.refs_3_, bf16[3,128,1024]{2,1,0:T(8,128)(2,1)} %copy-done.30), custom_call_target="tpu_custom_call" | custom-call | flops 1 | bytes 1 | tf_op jit(solution)/shard_map/row_grad/pallas_call | solution.py:110
  167.3 2.4 collective-permute-done.40.refs_2_
  172.8 5.8 %all-to-all-start.1 = ((bf16[4,1536,256]{2,1,0:T(8,128)(2,1)}), bf16[4,1536,256]{2,1,0:T(8,128)(2,1)}, u32[]{:S(2)}, u32[]{:S(2)}) async-start(bf16[4,1536,256]{2,1,0:T(8,128)(2,1)} %row_grad.1), calls=%async_computation.1 | async-start | bytes 6291456 | tf_op jit(solution)/shard_map/all_to_all | solution.py:689
  178.6 1.6 collective-permute-start.53
  182.4 12.1 %self_bwd.1 = (bf16[1024,384]{1,0:T(8,128)(2,1)}, bf16[128,1024]{1,0:T(8,128)(2,1)}, bf16[128,1024]{1,0:T(8,128)(2,1)}, bf16[128,1024]{1,0:T(8,128)(2,1)}, bf16[...) custom-call(s32[4]{0:T(128)} %pad_add_fusion.refs_0_.idx, ...), custom_call_target="tpu_custom_call" | custom-call | flops 999999995904 | bytes 1 | tf_op jit(solution)/shard_map/self_bwd/pallas_call | solution.py:110
  194.5 1.5 collective-permute-done.46
  197.6 1.2 collective-permute-start.55
  198.8 1.4 fusion.3.refs_5_
  201.8 3.3 %self_add.1 = (bf16[128,1024]{1,0:T(8,128)(2,1)}, bf16[128,1024]{1,0:T(8,128)(2,1)}, bf16[128,1024]{1,0:T(8,128)(2,1)}, bf16[128,1024]{1,0:T(8,128)(2,1)}) custom-call(s32[4]{0:T(128)} %pad_add_fusion.refs_0_.idx, bf16[128,1024]{1,0:T(8,128)(2,1)} %get-tuple-element.276.refs_1_.refs_7_, bf16[128,1024]{1,0:T(8,128)(2,1)} %get-tuple-element.277.refs_2_.refs_8_, ...), custom_call_target="tpu_custom_call" | custom-call | flops 1 | bytes 1 | tf_op jit(solution)/shard_map/self_add/pallas_call | solution.py:110
  205.1 2.0 collective-permute-start.56
  207.5 1.6 dynamic-slice_bitcast_fusion.refs_4_
  209.1 8.3 %self_grad.1 = bf16[4,704,256]{2,1,0:T(8,128)(2,1)} custom-call(s32[4]{0:T(128)} %pad_add_fusion.refs_0_.idx, bf16[1024,1024]{1,0:T(8,128)(2,1)} %refs_1_.15, bf16[1024,1024]{1,0:T(8,128)(2,1)} %get-tuple-element.292.refs_2_, bf16[1024,384]{1,0:T(8,128)(2,1)} %get-tuple-element.293.refs_3_, bf16[64,1024]{1,0:T(8,128)(2,1)} %dynamic-slice_bitcast_fusion.refs_4_, ...), custom_call_target="tpu_custom_call" | custom-call | flops 1 | bytes 1 | tf_op jit(solution)/shard_map/self_grad/pallas_call | solution.py:110
  217.4 7.6 %collective-permute-done.55.refs_4_ = bf16[1024,256]{1,0:T(8,128)(2,1)S(1)} collective-permute-done((bf16[1024,256]{1,0:T(8,128)(2,1)S(1)}, bf16[1024,256]{1,0:T(8,128)(2,1)S(1)}, u32[]{:S(2)}, u32[]{:S(2)}) %collective-permute-start.55) | collective-permute-done | bytes 524320 | tf_op jit(solution)/shard_map/ppermute | solution.py:921
  225.8 4.8 %all-to-all-start.2 = ((bf16[4,704,256]{2,1,0:T(8,128)(2,1)}), bf16[4,704,256]{2,1,0:T(8,128)(2,1)S(1)}, u32[]{:S(2)}, u32[]{:S(2)}) async-start(bf16[4,704,256]{2,1,0:T(8,128)(2,1)} %self_grad.1), calls=%async_computation.2 | async-start | bytes 2883584 | tf_op jit(solution)/shard_map/all_to_all | solution.py:689
  230.6 2.9 reduce_sum.43
  234.4 1.6 collective-permute-start.59
  236.6 2.8 collective-permute-done.58
  239.3 4.1 %collective-permute-done.59 = bf16[384,256]{1,0:T(8,128)(2,1)S(1)} collective-permute-done((bf16[384,256]{1,0:T(8,128)(2,1)S(1)}, bf16[384,256]{1,0:T(8,128)(2,1)S(1)}, u32[]{:S(2)}, u32[]{:S(2)}) %collective-permute-start.59) | collective-permute-done | bytes 196640 | tf_op jit(solution)/shard_map/ppermute | solution.py:985
  243.4 9.0 %collective-permute-done.60 = bf16[384,256]{1,0:T(8,128)(2,1)S(1)} collective-permute-done((bf16[384,256]{1,0:T(8,128)(2,1)S(1)}, bf16[384,256]{1,0:T(8,128)(2,1)S(1)}, u32[]{:S(2)}, u32[]{:S(2)}) %collective-permute-start.60) | collective-permute-done | bytes 196640 | tf_op jit(solution)/shard_map/ppermute | solution.py:985
  252.9 2.5 collective-permute-start.62
  255.5 1.4 broadcast_in_dim.20
  257.0 4.0 %all-to-all-start.3 = ((bf16[4,1024,256]{2,1,0:T(8,128)(2,1)}), bf16[4,1024,256]{2,1,0:T(8,128)(2,1)S(1)}, u32[]{:S(2)}, u32[]{:S(2)}) async-start(bf16[4,1024,256]{2,1,0:T(8,128)(2,1)} %broadcast_in_dim.20), calls=%async_computation.3 | async-start | bytes 4194304 | tf_op jit(solution)/shard_map/all_to_all | solution.py:674
  261.1 2.4 collective-permute-start.64
  265.1 1.2 collective-permute-start.61
  266.3 2.2 collective-permute-done.64
  268.5 8.3 %collective-permute-done.65 = bf16[80,512]{1,0:T(8,128)(2,1)S(1)} collective-permute-done((bf16[80,512]{1,0:T(8,128)(2,1)S(1)}, bf16[80,512]{1,0:T(8,128)(2,1)S(1)}, u32[]{:S(2)}, u32[]{:S(2)}) %collective-permute-start.65) | collective-permute-done | bytes 81952 | tf_op jit(solution)/shard_map/ppermute | solution.py:1011
  276.9 2.1 collective-permute-start.66
  279.0 2.0 add_convert_fusion
  281.0 4.7 %place_mlp.1 = (f32[512,1024]{1,0:T(8,128)}, f32[1024,512]{1,0:T(8,128)}) custom-call(s32[4]{0:T(128)} %pad_add_fusion.refs_0_.idx, bf16[1024,256]{1,0:T(8,128)(2,1)} %sum_mlp.1.refs_1_, bf16[1024,256]{1,0:T(8,128)(2,1)} %copy-done.36, bf16[1024,256]{1,0:T(8,128)(2,1)} %copy-done.37, bf16[1024,256]{1,0:T(8,128)(2,1)} %copy-done.38), custom_call_target="tpu_custom_call" | custom-call | flops 1 | bytes 1 | tf_op jit(solution)/shard_map/place_mlp/pallas_call | solution.py:110
  286.4 4.3 %tokens.1 = f32[128,1024]{1,0:T(8,128)} custom-call(s32[4]{0:T(128)} %pad_add_fusion.refs_0_.idx, bf16[1024,1024]{1,0:T(8,128)(2,1)} %refs_1_.15, bf16[3,1024]{1,0:T(4,128)(2,1)} %refs_2_.9, f32[128,1024]{1,0:T(8,128)} %get-tuple-element.318.refs_3_, bf16[128,1024]{1,0:T(8,128)(2,1)} %get-tuple-element.290.refs_4_, bf16[128,1024]{1,0:T(8,128)(2,1)} %copy-done.42, ...), custom_call_target="tpu_custom_call" | custom-call | flops 1 | bytes 1 | tf_op jit(solution)/shard_map/tokens/pallas_call | solution.py:110
  291.9 1.8 dynamic_update_slice.11
  295.0 1.3 copy-done.21
  296.3 4.8 %place.1 = (f32[128,1024]{1,0:T(8,128)}, f32[1024,128]{1,0:T(8,128)}, f32[128,1024]{1,0:T(8,128)}, f32[3,1024,128]{2,1,0:T(8,128)}, f32[2,1024,128]{2,1,0:T(8,128)}) custom-call(s32[4]{0:T(128)} %pad_add_fusion.refs_0_.idx, bf16[4,1024,256]{2,1,0:T(8,128)(2,1)} %copy-done.21), custom_call_target="tpu_custom_call" | custom-call | flops 1 | bytes 1 | tf_op jit(solution)/shard_map/place/pallas_call | solution.py:110
  (280 shorter events, 51.1 us)
Async XLA Ops:
  0.6 23.1 %collective-permute-start.3 = (bf16[512,1024]{1,0:T(8,128)(2,1)}, bf16[512,1024]{1,0:T(8,128)(2,1)S(1)}, u32[]{:S(2)}, u32[]{:S(2)}) collective-permute-start(bf16[512,1024]{1,0:T(8,128)(2,1)} %refs_1_.12), channel_id=1, source_target_pairs={{0,1},{1,0},{2,3},{3,2},{4,5},{5,4},{6,7},{7,6},{8,9},{9,8},{10,11... | collective-permute-start | bytes 3145736 | tf_op jit(solution)/shard_map/ppermute | solution.py:703
  3.6 17.9 %collective-permute-start = (bf16[384,256]{1,0:T(8,128)(2,1)S(1)}, bf16[384,256]{1,0:T(8,128)(2,1)S(1)}, u32[]{:S(2)}, u32[]{:S(2)}) collective-permute-start(bf16[384,256]{1,0:T(8,128)(2,1)S(1)} %constant_dynamic-slice_fusion.2), channel_id=1, source_target_pairs={{0,2},{1,3},{2,0},{3,1},{4,6},{5,7},{6,4},{7,5},{8,10},{9,11},{10,... | collective-permute-start | bytes 589832 | tf_op jit(solution)/shard_map/ppermute | solution.py:702
  3.9 17.7 %collective-permute-start.1 = (bf16[384,256]{1,0:T(8,128)(2,1)S(1)}, bf16[384,256]{1,0:T(8,128)(2,1)S(1)}, u32[]{:S(2)}, u32[]{:S(2)}) collective-permute-start(bf16[384,256]{1,0:T(8,128)(2,1)S(1)} %constant_dynamic-slice_fusion.2), channel_id=1, source_target_pairs={{0,4},{1,5},{2,6},{3,7},{4,0},{5,1},{6,2},{7,3},{8,12},{9,13},{10,... | collective-permute-start | bytes 589832 | tf_op jit(solution)/shard_map/ppermute | solution.py:702
  6.2 17.6 %collective-permute-start.2 = (bf16[384,256]{1,0:T(8,128)(2,1)S(1)}, bf16[384,256]{1,0:T(8,128)(2,1)S(1)}, u32[]{:S(2)}, u32[]{:S(2)}) collective-permute-start(bf16[384,256]{1,0:T(8,128)(2,1)S(1)} %constant_dynamic-slice_fusion.2), channel_id=1, source_target_pairs={{0,6},{1,7},{2,4},{3,5},{4,2},{5,3},{6,0},{7,1},{8,14},{9,15},{10,... | collective-permute-start | bytes 589832 | tf_op jit(solution)/shard_map/ppermute | solution.py:702
  24.3 20.3 %collective-permute-start.4 = (bf16[1152,256]{1,0:T(8,128)(2,1)S(1)}, bf16[1152,256]{1,0:T(8,128)(2,1)S(1)}, u32[]{:S(2)}, u32[]{:S(2)}) collective-permute-start(bf16[1152,256]{1,0:T(8,128)(2,1)S(1)} %pack.1.refs_6_.refs_8_), channel_id=1, source_target_pairs={{0,8},{8,0},{16,24},{24,16},{1,9},{9,1},{17,25},{25,17},{2,10},{10... | collective-permute-start | bytes 1769480 | tf_op jit(solution)/shard_map/ppermute | solution.py:749
  24.7 20.4 %collective-permute-start.5 = (bf16[1152,256]{1,0:T(8,128)(2,1)S(1)}, bf16[1152,256]{1,0:T(8,128)(2,1)}, u32[]{:S(2)}, u32[]{:S(2)}) collective-permute-start(bf16[1152,256]{1,0:T(8,128)(2,1)S(1)} %pack.1.refs_6_.refs_8_), channel_id=1, source_target_pairs={{0,16},{8,24},{16,0},{24,8},{1,17},{9,25},{17,1},{25,9},{2,18},{10... | collective-permute-start | bytes 1769480 | tf_op jit(solution)/shard_map/ppermute | solution.py:749
  25.9 26.2 %collective-permute-start.6 = (bf16[1152,256]{1,0:T(8,128)(2,1)S(1)}, bf16[1152,256]{1,0:T(8,128)(2,1)}, u32[]{:S(2)}, u32[]{:S(2)}) collective-permute-start(bf16[1152,256]{1,0:T(8,128)(2,1)S(1)} %pack.1.refs_6_.refs_8_), channel_id=1, source_target_pairs={{0,24},{8,16},{16,8},{24,0},{1,25},{9,17},{17,9},{25,1},{2,26},{10... | collective-permute-start | bytes 1769480 | tf_op jit(solution)/shard_map/ppermute | solution.py:749
  27.1 4.1 %collective-permute-start.12 = (bf16[384,128]{1,0:T(8,128)(2,1)}, bf16[384,128]{1,0:T(8,128)(2,1)S(1)}, u32[]{:S(2)}, u32[]{:S(2)}) collective-permute-start(bf16[384,128]{1,0:T(8,128)(2,1)} %get-tuple-element.190), channel_id=1, source_target_pairs={{0,2},{1,3},{2,0},{3,1},{4,6},{5,7},{6,4},{7,5},{8,10},{9,11},{10,... | collective-permute-start | bytes 294920 | tf_op jit(solution)/shard_map/ppermute | solution.py:734
  27.1 5.8 %collective-permute-start.13 = (bf16[384,128]{1,0:T(8,128)(2,1)}, bf16[384,128]{1,0:T(8,128)(2,1)S(1)}, u32[]{:S(2)}, u32[]{:S(2)}) collective-permute-start(bf16[384,128]{1,0:T(8,128)(2,1)} %get-tuple-element.191), channel_id=1, source_target_pairs={{0,4},{1,5},{2,6},{3,7},{4,0},{5,1},{6,2},{7,3},{8,12},{9,13},{10,... | collective-permute-start | bytes 294920 | tf_op jit(solution)/shard_map/ppermute | solution.py:734
  31.1 13.4 %collective-permute-start.14 = (bf16[384,128]{1,0:T(8,128)(2,1)}, bf16[384,128]{1,0:T(8,128)(2,1)S(1)}, u32[]{:S(2)}, u32[]{:S(2)}) collective-permute-start(bf16[384,128]{1,0:T(8,128)(2,1)} %get-tuple-element.192), channel_id=1, source_target_pairs={{0,6},{1,7},{2,4},{3,5},{4,2},{5,3},{6,0},{7,1},{8,14},{9,15},{10,... | collective-permute-start | bytes 294920 | tf_op jit(solution)/shard_map/ppermute | solution.py:734
  32.9 22.8 %collective-permute-start.7 = (bf16[384,1024]{1,0:T(8,128)(2,1)S(1)}, bf16[384,1024]{1,0:T(8,128)(2,1)}, u32[]{:S(2)}, u32[]{:S(2)}) collective-permute-start(bf16[384,1024]{1,0:T(8,128)(2,1)S(1)} %pad_maximum_fusion.refs_5_.refs_7_), channel_id=1, source_target_pairs={{0,1},{1,0},{2,3},{3,2},{4,5},{5,4},{6,7},{7,6},{8,9},{9,8},{10,11... | collective-permute-start | bytes 2359304 | tf_op jit(solution)/shard_map/ppermute | solution.py:751
  44.5 10.0 %collective-permute-start.15 = (bf16[384,128]{1,0:T(8,128)(2,1)S(1)}, bf16[384,128]{1,0:T(8,128)(2,1)S(1)}, u32[]{:S(2)}, u32[]{:S(2)}) collective-permute-start(bf16[384,128]{1,0:T(8,128)(2,1)S(1)} %copy-done.49), channel_id=1, source_target_pairs={{0,1},{1,0},{2,3},{3,2},{4,5},{5,4},{6,7},{7,6},{8,9},{9,8},{10,11... | collective-permute-start | bytes 294920 | tf_op jit(solution)/shard_map/ppermute | solution.py:735
  44.6 10.0 %collective-permute-start.16 = (bf16[384,128]{1,0:T(8,128)(2,1)S(1)}, bf16[384,128]{1,0:T(8,128)(2,1)}, u32[]{:S(2)}, u32[]{:S(2)}) collective-permute-start(bf16[384,128]{1,0:T(8,128)(2,1)S(1)} %collective-permute-done.12.refs_16_.refs_21_), channel_id=1, source_target_pairs={{0,1},{1,0},{2,3},{3,2},{4,5},{5,4},{6,7},{7,6},{8,9},{9,8},{10,11... | collective-permute-start | bytes 294920 | tf_op jit(solution)/shard_map/ppermute | solution.py:735
  45.1 10.0 %collective-permute-start.17 = (bf16[384,128]{1,0:T(8,128)(2,1)S(1)}, bf16[384,128]{1,0:T(8,128)(2,1)}, u32[]{:S(2)}, u32[]{:S(2)}) collective-permute-start(bf16[384,128]{1,0:T(8,128)(2,1)S(1)} %collective-permute-done.13.refs_17_.refs_22_), channel_id=1, source_target_pairs={{0,1},{1,0},{2,3},{3,2},{4,5},{5,4},{6,7},{7,6},{8,9},{9,8},{10,11... | collective-permute-start | bytes 294920 | tf_op jit(solution)/shard_map/ppermute | solution.py:735
  52.1 3.1 %collective-permute-start.18 = (bf16[384,128]{1,0:T(8,128)(2,1)S(1)}, bf16[384,128]{1,0:T(8,128)(2,1)}, u32[]{:S(2)}, u32[]{:S(2)}) collective-permute-start(bf16[384,128]{1,0:T(8,128)(2,1)S(1)} %collective-permute-done.14.refs_18_.refs_23_), channel_id=1, source_target_pairs={{0,1},{1,0},{2,3},{3,2},{4,5},{5,4},{6,7},{7,6},{8,9},{9,8},{10,11... | collective-permute-start | bytes 294920 | tf_op jit(solution)/shard_map/ppermute | solution.py:735
  55.2 3.4 %collective-permute-start.8 = (bf16[1152,256]{1,0:T(8,128)(2,1)S(1)}, bf16[1152,256]{1,0:T(8,128)(2,1)S(1)}, u32[]{:S(2)}, u32[]{:S(2)}) collective-permute-start(bf16[1152,256]{1,0:T(8,128)(2,1)S(1)} %pack.1.refs_6_.refs_8_), channel_id=1, source_target_pairs={{0,1},{1,0},{2,3},{3,2},{4,5},{5,4},{6,7},{7,6},{8,9},{9,8},{10,11... | collective-permute-start | bytes 1769480 | tf_op jit(solution)/shard_map/ppermute | solution.py:751
  55.2 4.3 %collective-permute-start.9 = (bf16[1152,256]{1,0:T(8,128)(2,1)}, bf16[1152,256]{1,0:T(8,128)(2,1)}, u32[]{:S(2)}, u32[]{:S(2)}) collective-permute-start(bf16[1152,256]{1,0:T(8,128)(2,1)} %copy-done.31), channel_id=1, source_target_pairs={{0,1},{1,0},{2,3},{3,2},{4,5},{5,4},{6,7},{7,6},{8,9},{9,8},{10,11... | collective-permute-start | bytes 1769480 | tf_op jit(solution)/shard_map/ppermute | solution.py:751
  70.4 7.7 %collective-permute-start.21 = (bf16[128,1024]{1,0:T(8,128)(2,1)}, bf16[128,1024]{1,0:T(8,128)(2,1)S(1)}, u32[]{:S(2)}, u32[]{:S(2)}) collective-permute-start(bf16[128,1024]{1,0:T(8,128)(2,1)} %get-tuple-element.197.same), channel_id=1, source_target_pairs={{0,2},{1,3},{2,0},{3,1},{4,6},{5,7},{6,4},{7,5},{8,10},{9,11},{10,... | collective-permute-start | bytes 786440 | tf_op jit(solution)/shard_map/ppermute | solution.py:785
  70.4 7.8 %collective-permute-start.22 = (bf16[128,1024]{1,0:T(8,128)(2,1)}, bf16[128,1024]{1,0:T(8,128)(2,1)S(1)}, u32[]{:S(2)}, u32[]{:S(2)}) collective-permute-start(bf16[128,1024]{1,0:T(8,128)(2,1)} %get-tuple-element.197.same), channel_id=1, source_target_pairs={{0,6},{1,7},{2,4},{3,5},{4,2},{5,3},{6,0},{7,1},{8,14},{9,15},{10,... | collective-permute-start | bytes 786440 | tf_op jit(solution)/shard_map/ppermute | solution.py:785
  78.1 9.0 %collective-permute-start.23 = (bf16[128,1024]{1,0:T(8,128)(2,1)S(1)}, bf16[128,1024]{1,0:T(8,128)(2,1)S(1)}, u32[]{:S(2)}, u32[]{:S(2)}) collective-permute-start(bf16[128,1024]{1,0:T(8,128)(2,1)S(1)} %collective-permute-done.21.same), channel_id=1, source_target_pairs={{0,1},{1,0},{2,3},{3,2},{4,5},{5,4},{6,7},{7,6},{8,9},{9,8},{10,11... | collective-permute-start | bytes 786440 | tf_op jit(solution)/shard_map/ppermute | solution.py:803
  80.2 10.2 %collective-permute-start.25 = (bf16[128,1024]{1,0:T(8,128)(2,1)S(1)}, bf16[128,1024]{1,0:T(8,128)(2,1)S(1)}, u32[]{:S(2)}, u32[]{:S(2)}) collective-permute-start(bf16[128,1024]{1,0:T(8,128)(2,1)S(1)} %collective-permute-done.22.same), channel_id=1, source_target_pairs={{0,1},{1,0},{2,3},{3,2},{4,5},{5,4},{6,7},{7,6},{8,9},{9,8},{10,11... | collective-permute-start | bytes 786440 | tf_op jit(solution)/shard_map/ppermute | solution.py:803
  80.2 14.9 %collective-permute-start.26 = (bf16[128,1024]{1,0:T(8,128)(2,1)S(1)}, bf16[128,1024]{1,0:T(8,128)(2,1)S(1)}, u32[]{:S(2)}, u32[]{:S(2)}) collective-permute-start(bf16[128,1024]{1,0:T(8,128)(2,1)S(1)} %collective-permute-done.22.same), channel_id=1, source_target_pairs={{0,2},{1,3},{2,0},{3,1},{4,6},{5,7},{6,4},{7,5},{8,10},{9,11},{10,... | collective-permute-start | bytes 786440 | tf_op jit(solution)/shard_map/ppermute | solution.py:819
  94.4 6.2 %collective-permute-start.29 = (bf16[128,1536]{1,0:T(8,128)(2,1)S(1)}, bf16[128,1536]{1,0:T(8,128)(2,1)S(1)}, u32[]{:S(2)}, u32[]{:S(2)}) collective-permute-start(bf16[128,1536]{1,0:T(8,128)(2,1)S(1)} %get-tuple-element.217), channel_id=1, source_target_pairs={{0,1},{1,0},{2,3},{3,2},{4,5},{5,4},{6,7},{7,6},{8,9},{9,8},{10,11... | collective-permute-start | bytes 1179656 | tf_op jit(solution)/shard_map/ppermute | solution.py:814
  95.2 6.7 %collective-permute-start.24 = (bf16[128,1536]{1,0:T(8,128)(2,1)S(1)}, bf16[128,1536]{1,0:T(8,128)(2,1)S(1)}, u32[]{:S(2)}, u32[]{:S(2)}) collective-permute-start(bf16[128,1536]{1,0:T(8,128)(2,1)S(1)} %get-tuple-element.206), channel_id=1, source_target_pairs={{0,1},{1,0},{2,3},{3,2},{4,5},{5,4},{6,7},{7,6},{8,9},{9,8},{10,11... | collective-permute-start | bytes 1179656 | tf_op jit(solution)/shard_map/ppermute | solution.py:814
  100.6 7.8 %collective-permute-start.30 = (bf16[128,1024]{1,0:T(8,128)(2,1)S(1)}, bf16[128,1024]{1,0:T(8,128)(2,1)S(1)}, u32[]{:S(2)}, u32[]{:S(2)}) collective-permute-start(bf16[128,1024]{1,0:T(8,128)(2,1)S(1)} %add_convert_fusion.2), channel_id=1, source_target_pairs={{0,2},{1,3},{2,0},{3,1},{4,6},{5,7},{6,4},{7,5},{8,10},{9,11},{10,... | collective-permute-start | bytes 786440 | tf_op jit(solution)/shard_map/ppermute | solution.py:822
  101.4 9.8 %collective-permute-start.20 = (bf16[128,1536]{1,0:T(8,128)(2,1)S(1)}, bf16[128,1536]{1,0:T(8,128)(2,1)S(1)}, u32[]{:S(2)}, u32[]{:S(2)}) collective-permute-start(bf16[128,1536]{1,0:T(8,128)(2,1)S(1)} %get-tuple-element.200), channel_id=1, source_target_pairs={{0,1},{1,0},{2,3},{3,2},{4,5},{5,4},{6,7},{7,6},{8,9},{9,8},{10,11... | collective-permute-start | bytes 1179656 | tf_op jit(solution)/shard_map/ppermute | solution.py:814
  101.9 18.6 %collective-permute-start.31 = (bf16[128,1024]{1,0:T(8,128)(2,1)S(1)}, bf16[128,1024]{1,0:T(8,128)(2,1)S(1)}, u32[]{:S(2)}, u32[]{:S(2)}) collective-permute-start(bf16[128,1024]{1,0:T(8,128)(2,1)S(1)} %add_convert_fusion.4), channel_id=1, source_target_pairs={{0,2},{1,3},{2,0},{3,1},{4,6},{5,7},{6,4},{7,5},{8,10},{9,11},{10,... | collective-permute-start | bytes 786440 | tf_op jit(solution)/shard_map/ppermute | solution.py:820
  108.5 24.4 %collective-permute-start.32 = (bf16[128,1024]{1,0:T(8,128)(2,1)S(1)}, bf16[128,1024]{1,0:T(8,128)(2,1)S(1)}, u32[]{:S(2)}, u32[]{:S(2)}) collective-permute-start(bf16[128,1024]{1,0:T(8,128)(2,1)S(1)} %add_convert_fusion.1), channel_id=1, source_target_pairs={{0,4},{1,5},{2,6},{3,7},{4,0},{5,1},{6,2},{7,3},{8,12},{9,13},{10,... | collective-permute-start | bytes 786440 | tf_op jit(solution)/shard_map/ppermute | solution.py:823
  109.3 48.7 %collective-permute-start.38 = (bf16[3,128,1024]{2,1,0:T(8,128)(2,1)}, bf16[3,128,1024]{2,1,0:T(8,128)(2,1)}, u32[]{:S(2)}, u32[]{:S(2)}) collective-permute-start(bf16[3,128,1024]{2,1,0:T(8,128)(2,1)} %get-tuple-element.255.refs_1_), channel_id=1, source_target_pairs={{0,1},{1,0},{2,3},{3,2},{4,5},{5,4},{6,7},{7,6},{8,9},{9,8},{10,11... | collective-permute-start | bytes 2359304 | tf_op jit(solution)/shard_map/ppermute | solution.py:786
  121.2 30.4 %all-to-all-start = ((bf16[4,1040,256]{2,1,0:T(8,128)(2,1)}), bf16[4,1040,256]{2,1,0:T(8,128)(2,1)}, u32[]{:S(2)}, u32[]{:S(2)}) async-start(bf16[4,1040,256]{2,1,0:T(8,128)(2,1)} %mlp_grad.1), calls=%async_computation | async-start | bytes 4259840 | tf_op jit(solution)/shard_map/all_to_all | solution.py:689
  133.0 15.0 %collective-permute-start.33 = (bf16[128,1024]{1,0:T(8,128)(2,1)}, bf16[128,1024]{1,0:T(8,128)(2,1)}, u32[]{:S(2)}, u32[]{:S(2)}) collective-permute-start(bf16[128,1024]{1,0:T(8,128)(2,1)} %get-tuple-element.249), channel_id=1, source_target_pairs={{0,2},{1,3},{2,0},{3,1},{4,6},{5,7},{6,4},{7,5},{8,10},{9,11},{10,... | collective-permute-start | bytes 786440 | tf_op jit(solution)/shard_map/ppermute | solution.py:862
  133.8 14.2 %collective-permute-start.34 = (bf16[128,1024]{1,0:T(8,128)(2,1)}, bf16[128,1024]{1,0:T(8,128)(2,1)}, u32[]{:S(2)}, u32[]{:S(2)}) collective-permute-start(bf16[128,1024]{1,0:T(8,128)(2,1)} %get-tuple-element.250), channel_id=1, source_target_pairs={{0,4},{1,5},{2,6},{3,7},{4,0},{5,1},{6,2},{7,3},{8,12},{9,13},{10,... | collective-permute-start | bytes 786440 | tf_op jit(solution)/shard_map/ppermute | solution.py:862
  151.6 9.0 %collective-permute-start.39 = (bf16[3,128,1024]{2,1,0:T(8,128)(2,1)}, bf16[3,128,1024]{2,1,0:T(8,128)(2,1)S(1)}, u32[]{:S(2)}, u32[]{:S(2)}) collective-permute-start(bf16[3,128,1024]{2,1,0:T(8,128)(2,1)} %get-tuple-element.256.refs_3_), channel_id=1, source_target_pairs={{0,1},{1,0},{2,3},{3,2},{4,5},{5,4},{6,7},{7,6},{8,9},{9,8},{10,11... | collective-permute-start | bytes 2359304 | tf_op jit(solution)/shard_map/ppermute | solution.py:913
  155.9 13.8 %collective-permute-start.40 = (bf16[1024,256]{1,0:T(8,128)(2,1)}, bf16[1024,256]{1,0:T(8,128)(2,1)S(1)}, u32[]{:S(2)}, u32[]{:S(2)}) collective-permute-start(bf16[1024,256]{1,0:T(8,128)(2,1)} %sum_mlp.1.refs_1_), channel_id=1, source_target_pairs={{0,8},{8,0},{16,24},{24,16},{1,9},{9,1},{17,25},{25,17},{2,10},{10... | collective-permute-start | bytes 1572872 | tf_op jit(solution)/shard_map/ppermute | solution.py:901
  156.3 13.4 %collective-permute-start.41 = (bf16[1024,256]{1,0:T(8,128)(2,1)}, bf16[1024,256]{1,0:T(8,128)(2,1)S(1)}, u32[]{:S(2)}, u32[]{:S(2)}) collective-permute-start(bf16[1024,256]{1,0:T(8,128)(2,1)} %sum_mlp.1.refs_1_), channel_id=1, source_target_pairs={{0,16},{8,24},{16,0},{24,8},{1,17},{9,25},{17,1},{25,9},{2,18},{10... | collective-permute-start | bytes 1572872 | tf_op jit(solution)/shard_map/ppermute | solution.py:901
  158.1 8.9 %collective-permute-start.35 = (bf16[2,128,128]{2,1,0:T(8,128)(2,1)S(1)}, bf16[2,128,128]{2,1,0:T(8,128)(2,1)S(1)}, u32[]{:S(2)}, u32[]{:S(2)}) collective-permute-start(bf16[2,128,128]{2,1,0:T(8,128)(2,1)S(1)} %copy-done.66), channel_id=1, source_target_pairs={{0,2},{1,3},{2,0},{3,1},{4,6},{5,7},{6,4},{7,5},{8,10},{9,11},{10,... | collective-permute-start | bytes 196616 | tf_op jit(solution)/shard_map/ppermute | solution.py:904
  159.0 8.0 %collective-permute-start.36 = (bf16[2,128,128]{2,1,0:T(8,128)(2,1)S(1)}, bf16[2,128,128]{2,1,0:T(8,128)(2,1)S(1)}, u32[]{:S(2)}, u32[]{:S(2)}) collective-permute-start(bf16[2,128,128]{2,1,0:T(8,128)(2,1)S(1)} %copy-done.65), channel_id=1, source_target_pairs={{0,4},{1,5},{2,6},{3,7},{4,0},{5,1},{6,2},{7,3},{8,12},{9,13},{10,... | collective-permute-start | bytes 196616 | tf_op jit(solution)/shard_map/ppermute | solution.py:904
  160.7 6.6 %collective-permute-start.37 = (bf16[2,128,128]{2,1,0:T(8,128)(2,1)S(1)}, bf16[2,128,128]{2,1,0:T(8,128)(2,1)S(1)}, u32[]{:S(2)}, u32[]{:S(2)}) collective-permute-start(bf16[2,128,128]{2,1,0:T(8,128)(2,1)S(1)} %copy-done.63), channel_id=1, source_target_pairs={{0,6},{1,7},{2,4},{3,5},{4,2},{5,3},{6,0},{7,1},{8,14},{9,15},{10,... | collective-permute-start | bytes 196616 | tf_op jit(solution)/shard_map/ppermute | solution.py:904
  169.7 8.9 %collective-permute-start.42 = (bf16[2,128,128]{2,1,0:T(8,128)(2,1)S(1)}, bf16[2,128,128]{2,1,0:T(8,128)(2,1)S(1)}, u32[]{:S(2)}, u32[]{:S(2)}) collective-permute-start(bf16[2,128,128]{2,1,0:T(8,128)(2,1)S(1)} %copy-done.60), channel_id=1, source_target_pairs={{0,1},{1,0},{2,3},{3,2},{4,5},{5,4},{6,7},{7,6},{8,9},{9,8},{10,11... | collective-permute-start | bytes 196616 | tf_op jit(solution)/shard_map/ppermute | solution.py:922
  170.9 9.4 %collective-permute-start.43 = (bf16[2,128,128]{2,1,0:T(8,128)(2,1)S(1)}, bf16[2,128,128]{2,1,0:T(8,128)(2,1)S(1)}, u32[]{:S(2)}, u32[]{:S(2)}) collective-permute-start(bf16[2,128,128]{2,1,0:T(8,128)(2,1)S(1)} %collective-permute-done.35.refs_5_), channel_id=1, source_target_pairs={{0,1},{1,0},{2,3},{3,2},{4,5},{5,4},{6,7},{7,6},{8,9},{9,8},{10,11... | collective-permute-start | bytes 196616 | tf_op jit(solution)/shard_map/ppermute | solution.py:922
  170.9 9.6 %collective-permute-start.44 = (bf16[2,128,128]{2,1,0:T(8,128)(2,1)S(1)}, bf16[2,128,128]{2,1,0:T(8,128)(2,1)S(1)}, u32[]{:S(2)}, u32[]{:S(2)}) collective-permute-start(bf16[2,128,128]{2,1,0:T(8,128)(2,1)S(1)} %collective-permute-done.36.refs_6_), channel_id=1, source_target_pairs={{0,1},{1,0},{2,3},{3,2},{4,5},{5,4},{6,7},{7,6},{8,9},{9,8},{10,11... | collective-permute-start | bytes 196616 | tf_op jit(solution)/shard_map/ppermute | solution.py:922
  171.4 10.4 %collective-permute-start.45 = (bf16[2,128,128]{2,1,0:T(8,128)(2,1)S(1)}, bf16[2,128,128]{2,1,0:T(8,128)(2,1)S(1)}, u32[]{:S(2)}, u32[]{:S(2)}) collective-permute-start(bf16[2,128,128]{2,1,0:T(8,128)(2,1)S(1)} %collective-permute-done.37.refs_7_), channel_id=1, source_target_pairs={{0,1},{1,0},{2,3},{3,2},{4,5},{5,4},{6,7},{7,6},{8,9},{9,8},{10,11... | collective-permute-start | bytes 196616 | tf_op jit(solution)/shard_map/ppermute | solution.py:922
  172.1 24.9 %collective-permute-start.52 = (bf16[2,64,128]{2,1,0:T(8,128)(2,1)}, bf16[2,64,128]{2,1,0:T(8,128)(2,1)}, u32[]{:S(2)}, u32[]{:S(2)}) collective-permute-start(bf16[2,64,128]{2,1,0:T(8,128)(2,1)} %get-tuple-element.349), channel_id=1, source_target_pairs={{0,2},{1,3},{2,0},{3,1},{4,6},{5,7},{6,4},{7,5},{8,10},{9,11},{10,... | collective-permute-start | bytes 98312 | tf_op jit(solution)/shard_map/ppermute | solution.py:953
  172.8 53.0 %all-to-all-start.1 = ((bf16[4,1536,256]{2,1,0:T(8,128)(2,1)}), bf16[4,1536,256]{2,1,0:T(8,128)(2,1)}, u32[]{:S(2)}, u32[]{:S(2)}) async-start(bf16[4,1536,256]{2,1,0:T(8,128)(2,1)} %row_grad.1), calls=%async_computation.1 | async-start | bytes 6291456 | tf_op jit(solution)/shard_map/all_to_all | solution.py:689
  178.6 18.9 %collective-permute-start.53 = (bf16[2,64,128]{2,1,0:T(8,128)(2,1)}, bf16[2,64,128]{2,1,0:T(8,128)(2,1)}, u32[]{:S(2)}, u32[]{:S(2)}) collective-permute-start(bf16[2,64,128]{2,1,0:T(8,128)(2,1)} %get-tuple-element.351), channel_id=1, source_target_pairs={{0,4},{1,5},{2,6},{3,7},{4,0},{5,1},{6,2},{7,3},{8,12},{9,13},{10,... | collective-permute-start | bytes 98312 | tf_op jit(solution)/shard_map/ppermute | solution.py:953
  180.3 17.4 %collective-permute-start.54 = (bf16[2,64,128]{2,1,0:T(8,128)(2,1)}, bf16[2,64,128]{2,1,0:T(8,128)(2,1)}, u32[]{:S(2)}, u32[]{:S(2)}) collective-permute-start(bf16[2,64,128]{2,1,0:T(8,128)(2,1)} %get-tuple-element.350), channel_id=1, source_target_pairs={{0,6},{1,7},{2,4},{3,5},{4,2},{5,3},{6,0},{7,1},{8,14},{9,15},{10,... | collective-permute-start | bytes 98312 | tf_op jit(solution)/shard_map/ppermute | solution.py:953
  180.5 15.4 %collective-permute-start.46 = (bf16[128,1024]{1,0:T(8,128)(2,1)}, bf16[128,1024]{1,0:T(8,128)(2,1)}, u32[]{:S(2)}, u32[]{:S(2)}) collective-permute-start(bf16[128,1024]{1,0:T(8,128)(2,1)} %get-tuple-element.275), channel_id=1, source_target_pairs={{0,6},{1,7},{2,4},{3,5},{4,2},{5,3},{6,0},{7,1},{8,14},{9,15},{10,... | collective-permute-start | bytes 786440 | tf_op jit(solution)/shard_map/ppermute | solution.py:924
  195.9 4.3 %collective-permute-start.47 = (bf16[128,1024]{1,0:T(8,128)(2,1)}, bf16[128,1024]{1,0:T(8,128)(2,1)S(1)}, u32[]{:S(2)}, u32[]{:S(2)}) collective-permute-start(bf16[128,1024]{1,0:T(8,128)(2,1)} %get-tuple-element.280.refs_11_), channel_id=1, source_target_pairs={{0,1},{1,0},{2,3},{3,2},{4,5},{5,4},{6,7},{7,6},{8,9},{9,8},{10,11... | collective-permute-start | bytes 786440 | tf_op jit(solution)/shard_map/ppermute | solution.py:950
  197.0 3.2 %collective-permute-start.48 = (bf16[128,1024]{1,0:T(8,128)(2,1)}, bf16[128,1024]{1,0:T(8,128)(2,1)S(1)}, u32[]{:S(2)}, u32[]{:S(2)}) collective-permute-start(bf16[128,1024]{1,0:T(8,128)(2,1)} %get-tuple-element.281.refs_12_), channel_id=1, source_target_pairs={{0,1},{1,0},{2,3},{3,2},{4,5},{5,4},{6,7},{7,6},{8,9},{9,8},{10,11... | collective-permute-start | bytes 786440 | tf_op jit(solution)/shard_map/ppermute | solution.py:950
  197.0 3.2 %collective-permute-start.49 = (bf16[128,1024]{1,0:T(8,128)(2,1)}, bf16[128,1024]{1,0:T(8,128)(2,1)S(1)}, u32[]{:S(2)}, u32[]{:S(2)}) collective-permute-start(bf16[128,1024]{1,0:T(8,128)(2,1)} %get-tuple-element.282.refs_13_), channel_id=1, source_target_pairs={{0,1},{1,0},{2,3},{3,2},{4,5},{5,4},{6,7},{7,6},{8,9},{9,8},{10,11... | collective-permute-start | bytes 786440 | tf_op jit(solution)/shard_map/ppermute | solution.py:950
  197.6 27.4 %collective-permute-start.55 = (bf16[1024,256]{1,0:T(8,128)(2,1)S(1)}, bf16[1024,256]{1,0:T(8,128)(2,1)S(1)}, u32[]{:S(2)}, u32[]{:S(2)}) collective-permute-start(bf16[1024,256]{1,0:T(8,128)(2,1)S(1)} %copy-done.24), channel_id=1, source_target_pairs={{0,24},{8,16},{16,8},{24,0},{1,25},{9,17},{17,9},{25,1},{2,26},{10... | collective-permute-start | bytes 1572872 | tf_op jit(solution)/shard_map/ppermute | solution.py:921
  205.1 20.6 %collective-permute-start.56 = (bf16[128,1024]{1,0:T(8,128)(2,1)}, bf16[128,1024]{1,0:T(8,128)(2,1)S(1)}, u32[]{:S(2)}, u32[]{:S(2)}) collective-permute-start(bf16[128,1024]{1,0:T(8,128)(2,1)} %get-tuple-element.300), channel_id=1, source_target_pairs={{0,2},{1,3},{2,0},{3,1},{4,6},{5,7},{6,4},{7,5},{8,10},{9,11},{10,... | collective-permute-start | bytes 786440 | tf_op jit(solution)/shard_map/ppermute | solution.py:957
  207.1 18.7 %collective-permute-start.57 = (bf16[128,1024]{1,0:T(8,128)(2,1)}, bf16[128,1024]{1,0:T(8,128)(2,1)}, u32[]{:S(2)}, u32[]{:S(2)}) collective-permute-start(bf16[128,1024]{1,0:T(8,128)(2,1)} %get-tuple-element.301), channel_id=1, source_target_pairs={{0,4},{1,5},{2,6},{3,7},{4,0},{5,1},{6,2},{7,3},{8,12},{9,13},{10,... | collective-permute-start | bytes 786440 | tf_op jit(solution)/shard_map/ppermute | solution.py:957
  225.8 26.6 %all-to-all-start.2 = ((bf16[4,704,256]{2,1,0:T(8,128)(2,1)}), bf16[4,704,256]{2,1,0:T(8,128)(2,1)S(1)}, u32[]{:S(2)}, u32[]{:S(2)}) async-start(bf16[4,704,256]{2,1,0:T(8,128)(2,1)} %self_grad.1), calls=%async_computation.2 | async-start | bytes 2883584 | tf_op jit(solution)/shard_map/all_to_all | solution.py:689
  233.6 5.8 %collective-permute-start.58 = (bf16[384,256]{1,0:T(8,128)(2,1)S(1)}, bf16[384,256]{1,0:T(8,128)(2,1)S(1)}, u32[]{:S(2)}, u32[]{:S(2)}) collective-permute-start(bf16[384,256]{1,0:T(8,128)(2,1)S(1)} %get-tuple-element.336), channel_id=1, source_target_pairs={{0,2},{1,3},{2,0},{3,1},{4,6},{5,7},{6,4},{7,5},{8,10},{9,11},{10,... | collective-permute-start | bytes 589832 | tf_op jit(solution)/shard_map/ppermute | solution.py:985
  234.4 9.0 %collective-permute-start.59 = (bf16[384,256]{1,0:T(8,128)(2,1)S(1)}, bf16[384,256]{1,0:T(8,128)(2,1)S(1)}, u32[]{:S(2)}, u32[]{:S(2)}) collective-permute-start(bf16[384,256]{1,0:T(8,128)(2,1)S(1)} %get-tuple-element.335), channel_id=1, source_target_pairs={{0,4},{1,5},{2,6},{3,7},{4,0},{5,1},{6,2},{7,3},{8,12},{9,13},{10,... | collective-permute-start | bytes 589832 | tf_op jit(solution)/shard_map/ppermute | solution.py:985
  236.0 16.3 %collective-permute-start.60 = (bf16[384,256]{1,0:T(8,128)(2,1)S(1)}, bf16[384,256]{1,0:T(8,128)(2,1)S(1)}, u32[]{:S(2)}, u32[]{:S(2)}) collective-permute-start(bf16[384,256]{1,0:T(8,128)(2,1)S(1)} %get-tuple-element.334), channel_id=1, source_target_pairs={{0,6},{1,7},{2,4},{3,5},{4,2},{5,3},{6,0},{7,1},{8,14},{9,15},{10,... | collective-permute-start | bytes 589832 | tf_op jit(solution)/shard_map/ppermute | solution.py:985
  252.9 8.2 %collective-permute-start.62 = (bf16[80,512]{1,0:T(8,128)(2,1)S(1)}, bf16[80,512]{1,0:T(8,128)(2,1)S(1)}, u32[]{:S(2)}, u32[]{:S(2)}) collective-permute-start(bf16[80,512]{1,0:T(8,128)(2,1)S(1)} %constant_dynamic-slice_fusion), channel_id=1, source_target_pairs={{0,1},{1,0},{2,3},{3,2},{4,5},{5,4},{6,7},{7,6},{8,9},{9,8},{10,11... | collective-permute-start | bytes 245768 | tf_op jit(solution)/shard_map/ppermute | solution.py:1010
  257.0 38.0 %all-to-all-start.3 = ((bf16[4,1024,256]{2,1,0:T(8,128)(2,1)}), bf16[4,1024,256]{2,1,0:T(8,128)(2,1)S(1)}, u32[]{:S(2)}, u32[]{:S(2)}) async-start(bf16[4,1024,256]{2,1,0:T(8,128)(2,1)} %broadcast_in_dim.20), calls=%async_computation.3 | async-start | bytes 4194304 | tf_op jit(solution)/shard_map/all_to_all | solution.py:674
  261.1 5.2 %collective-permute-start.63 = (bf16[80,512]{1,0:T(8,128)(2,1)S(1)}, bf16[80,512]{1,0:T(8,128)(2,1)S(1)}, u32[]{:S(2)}, u32[]{:S(2)}) collective-permute-start(bf16[80,512]{1,0:T(8,128)(2,1)S(1)} %add_convert_fusion.8), channel_id=1, source_target_pairs={{0,2},{1,3},{2,0},{3,1},{4,6},{5,7},{6,4},{7,5},{8,10},{9,11},{10,... | collective-permute-start | bytes 245768 | tf_op jit(solution)/shard_map/ppermute | solution.py:1011
  261.1 7.4 %collective-permute-start.64 = (bf16[80,512]{1,0:T(8,128)(2,1)S(1)}, bf16[80,512]{1,0:T(8,128)(2,1)S(1)}, u32[]{:S(2)}, u32[]{:S(2)}) collective-permute-start(bf16[80,512]{1,0:T(8,128)(2,1)S(1)} %add_convert_fusion.8), channel_id=1, source_target_pairs={{0,4},{1,5},{2,6},{3,7},{4,0},{5,1},{6,2},{7,3},{8,12},{9,13},{10,... | collective-permute-start | bytes 245768 | tf_op jit(solution)/shard_map/ppermute | solution.py:1011
  263.5 13.4 %collective-permute-start.65 = (bf16[80,512]{1,0:T(8,128)(2,1)S(1)}, bf16[80,512]{1,0:T(8,128)(2,1)S(1)}, u32[]{:S(2)}, u32[]{:S(2)}) collective-permute-start(bf16[80,512]{1,0:T(8,128)(2,1)S(1)} %add_convert_fusion.8), channel_id=1, source_target_pairs={{0,6},{1,7},{2,4},{3,5},{4,2},{5,3},{6,0},{7,1},{8,14},{9,15},{10,... | collective-permute-start | bytes 245768 | tf_op jit(solution)/shard_map/ppermute | solution.py:1011
  265.1 20.6 %collective-permute-start.61 = (bf16[128,1024]{1,0:T(8,128)(2,1)}, bf16[128,1024]{1,0:T(8,128)(2,1)S(1)}, u32[]{:S(2)}, u32[]{:S(2)}) collective-permute-start(bf16[128,1024]{1,0:T(8,128)(2,1)} %get-tuple-element.321), channel_id=1, source_target_pairs={{0,6},{1,7},{2,4},{3,5},{4,2},{5,3},{6,0},{7,1},{8,14},{9,15},{10,... | collective-permute-start | bytes 786440 | tf_op jit(solution)/shard_map/ppermute | solution.py:957
  276.9 13.8 %collective-permute-start.66 = (f32[80,512]{1,0:T(8,128)S(1)}, f32[80,512]{1,0:T(8,128)S(1)}, u32[]{:S(2)}, u32[]{:S(2)}) collective-permute-start(f32[80,512]{1,0:T(8,128)S(1)} %get-tuple-element.333), channel_id=1, source_target_pairs={{0,1},{1,0},{2,3},{3,2},{4,5},{5,4},{6,7},{7,6},{8,9},{9,8},{10,11... | collective-permute-start | bytes 491528 | tf_op jit(solution)/shard_map/ppermute | solution.py:1013
  (78 other events, 659.8 us)
where the time goes:
time: 303 us; the launch traced here: 301 us
  Pallas kernels  111 us (37%)
  starting transfers between devices  91.5 us (30%)
  waiting for transfers between devices  57.8 us (19%)
  local copies, waits for them, and re-layouts  25.1 us (8%)
  other arithmetic  11.8 us (4%)
  between operations  3.71 us (1%)
    pallas_call x19, Pallas kernels, call(): pl.pallas_call(kernel, out_shape=out_shape, in_specs=[pl.BlockSpec(memory...  111 us
    unnamed x144, local copies, waits for them, and re-layouts  17.2 us
    all_to_all x3, starting transfers between devices, swap_dp(): return lax.all_to_all(pieces, 'dp', 0, 0)  15.9 us
    ppermute x3, waiting for transfers between devices, body(): row_parts = [row_piece[0]] + [to_z[k](row_piece[k]) for k in far]  15.8 us
    ppermute x3, waiting for transfers between devices, body(): state_half = total(state_half, *[to_z[k](state_half) for k in far])  10.6 us
    ppermute x4, starting transfers between devices, body(): att2 = [to_core(x) for x in att]  9.3 us
    ppermute x1, waiting for transfers between devices, body(): mlp_all += [to_dp[q](mlp_all[0]) for q in range(3, dps)]  7.58 us
    ppermute x1, starting transfers between devices, body(): n3s[2] = to_z[1](n3s[3])  6.9 us
  transfers between devices with their start and end apart: 71, of which 23 were waited for; matrix products, arithmetic and copies ran while one was open for 7% of the time, Pallas kernels for 32%

commit v1 on v0

--- a/solution.py
+++ b/solution.py
@@ -82,13 +82,13 @@
 
 
 def call(
-    kernel, outs, idx, *args, scratch=(), after=(), stage=False, tight=False, raw=(), cost=1, name=None, spill=8
+    kernel, outs, idx, *args, scratch=(), after=(), stage=False, tight=False, raw=(), near=(), sent=(), cost=1, name=None, spill=8
 ):
     if after:
         idx = lax.optimization_barrier((idx, *after))[0]
     out_shape = [jax.ShapeDtypeStruct(s, t) for s, t in outs]
     big = lambda a: bool(stage) and a.size >= 1 << 15
-    ins_far = [big(a) and i not in raw for i, a in enumerate(args)]
+    ins_far = [big(a) and i not in raw and i not in near for i, a in enumerate(args)]
     outs_far = [big(a) for a in out_shape]
     vmem = pl.BlockSpec(memory_space=pltpu.VMEM)
     hbm = pl.BlockSpec(memory_space=pltpu.HBM)
@@ -99,6 +99,7 @@
     for a in scratch:
         if len(getattr(a, "shape", ())) > 1 and a.dtype in (F32, BF16):
             held += math.prod(a.shape) * jnp.dtype(a.dtype).itemsize
+    out_shape = [pltpu.HBM(a.shape, a.dtype) if i in sent else a for i, a in enumerate(out_shape)]
     scratch = list(scratch)
     if any(ins_far) or any(outs_far):
         kernel = functools.partial(staged, kernel, ins_far, outs_far, len(scratch))
@@ -112,7 +113,7 @@
         out_shape=out_shape,
         in_specs=[pl.BlockSpec(memory_space=pltpu.SMEM)]
         + [hbm if far or i in raw else vmem for i, far in enumerate(ins_far)],
-        out_specs=[hbm if far else vmem for far in outs_far],
+        out_specs=[hbm if far or i in sent else vmem for i, far in enumerate(outs_far)],
         scratch_shapes=scratch,
         cost_estimate=pl.CostEstimate(flops=cost, bytes_accessed=1, transcendentals=0),
         compiler_params=pltpu.CompilerParams(
@@ -292,11 +293,15 @@
         outs[k][...] = part[k]
 
 
-def hidden_kernel(idx, same, other, weight, bias, grad_active, n3_o, act_o, ghi_o, bs_o, bo_o, back):
+def hidden_kernel(idx, same, other, weight, bias, grad_active, *rest):
+    n3_h, act_h, ghi_h, bs_o, bo_o, back, n3_o, act_o, ghi_o, sem = rest
     own = same.shape[0]
     core = lax.rem(idx[0], 2)
+    pairs = ((n3_o, n3_h), (act_o, act_h), (ghi_o, ghi_h))
+    keep = [pltpu.make_async_copy(a, b, sem.at[i]) for i, (a, b) in enumerate(pairs)]
     n3_o[at(core, own), :] = same[...]
     n3_o[at(1 - core, own), :] = other[...]
+    keep[0].start()
     v = dot_nn(n3_o[...], weight[...]) + bias[...].astype(F32)
     root = 0.7978845608028654
     square = v * v
@@ -305,11 +310,15 @@
     slope = 0.5 * (1.0 + t) + 0.5 * v * (1.0 - t * t) * (root * (1.0 + 0.134145 * square))
     ghi = (grad_active[...] * slope).astype(BF16)
     ghi_o[...] = ghi
+    keep[1].start()
+    keep[2].start()
     back[...] = dot_nt(ghi, weight[...])
     bs_o[...] = back[at(core, own), :].astype(BF16)
     dim = back.shape[1]
     bo_o[:, 0:dim] = back[at(1 - core, own), :].astype(BF16)
     bo_o[:, dim:] = act_o[at(1 - core, own), :]
+    for copy in keep:
+        copy.wait()
 
 
 def mlp_out_kernel(chips, idx, weight, weight2, *rest):
@@ -567,9 +576,16 @@
 
 def add_kernel(idx, *refs):
     count = len(refs) // 3
-    for k in range(count):
-        total = refs[k][...].astype(F32) + refs[count + k][...].astype(F32)
-        refs[2 * count + k][...] = total.astype(BF16)
+    step = math.gcd(refs[0].shape[0], 32)
+
+    def add_rows(i, carry):
+        here = at(i, step)
+        for k in range(count):
+            total = refs[k][here, :].astype(F32) + refs[count + k][here, :].astype(F32)
+            refs[2 * count + k][here, :] = total.astype(BF16)
+        return carry
+
+    lax.fori_loop(0, refs[0].shape[0] // step, add_rows, 0)
 
 
 def sum_kernel(idx, pieces, out):
@@ -804,7 +820,14 @@
             hidden_weight,
             bias_row,
             grad_active[k],
-            scratch=[pltpu.VMEM((2 * own, dim), F32)],
+            scratch=[
+                pltpu.VMEM((2 * own, dim), F32),
+                pltpu.VMEM((2 * own, dim), BF16),
+                pltpu.VMEM((2 * own, hid), BF16),
+                pltpu.VMEM((2 * own, hid), BF16),
+                pltpu.SemaphoreType.DMA((3,)),
+            ],
+            sent=(0, 1, 2),
             after=done,
             tight=True,
             name="hidden",
@@ -954,7 +977,7 @@
 
     *bos, gp = lax.optimization_barrier((*bos, gp))
     sent = add_all(bs, bos, "self_add")
-    parts = sent[:1] + [to_z[k](sent[k]) for k in far]
+    parts = sent[:1] + [to_z[k](sent[k]) for k in far[:2]]
 
     (self_part,) = call(
         functools.partial(self_grad_kernel, chips, dps),
@@ -983,7 +1006,8 @@
     self_swap = swap_dp(self_part)
     row_piece = sum_dp(row_swap).reshape(chips, 3 * width, cut)
     row_parts = [row_piece[0]] + [to_z[k](row_piece[k]) for k in far]
-    row_parts, self_swap = lax.optimization_barrier((row_parts, self_swap))
+    row_parts, self_swap, sent = lax.optimization_barrier((row_parts, self_swap, sent))
+    parts += [to_z[k](sent[k]) for k in far[2:]]
     row_piece = total(*row_parts).astype(BF16)
     self_sum = sum_dp(self_swap)
     piece = jnp.concatenate([row_piece, self_sum[: 5 * width]], 0)
@@ -1008,16 +1032,8 @@
     core = lax.rem(me, 2)
     half_of = lambda c: lax.dynamic_slice_in_dim(state_part, c * (dim // 2), dim // 2, 1)
     state_half = total(half_of(core), to_core(half_of(1 - core))).astype(BF16)
-    state_half = total(state_half, *[to_z[k](state_half) for k in far])
-    state_sum = jnp.zeros((state_part.shape[0], dim), F32)
-    for c, part in ((core, state_half), (1 - core, to_core(state_half))):
-        state_sum = lax.dynamic_update_slice(state_sum, part, (0, c * (dim // 2)))
-    grad_states = lax.dynamic_update_slice(
-        jnp.zeros(states.shape, F32), state_sum[None, :SEEN], (state_row[0], begin, 0)
-    )
-    stats = state_sum[SEEN:]
-
-    def place(pieces, plan, shapes, name):
+    state_got = [to_z[k](state_half) for k in far]
+    def place(pieces, plan, shapes, name, **kept):
         return call(
             functools.partial(place_kernel, plan),
             [(s, F32) for s in shapes],
@@ -1025,15 +1041,25 @@
             *pieces,
             stage=True,
             name=name,
+            **kept,
         )
 
     block_output = (second + total(*mlp_parts) + output_bias.astype(F32)).astype(BF16)
     grad_output_weight, grad_hidden_weight = place(
         mlp_all, ((hid, None, False), (hid, None, True)), ((hid, dim), (dim, hid)), "place_mlp"
     )
-    swapped, block_output, grad_output_weight, grad_tokens, state_sum = lax.optimization_barrier(
-        (swapped, block_output, grad_output_weight, grad_tokens, state_sum)
-    )
+    state_got, block_output, grad_output_weight, grad_tokens = lax.optimization_barrier(
+        (state_got, block_output, grad_output_weight, grad_tokens)
+    )
+    state_half = total(state_half, *state_got)
+    state_sum = jnp.zeros((state_part.shape[0], dim), F32)
+    for c, part in ((core, state_half), (1 - core, to_core(state_half))):
+        state_sum = lax.dynamic_update_slice(state_sum, part, (0, c * (dim // 2)))
+    grad_states = lax.dynamic_update_slice(
+        jnp.zeros(states.shape, F32), state_sum[None, :SEEN], (state_row[0], begin, 0)
+    )
+    stats = state_sum[SEEN:]
+    swapped, state_sum = lax.optimization_barrier((swapped, state_sum))
     (
         grad_self_output,
         grad_cross_query,
@@ -1057,6 +1083,8 @@
             (2, dim, width),
         ),
         "place",
+        near=(0,),
+        tight=True,
     )
     grad_norm_gain = jnp.stack([stats[0], stats[4], stats[2]])
     grad_norm_shift = jnp.stack([stats[1], stats[5], stats[3]])

time: 303 us -> 295 us (0.974)
  local copies, waits for them, and re-layouts: 25.1 us -> 17.7 us
  waiting for transfers between devices: 57.8 us -> 53 us
    ppermute x6, waiting for transfers between devices: 10.6 us -> 0.02 us  [the longest x3 0.01 us: body(): state_got = [to_z[k](state_half) for k in far]]
    unnamed x144 -> x118, local copies, waits for them, and re-layouts: 17.2 us -> 9.18 us
    ppermute x1, starting transfers between devices: 2.53 us -> 5.63 us  [body(): state_half = total(half_of(core), to_core(half_of(1 - core))).astype(BF16)]
  transfers between devices with their start and end apart: 71 -> 71, of which waited for: 23 -> 22; matrix products, arithmetic and copies ran while one was open for 7% -> 8% of each run, Pallas kernels for 32% -> 33%
where the time goes in v1:
time: 295 us; the launch traced here: 293 us
  Pallas kernels  111 us (38%)
  starting transfers between devices  94.1 us (32%)
  waiting for transfers between devices  53 us (18%)
  local copies, waits for them, and re-layouts  17.7 us (6%)
  other arithmetic  13.7 us (5%)
  between operations  3.65 us (1%)
    pallas_call x19, Pallas kernels, call(): pl.pallas_call(kernel, out_shape=out_shape, in_specs=[pl.BlockSpec(memory...  111 us
    ppermute x3, waiting for transfers between devices, body(): row_parts = [row_piece[0]] + [to_z[k](row_piece[k]) for k in far]  16 us
    all_to_all x3, starting transfers between devices, swap_dp(): return lax.all_to_all(pieces, 'dp', 0, 0)  15.9 us
    unnamed x118, local copies, waits for them, and re-layouts  9.18 us
    ppermute x4, starting transfers between devices, body(): att2 = [to_core(x) for x in att]  9.15 us
    ppermute x1, waiting for transfers between devices, body(): mlp_all += [to_dp[q](mlp_all[0]) for q in range(3, dps)]  7.33 us
    ppermute x1, starting transfers between devices, body(): n3s[2] = to_z[1](n3s[3])  6.92 us
  transfers between devices with their start and end apart: 71, of which 22 were waited for; matrix products, arithmetic and copies ran while one was open for 8% of the time, Pallas kernels for 33%

profile of v1, /device:TPU:11, one launch (start us, length us, event | category | flops | bytes accessed | tf_op | source)
XLA Modules:
  0.0 293.4 jit_solution(6293361538934961162)
XLA Ops:
  3.9 2.3 collective-permute-start.1
  8.3 13.3 %self_fwd.1 = (bf16[1024,1024]{1,0:T(8,128)(2,1)}, bf16[3,1024,128]{2,1,0:T(8,128)(2,1)}, bf16[2,1024,1024]{2,1,0:T(8,128)(2,1)}, bf16[384,128]{1,0:T(8,128)(2,1...) custom-call(s32[4]{0:T(128)} %pad_add_fusion.refs_0_.idx, ...), custom_call_target="tpu_custom_call" | custom-call | flops 1 | bytes 1 | tf_op jit(solution)/shard_map/self_fwd/pallas_call | solution.py:111
  21.6 2.1 collective-permute-done.2.refs_2_
  24.6 1.2 collective-permute-start.5
  27.0 2.5 collective-permute-start.13
  29.5 1.5 collective-permute-done.12.refs_16_.refs_21_
  31.0 1.3 collective-permute-start.14
  33.0 4.2 %collective-permute-start.7 = (bf16[384,1024]{1,0:T(8,128)(2,1)S(1)}, bf16[384,1024]{1,0:T(8,128)(2,1)}, u32[]{:S(2)}, u32[]{:S(2)}) collective-permute-start(bf16[384,1024]{1,0:T(8,128)(2,1)S(1)} %pad_maximum_fusion.refs_5_.refs_7_), channel_id=1, source_target_pairs={{0,1},{1,0},{2,3},{3,2},{4,5},{5,4},{6,7},{7,6},{8,9},{9,8},{10,11... | collective-permute-start | bytes 2359304 | tf_op jit(solution)/shard_map/ppermute | solution.py:767
  37.2 6.0 %grad_active.1 = (f32[256,512]{1,0:T(8,128)}, f32[256,512]{1,0:T(8,128)}, f32[256,512]{1,0:T(8,128)}, f32[256,512]{1,0:T(8,128)}) custom-call(s32[4]{0:T(128)} %pad_add_fusion.refs_0_.idx, bf16[1024,1024]{1,0:T(8,128)(2,1)} %refs_1_.13, bf16[512,1024]{1,0:T(8,128)(2,1)} %refs_1_.12), custom_call_target="tpu_custom_call" | custom-call | flops 1 | bytes 1 | tf_op jit(solution)/shard_map/grad_active/pallas_call | solution.py:111
  45.1 7.0 %collective-permute-start.17 = (bf16[384,128]{1,0:T(8,128)(2,1)}, bf16[384,128]{1,0:T(8,128)(2,1)}, u32[]{:S(2)}, u32[]{:S(2)}) collective-permute-start(bf16[384,128]{1,0:T(8,128)(2,1)} %collective-permute-done.13.refs_17_.refs_22_), channel_id=1, source_target_pairs={{0,1},{1,0},{2,3},{3,2},{4,5},{5,4},{6,7},{7,6},{8,9},{9,8},{10,11... | collective-permute-start | bytes 294920 | tf_op jit(solution)/shard_map/ppermute | solution.py:751
  52.1 1.6 collective-permute-start.18
  55.5 1.2 collective-permute-done.10.refs_13_.refs_15_
  59.4 10.6 %cross_fwd.1 = (f32[128,1024]{1,0:T(8,128)}, bf16[3,128,1024]{2,1,0:T(8,128)(2,1)}, bf16[128,1024]{1,0:T(8,128)(2,1)}, bf16[8,128,128]{2,1,0:T(8,128)(2,1)}, f32...) custom-call(s32[4]{0:T(128)} %pad_add_fusion.refs_0_.idx, bf16[1024,1024]{1,0:T(8,128)(2,1)} %refs_1_.15, ...), custom_call_target="tpu_custom_call" | custom-call | flops 1 | bytes 1 | tf_op jit(solution)/shard_map/cross_fwd/pallas_call | solution.py:111
  70.2 1.4 collective-permute-start.22
  72.8 2.1 hidden.4
  74.9 3.0 %collective-permute-done.21.same = bf16[128,1024]{1,0:T(8,128)(2,1)S(1)} collective-permute-done((bf16[128,1024]{1,0:T(8,128)(2,1)}, bf16[128,1024]{1,0:T(8,128)(2,1)S(1)}, u32[]{:S(2)}, u32[]{:S(2)}) %collective-permute-start.21) | collective-permute-done | bytes 262176 | tf_op jit(solution)/shard_map/ppermute | solution.py:801
  77.9 2.0 collective-permute-start.23
  80.0 6.9 %collective-permute-start.26 = (bf16[128,1024]{1,0:T(8,128)(2,1)S(1)}, bf16[128,1024]{1,0:T(8,128)(2,1)S(1)}, u32[]{:S(2)}, u32[]{:S(2)}) collective-permute-start(bf16[128,1024]{1,0:T(8,128)(2,1)S(1)} %collective-permute-done.22.same), channel_id=1, source_target_pairs={{0,2},{1,3},{2,0},{3,1},{4,6},{5,7},{6,4},{7,5},{8,10},{9,11},{10,... | collective-permute-start | bytes 786440 | tf_op jit(solution)/shard_map/ppermute | solution.py:842
  87.0 2.1 hidden.5
  89.1 2.1 hidden.6
  95.4 2.2 hidden.7
  98.1 1.5 collective-permute-start.30
  100.2 5.7 %collective-permute-done.30 = bf16[128,1024]{1,0:T(8,128)(2,1)S(1)} collective-permute-done((bf16[128,1024]{1,0:T(8,128)(2,1)S(1)}, bf16[128,1024]{1,0:T(8,128)(2,1)S(1)}, u32[]{:S(2)}, u32[]{:S(2)}) %collective-permute-start.30) | collective-permute-done | bytes 262176 | tf_op jit(solution)/shard_map/ppermute | solution.py:845
  106.0 1.5 collective-permute-start.32
  107.6 1.8 collective-permute-start.38
  110.2 8.4 %mlp_grad.1 = bf16[4,1040,256]{2,1,0:T(8,128)(2,1)} custom-call(s32[4]{0:T(128)} %pad_add_fusion.refs_0_.idx, bf16[1024,1024]{1,0:T(8,128)(2,1)} %refs_1_.13, bf16[256,512]{1,0:T(8,128)(2,1)} %get-tuple-element.205.refs_2_.refs_3_, bf16[256,512]{1,0:T(8,128)(2,1)} %get-tuple-element.211.refs_3_.refs_4_, bf16[256,512]{1,0:T(8,128)(2,1)} %get-tuple-element.223.refs_4_.refs_5_, ...), custom_call_target="tpu_custom_call" | custom-call | flops 1 | bytes 1 | tf_op jit(solution)/shard_map/mlp_grad/pallas_call | solution.py:111
  119.4 5.3 %all-to-all-start = ((bf16[4,1040,256]{2,1,0:T(8,128)(2,1)}), bf16[4,1040,256]{2,1,0:T(8,128)(2,1)}, u32[]{:S(2)}, u32[]{:S(2)}) async-start(bf16[4,1040,256]{2,1,0:T(8,128)(2,1)} %mlp_grad.1), calls=%async_computation | async-start | bytes 4259840 | tf_op jit(solution)/shard_map/all_to_all | solution.py:705
  124.7 6.4 %mlp_out.1 = (bf16[128,1024]{1,0:T(8,128)(2,1)}, bf16[128,1024]{1,0:T(8,128)(2,1)}, bf16[128,1024]{1,0:T(8,128)(2,1)}, bf16[128,1024]{1,0:T(8,128)(2,1)}) custom-call(s32[4]{0:T(128)} %pad_add_fusion.refs_0_.idx, bf16[512,1024]{1,0:T(8,128)(2,1)} %refs_1_.12, bf16[512,1024]{1,0:T(8,128)(2,1)} %collective-permute-done.3.refs_2_, ...), custom_call_target="tpu_custom_call" | custom-call | flops 1 | bytes 1 | tf_op jit(solution)/shard_map/mlp_out/pallas_call | solution.py:111
  131.6 2.0 collective-permute-start.34
  133.6 12.5 %cross_bwd.1 = (bf16[3,128,1024]{2,1,0:T(8,128)(2,1)}, f32[128,1024]{1,0:T(8,128)}, f32[8,1024]{1,0:T(8,128)}, bf16[4,2,64,128]{3,2,1,0:T(8,128)(2,1)}, bf16[4,2...) custom-call(s32[4]{0:T(128)} %pad_add_fusion.refs_0_.idx, ...), custom_call_target="tpu_custom_call" | custom-call | flops 999999995904 | bytes 1 | tf_op jit(solution)/shard_map/cross_bwd/pallas_call | solution.py:111
  146.2 3.7 %all-to-all-done.refs_1_ = bf16[4,1040,256]{2,1,0:T(8,128)(2,1)} async-done(((bf16[4,1040,256]{2,1,0:T(8,128)(2,1)}), bf16[4,1040,256]{2,1,0:T(8,128)(2,1)}, u32[]{:S(2)}, u32[]{:S(2)}) %all-to-all-start) | async-done | bytes 2129952 | tf_op jit(solution)/shard_map/all_to_all | solution.py:705
  150.7 3.4 %sum_mlp.1.refs_1_ = bf16[1024,256]{1,0:T(8,128)(2,1)} custom-call(s32[4]{0:T(128)} %pad_add_fusion.refs_0_.idx, bf16[4,1040,256]{2,1,0:T(8,128)(2,1)} %all-to-all-done.refs_1_), custom_call_target="tpu_custom_call" | custom-call | flops 1 | bytes 1 | tf_op jit(solution)/shard_map/sum_mlp/pallas_call | solution.py:111
  154.5 1.2 collective-permute-start.41
  157.2 1.4 collective-permute-start.36
  159.5 5.4 %row_grad.1 = bf16[4,1536,256]{2,1,0:T(8,128)(2,1)} custom-call(s32[4]{0:T(128)} %pad_add_fusion.refs_0_.idx, bf16[3,128,1024]{2,1,0:T(8,128)(2,1)} %get-tuple-element.259.refs_1_, bf16[3,128,1024]{2,1,0:T(8,128)(2,1)} %collective-permute-done.38.refs_2_, bf16[3,128,1024]{2,1,0:T(8,128)(2,1)} %get-tuple-element.260.refs_3_, bf16[3,128,1024]{2,1,0:T(8,128)(2,1)} %copy-done.17), custom_call_target="tpu_custom_call" | custom-call | flops 1 | bytes 1 | tf_op jit(solution)/shard_map/row_grad/pallas_call | solution.py:111
  165.3 2.5 collective-permute-done.40.refs_2_
  170.7 5.8 %all-to-all-start.1 = ((bf16[4,1536,256]{2,1,0:T(8,128)(2,1)}), bf16[4,1536,256]{2,1,0:T(8,128)(2,1)}, u32[]{:S(2)}, u32[]{:S(2)}) async-start(bf16[4,1536,256]{2,1,0:T(8,128)(2,1)} %row_grad.1), calls=%async_computation.1 | async-start | bytes 6291456 | tf_op jit(solution)/shard_map/all_to_all | solution.py:705
  176.5 2.0 collective-permute-start.53
  178.7 1.2 collective-permute-start.46
  180.5 12.1 %self_bwd.1 = (bf16[1024,384]{1,0:T(8,128)(2,1)}, bf16[128,1024]{1,0:T(8,128)(2,1)}, bf16[128,1024]{1,0:T(8,128)(2,1)}, bf16[128,1024]{1,0:T(8,128)(2,1)}, bf16[...) custom-call(s32[4]{0:T(128)} %pad_add_fusion.refs_0_.idx, ...), custom_call_target="tpu_custom_call" | custom-call | flops 999999995904 | bytes 1 | tf_op jit(solution)/shard_map/self_bwd/pallas_call | solution.py:111
  192.7 1.4 collective-permute-done.46
  195.8 1.2 collective-permute-start.55
  197.0 1.5 fusion.3.refs_5_
  200.1 3.4 %self_add.1 = (bf16[128,1024]{1,0:T(8,128)(2,1)}, bf16[128,1024]{1,0:T(8,128)(2,1)}, bf16[128,1024]{1,0:T(8,128)(2,1)}, bf16[128,1024]{1,0:T(8,128)(2,1)}) custom-call(s32[4]{0:T(128)} %pad_add_fusion.refs_0_.idx, bf16[128,1024]{1,0:T(8,128)(2,1)} %get-tuple-element.287.refs_1_.refs_7_, bf16[128,1024]{1,0:T(8,128)(2,1)} %get-tuple-element.288.refs_2_.refs_8_, ...), custom_call_target="tpu_custom_call" | custom-call | flops 1 | bytes 1 | tf_op jit(solution)/shard_map/self_add/pallas_call | solution.py:111
  203.5 1.3 collective-permute-start.56
  205.6 1.6 dynamic-slice_bitcast_fusion.refs_4_
  207.2 8.3 %self_grad.1 = bf16[4,704,256]{2,1,0:T(8,128)(2,1)} custom-call(s32[4]{0:T(128)} %pad_add_fusion.refs_0_.idx, bf16[1024,1024]{1,0:T(8,128)(2,1)} %refs_1_.15, bf16[1024,1024]{1,0:T(8,128)(2,1)} %get-tuple-element.297.refs_2_, bf16[1024,384]{1,0:T(8,128)(2,1)} %get-tuple-element.298.refs_3_, bf16[64,1024]{1,0:T(8,128)(2,1)} %dynamic-slice_bitcast_fusion.refs_4_, ...), custom_call_target="tpu_custom_call" | custom-call | flops 1 | bytes 1 | tf_op jit(solution)/shard_map/self_grad/pallas_call | solution.py:111
  215.5 7.3 %collective-permute-done.55.refs_4_ = bf16[1024,256]{1,0:T(8,128)(2,1)S(1)} collective-permute-done((bf16[1024,256]{1,0:T(8,128)(2,1)S(1)}, bf16[1024,256]{1,0:T(8,128)(2,1)S(1)}, u32[]{:S(2)}, u32[]{:S(2)}) %collective-permute-start.55) | collective-permute-done | bytes 524320 | tf_op jit(solution)/shard_map/ppermute | solution.py:944
  223.7 4.8 %all-to-all-start.2 = ((bf16[4,704,256]{2,1,0:T(8,128)(2,1)}), bf16[4,704,256]{2,1,0:T(8,128)(2,1)S(1)}, u32[]{:S(2)}, u32[]{:S(2)}) async-start(bf16[4,704,256]{2,1,0:T(8,128)(2,1)} %self_grad.1), calls=%async_computation.2 | async-start | bytes 2883584 | tf_op jit(solution)/shard_map/all_to_all | solution.py:705
  228.5 2.9 reduce_sum.43
  234.4 3.7 %collective-permute-done.58 = bf16[384,256]{1,0:T(8,128)(2,1)S(1)} collective-permute-done((bf16[384,256]{1,0:T(8,128)(2,1)S(1)}, bf16[384,256]{1,0:T(8,128)(2,1)S(1)}, u32[]{:S(2)}, u32[]{:S(2)}) %collective-permute-start.58) | collective-permute-done | bytes 196640 | tf_op jit(solution)/shard_map/ppermute | solution.py:1008
  238.1 2.8 collective-permute-done.59
  240.9 9.5 %collective-permute-done.60 = bf16[384,256]{1,0:T(8,128)(2,1)S(1)} collective-permute-done((bf16[384,256]{1,0:T(8,128)(2,1)S(1)}, bf16[384,256]{1,0:T(8,128)(2,1)S(1)}, u32[]{:S(2)}, u32[]{:S(2)}) %collective-permute-start.60) | collective-permute-done | bytes 196640 | tf_op jit(solution)/shard_map/ppermute | solution.py:1008
  253.3 5.6 %collective-permute-start.61 = (bf16[80,512]{1,0:T(8,128)(2,1)}, bf16[80,512]{1,0:T(8,128)(2,1)}, u32[]{:S(2)}, u32[]{:S(2)}) collective-permute-start(bf16[80,512]{1,0:T(8,128)(2,1)} %constant_dynamic-slice_fusion), channel_id=1, source_target_pairs={{0,1},{1,0},{2,3},{3,2},{4,5},{5,4},{6,7},{7,6},{8,9},{9,8},{10,11... | collective-permute-start | bytes 245768 | tf_op jit(solution)/shard_map/ppermute | solution.py:1034
  260.0 1.4 broadcast_in_dim.23
  261.5 4.1 %all-to-all-start.3 = ((bf16[4,1024,256]{2,1,0:T(8,128)(2,1)}), bf16[4,1024,256]{2,1,0:T(8,128)(2,1)S(1)}, u32[]{:S(2)}, u32[]{:S(2)}) async-start(bf16[4,1024,256]{2,1,0:T(8,128)(2,1)} %broadcast_in_dim.23), calls=%async_computation.3 | async-start | bytes 4194304 | tf_op jit(solution)/shard_map/all_to_all | solution.py:690
  266.5 1.9 collective-permute-start.63
  269.2 2.0 add_convert_fusion
  271.2 4.7 %place_mlp.1 = (f32[512,1024]{1,0:T(8,128)}, f32[1024,512]{1,0:T(8,128)}) custom-call(s32[4]{0:T(128)} %pad_add_fusion.refs_0_.idx, bf16[1024,256]{1,0:T(8,128)(2,1)} %sum_mlp.1.refs_1_, bf16[1024,256]{1,0:T(8,128)(2,1)} %copy-done.25, bf16[1024,256]{1,0:T(8,128)(2,1)} %copy-done.26, bf16[1024,256]{1,0:T(8,128)(2,1)} %copy-done.27), custom_call_target="tpu_custom_call" | custom-call | flops 1 | bytes 1 | tf_op jit(solution)/shard_map/place_mlp/pallas_call | solution.py:111
  276.6 4.3 %tokens.1 = f32[128,1024]{1,0:T(8,128)} custom-call(s32[4]{0:T(128)} %pad_add_fusion.refs_0_.idx, bf16[1024,1024]{1,0:T(8,128)(2,1)} %refs_1_.15, bf16[3,1024]{1,0:T(4,128)(2,1)} %refs_2_.9, f32[128,1024]{1,0:T(8,128)} %get-tuple-element.319.refs_3_, bf16[128,1024]{1,0:T(8,128)(2,1)} %get-tuple-element.295.refs_4_, bf16[128,1024]{1,0:T(8,128)(2,1)} %copy-done.31, ...), custom_call_target="tpu_custom_call" | custom-call | flops 1 | bytes 1 | tf_op jit(solution)/shard_map/tokens/pallas_call | solution.py:111
  281.0 1.2 collective-permute-start.66
  284.7 1.7 dynamic_update_slice.11
  287.6 2.5 all-to-all-done.3.refs_1_
  290.2 3.0 %place.1 = (f32[128,1024]{1,0:T(8,128)}, f32[1024,128]{1,0:T(8,128)}, f32[128,1024]{1,0:T(8,128)}, f32[3,1024,128]{2,1,0:T(8,128)}, f32[2,1024,128]{2,1,0:T(8,128)}) custom-call(s32[4]{0:T(128)S(1)} %copy-done.9, bf16[4,1024,256]{2,1,0:T(8,128)(2,1)S(1)} %all-to-all-done.3.refs_1_), custom_call_target="tpu_custom_call" | custom-call | flops 1 | bytes 1 | tf_op jit(solution)/shard_map/place/pallas_call | solution.py:111
  (254 shorter events, 47.0 us)
Async XLA Ops:
  0.6 23.1 %collective-permute-start.3 = (bf16[512,1024]{1,0:T(8,128)(2,1)}, bf16[512,1024]{1,0:T(8,128)(2,1)}, u32[]{:S(2)}, u32[]{:S(2)}) collective-permute-start(bf16[512,1024]{1,0:T(8,128)(2,1)} %refs_1_.12), channel_id=1, source_target_pairs={{0,1},{1,0},{2,3},{3,2},{4,5},{5,4},{6,7},{7,6},{8,9},{9,8},{10,11... | collective-permute-start | bytes 3145736 | tf_op jit(solution)/shard_map/ppermute | solution.py:719
  3.6 17.9 %collective-permute-start = (bf16[384,256]{1,0:T(8,128)(2,1)S(1)}, bf16[384,256]{1,0:T(8,128)(2,1)S(1)}, u32[]{:S(2)}, u32[]{:S(2)}) collective-permute-start(bf16[384,256]{1,0:T(8,128)(2,1)S(1)} %constant_dynamic-slice_fusion.2), channel_id=1, source_target_pairs={{0,2},{1,3},{2,0},{3,1},{4,6},{5,7},{6,4},{7,5},{8,10},{9,11},{10,... | collective-permute-start | bytes 589832 | tf_op jit(solution)/shard_map/ppermute | solution.py:718
  3.9 17.7 %collective-permute-start.1 = (bf16[384,256]{1,0:T(8,128)(2,1)S(1)}, bf16[384,256]{1,0:T(8,128)(2,1)S(1)}, u32[]{:S(2)}, u32[]{:S(2)}) collective-permute-start(bf16[384,256]{1,0:T(8,128)(2,1)S(1)} %constant_dynamic-slice_fusion.2), channel_id=1, source_target_pairs={{0,4},{1,5},{2,6},{3,7},{4,0},{5,1},{6,2},{7,3},{8,12},{9,13},{10,... | collective-permute-start | bytes 589832 | tf_op jit(solution)/shard_map/ppermute | solution.py:718
  6.2 17.5 %collective-permute-start.2 = (bf16[384,256]{1,0:T(8,128)(2,1)S(1)}, bf16[384,256]{1,0:T(8,128)(2,1)S(1)}, u32[]{:S(2)}, u32[]{:S(2)}) collective-permute-start(bf16[384,256]{1,0:T(8,128)(2,1)S(1)} %constant_dynamic-slice_fusion.2), channel_id=1, source_target_pairs={{0,6},{1,7},{2,4},{3,5},{4,2},{5,3},{6,0},{7,1},{8,14},{9,15},{10,... | collective-permute-start | bytes 589832 | tf_op jit(solution)/shard_map/ppermute | solution.py:718
  24.3 20.3 %collective-permute-start.4 = (bf16[1152,256]{1,0:T(8,128)(2,1)S(1)}, bf16[1152,256]{1,0:T(8,128)(2,1)S(1)}, u32[]{:S(2)}, u32[]{:S(2)}) collective-permute-start(bf16[1152,256]{1,0:T(8,128)(2,1)S(1)} %pack.1.refs_6_.refs_8_), channel_id=1, source_target_pairs={{0,8},{8,0},{16,24},{24,16},{1,9},{9,1},{17,25},{25,17},{2,10},{10... | collective-permute-start | bytes 1769480 | tf_op jit(solution)/shard_map/ppermute | solution.py:765
  24.6 20.5 %collective-permute-start.5 = (bf16[1152,256]{1,0:T(8,128)(2,1)S(1)}, bf16[1152,256]{1,0:T(8,128)(2,1)S(1)}, u32[]{:S(2)}, u32[]{:S(2)}) collective-permute-start(bf16[1152,256]{1,0:T(8,128)(2,1)S(1)} %pack.1.refs_6_.refs_8_), channel_id=1, source_target_pairs={{0,16},{8,24},{16,0},{24,8},{1,17},{9,25},{17,1},{25,9},{2,18},{10... | collective-permute-start | bytes 1769480 | tf_op jit(solution)/shard_map/ppermute | solution.py:765
  25.9 26.2 %collective-permute-start.6 = (bf16[1152,256]{1,0:T(8,128)(2,1)S(1)}, bf16[1152,256]{1,0:T(8,128)(2,1)S(1)}, u32[]{:S(2)}, u32[]{:S(2)}) collective-permute-start(bf16[1152,256]{1,0:T(8,128)(2,1)S(1)} %pack.1.refs_6_.refs_8_), channel_id=1, source_target_pairs={{0,24},{8,16},{16,8},{24,0},{1,25},{9,17},{17,9},{25,1},{2,26},{10... | collective-permute-start | bytes 1769480 | tf_op jit(solution)/shard_map/ppermute | solution.py:765
  27.0 4.0 %collective-permute-start.12 = (bf16[384,128]{1,0:T(8,128)(2,1)}, bf16[384,128]{1,0:T(8,128)(2,1)}, u32[]{:S(2)}, u32[]{:S(2)}) collective-permute-start(bf16[384,128]{1,0:T(8,128)(2,1)} %get-tuple-element.194), channel_id=1, source_target_pairs={{0,2},{1,3},{2,0},{3,1},{4,6},{5,7},{6,4},{7,5},{8,10},{9,11},{10,... | collective-permute-start | bytes 294920 | tf_op jit(solution)/shard_map/ppermute | solution.py:750
  27.0 5.9 %collective-permute-start.13 = (bf16[384,128]{1,0:T(8,128)(2,1)}, bf16[384,128]{1,0:T(8,128)(2,1)}, u32[]{:S(2)}, u32[]{:S(2)}) collective-permute-start(bf16[384,128]{1,0:T(8,128)(2,1)} %get-tuple-element.195), channel_id=1, source_target_pairs={{0,4},{1,5},{2,6},{3,7},{4,0},{5,1},{6,2},{7,3},{8,12},{9,13},{10,... | collective-permute-start | bytes 294920 | tf_op jit(solution)/shard_map/ppermute | solution.py:750
  31.0 13.5 %collective-permute-start.14 = (bf16[384,128]{1,0:T(8,128)(2,1)}, bf16[384,128]{1,0:T(8,128)(2,1)}, u32[]{:S(2)}, u32[]{:S(2)}) collective-permute-start(bf16[384,128]{1,0:T(8,128)(2,1)} %get-tuple-element.196), channel_id=1, source_target_pairs={{0,6},{1,7},{2,4},{3,5},{4,2},{5,3},{6,0},{7,1},{8,14},{9,15},{10,... | collective-permute-start | bytes 294920 | tf_op jit(solution)/shard_map/ppermute | solution.py:750
  33.0 22.6 %collective-permute-start.7 = (bf16[384,1024]{1,0:T(8,128)(2,1)S(1)}, bf16[384,1024]{1,0:T(8,128)(2,1)}, u32[]{:S(2)}, u32[]{:S(2)}) collective-permute-start(bf16[384,1024]{1,0:T(8,128)(2,1)S(1)} %pad_maximum_fusion.refs_5_.refs_7_), channel_id=1, source_target_pairs={{0,1},{1,0},{2,3},{3,2},{4,5},{5,4},{6,7},{7,6},{8,9},{9,8},{10,11... | collective-permute-start | bytes 2359304 | tf_op jit(solution)/shard_map/ppermute | solution.py:767
  44.5 9.9 %collective-permute-start.15 = (bf16[384,128]{1,0:T(8,128)(2,1)}, bf16[384,128]{1,0:T(8,128)(2,1)}, u32[]{:S(2)}, u32[]{:S(2)}) collective-permute-start(bf16[384,128]{1,0:T(8,128)(2,1)} %get-tuple-element.180.refs_15_.refs_20_), channel_id=1, source_target_pairs={{0,1},{1,0},{2,3},{3,2},{4,5},{5,4},{6,7},{7,6},{8,9},{9,8},{10,11... | collective-permute-start | bytes 294920 | tf_op jit(solution)/shard_map/ppermute | solution.py:751
  44.6 10.0 %collective-permute-start.16 = (bf16[384,128]{1,0:T(8,128)(2,1)}, bf16[384,128]{1,0:T(8,128)(2,1)}, u32[]{:S(2)}, u32[]{:S(2)}) collective-permute-start(bf16[384,128]{1,0:T(8,128)(2,1)} %collective-permute-done.12.refs_16_.refs_21_), channel_id=1, source_target_pairs={{0,1},{1,0},{2,3},{3,2},{4,5},{5,4},{6,7},{7,6},{8,9},{9,8},{10,11... | collective-permute-start | bytes 294920 | tf_op jit(solution)/shard_map/ppermute | solution.py:751
  45.1 9.9 %collective-permute-start.17 = (bf16[384,128]{1,0:T(8,128)(2,1)}, bf16[384,128]{1,0:T(8,128)(2,1)}, u32[]{:S(2)}, u32[]{:S(2)}) collective-permute-start(bf16[384,128]{1,0:T(8,128)(2,1)} %collective-permute-done.13.refs_17_.refs_22_), channel_id=1, source_target_pairs={{0,1},{1,0},{2,3},{3,2},{4,5},{5,4},{6,7},{7,6},{8,9},{9,8},{10,11... | collective-permute-start | bytes 294920 | tf_op jit(solution)/shard_map/ppermute | solution.py:751
  52.1 3.1 %collective-permute-start.18 = (bf16[384,128]{1,0:T(8,128)(2,1)}, bf16[384,128]{1,0:T(8,128)(2,1)}, u32[]{:S(2)}, u32[]{:S(2)}) collective-permute-start(bf16[384,128]{1,0:T(8,128)(2,1)} %collective-permute-done.14.refs_18_.refs_23_), channel_id=1, source_target_pairs={{0,1},{1,0},{2,3},{3,2},{4,5},{5,4},{6,7},{7,6},{8,9},{9,8},{10,11... | collective-permute-start | bytes 294920 | tf_op jit(solution)/shard_map/ppermute | solution.py:751
  54.7 2.9 collective-permute-start.11
  55.0 3.4 %collective-permute-start.8 = (bf16[1152,256]{1,0:T(8,128)(2,1)S(1)}, bf16[1152,256]{1,0:T(8,128)(2,1)S(1)}, u32[]{:S(2)}, u32[]{:S(2)}) collective-permute-start(bf16[1152,256]{1,0:T(8,128)(2,1)S(1)} %pack.1.refs_6_.refs_8_), channel_id=1, source_target_pairs={{0,1},{1,0},{2,3},{3,2},{4,5},{5,4},{6,7},{7,6},{8,9},{9,8},{10,11... | collective-permute-start | bytes 1769480 | tf_op jit(solution)/shard_map/ppermute | solution.py:767
  55.2 4.2 %collective-permute-start.9 = (bf16[1152,256]{1,0:T(8,128)(2,1)S(1)}, bf16[1152,256]{1,0:T(8,128)(2,1)}, u32[]{:S(2)}, u32[]{:S(2)}) collective-permute-start(bf16[1152,256]{1,0:T(8,128)(2,1)S(1)} %collective-permute-done.4.refs_7_.refs_9_), channel_id=1, source_target_pairs={{0,1},{1,0},{2,3},{3,2},{4,5},{5,4},{6,7},{7,6},{8,9},{9,8},{10,11... | collective-permute-start | bytes 1769480 | tf_op jit(solution)/shard_map/ppermute | solution.py:767
  70.2 7.7 %collective-permute-start.21 = (bf16[128,1024]{1,0:T(8,128)(2,1)}, bf16[128,1024]{1,0:T(8,128)(2,1)S(1)}, u32[]{:S(2)}, u32[]{:S(2)}) collective-permute-start(bf16[128,1024]{1,0:T(8,128)(2,1)} %get-tuple-element.201.same), channel_id=1, source_target_pairs={{0,2},{1,3},{2,0},{3,1},{4,6},{5,7},{6,4},{7,5},{8,10},{9,11},{10,... | collective-permute-start | bytes 786440 | tf_op jit(solution)/shard_map/ppermute | solution.py:801
  70.2 7.7 %collective-permute-start.22 = (bf16[128,1024]{1,0:T(8,128)(2,1)}, bf16[128,1024]{1,0:T(8,128)(2,1)S(1)}, u32[]{:S(2)}, u32[]{:S(2)}) collective-permute-start(bf16[128,1024]{1,0:T(8,128)(2,1)} %get-tuple-element.201.same), channel_id=1, source_target_pairs={{0,6},{1,7},{2,4},{3,5},{4,2},{5,3},{6,0},{7,1},{8,14},{9,15},{10,... | collective-permute-start | bytes 786440 | tf_op jit(solution)/shard_map/ppermute | solution.py:801
  77.9 9.0 %collective-permute-start.23 = (bf16[128,1024]{1,0:T(8,128)(2,1)S(1)}, bf16[128,1024]{1,0:T(8,128)(2,1)S(1)}, u32[]{:S(2)}, u32[]{:S(2)}) collective-permute-start(bf16[128,1024]{1,0:T(8,128)(2,1)S(1)} %collective-permute-done.21.same), channel_id=1, source_target_pairs={{0,1},{1,0},{2,3},{3,2},{4,5},{5,4},{6,7},{7,6},{8,9},{9,8},{10,11... | collective-permute-start | bytes 786440 | tf_op jit(solution)/shard_map/ppermute | solution.py:819
  80.0 9.1 %collective-permute-start.25 = (bf16[128,1024]{1,0:T(8,128)(2,1)S(1)}, bf16[128,1024]{1,0:T(8,128)(2,1)S(1)}, u32[]{:S(2)}, u32[]{:S(2)}) collective-permute-start(bf16[128,1024]{1,0:T(8,128)(2,1)S(1)} %collective-permute-done.22.same), channel_id=1, source_target_pairs={{0,1},{1,0},{2,3},{3,2},{4,5},{5,4},{6,7},{7,6},{8,9},{9,8},{10,11... | collective-permute-start | bytes 786440 | tf_op jit(solution)/shard_map/ppermute | solution.py:819
  80.0 13.1 %collective-permute-start.26 = (bf16[128,1024]{1,0:T(8,128)(2,1)S(1)}, bf16[128,1024]{1,0:T(8,128)(2,1)S(1)}, u32[]{:S(2)}, u32[]{:S(2)}) collective-permute-start(bf16[128,1024]{1,0:T(8,128)(2,1)S(1)} %collective-permute-done.22.same), channel_id=1, source_target_pairs={{0,2},{1,3},{2,0},{3,1},{4,6},{5,7},{6,4},{7,5},{8,10},{9,11},{10,... | collective-permute-start | bytes 786440 | tf_op jit(solution)/shard_map/ppermute | solution.py:842
  91.2 6.8 %collective-permute-start.29 = (bf16[128,1536]{1,0:T(8,128)(2,1)S(1)}, bf16[128,1536]{1,0:T(8,128)(2,1)S(1)}, u32[]{:S(2)}, u32[]{:S(2)}) collective-permute-start(bf16[128,1536]{1,0:T(8,128)(2,1)S(1)} %get-tuple-element.221), channel_id=1, source_target_pairs={{0,1},{1,0},{2,3},{3,2},{4,5},{5,4},{6,7},{7,6},{8,9},{9,8},{10,11... | collective-permute-start | bytes 1179656 | tf_op jit(solution)/shard_map/ppermute | solution.py:837
  94.2 5.8 %collective-permute-start.24 = (bf16[128,1536]{1,0:T(8,128)(2,1)S(1)}, bf16[128,1536]{1,0:T(8,128)(2,1)S(1)}, u32[]{:S(2)}, u32[]{:S(2)}) collective-permute-start(bf16[128,1536]{1,0:T(8,128)(2,1)S(1)} %get-tuple-element.210), channel_id=1, source_target_pairs={{0,1},{1,0},{2,3},{3,2},{4,5},{5,4},{6,7},{7,6},{8,9},{9,8},{10,11... | collective-permute-start | bytes 1179656 | tf_op jit(solution)/shard_map/ppermute | solution.py:837
  98.1 7.8 %collective-permute-start.30 = (bf16[128,1024]{1,0:T(8,128)(2,1)S(1)}, bf16[128,1024]{1,0:T(8,128)(2,1)S(1)}, u32[]{:S(2)}, u32[]{:S(2)}) collective-permute-start(bf16[128,1024]{1,0:T(8,128)(2,1)S(1)} %add_convert_fusion.2), channel_id=1, source_target_pairs={{0,2},{1,3},{2,0},{3,1},{4,6},{5,7},{6,4},{7,5},{8,10},{9,11},{10,... | collective-permute-start | bytes 786440 | tf_op jit(solution)/shard_map/ppermute | solution.py:845
  99.6 9.7 %collective-permute-start.20 = (bf16[128,1536]{1,0:T(8,128)(2,1)S(1)}, bf16[128,1536]{1,0:T(8,128)(2,1)S(1)}, u32[]{:S(2)}, u32[]{:S(2)}) collective-permute-start(bf16[128,1536]{1,0:T(8,128)(2,1)S(1)} %get-tuple-element.204), channel_id=1, source_target_pairs={{0,1},{1,0},{2,3},{3,2},{4,5},{5,4},{6,7},{7,6},{8,9},{9,8},{10,11... | collective-permute-start | bytes 1179656 | tf_op jit(solution)/shard_map/ppermute | solution.py:837
  100.1 18.6 %collective-permute-start.31 = (bf16[128,1024]{1,0:T(8,128)(2,1)S(1)}, bf16[128,1024]{1,0:T(8,128)(2,1)S(1)}, u32[]{:S(2)}, u32[]{:S(2)}) collective-permute-start(bf16[128,1024]{1,0:T(8,128)(2,1)S(1)} %add_convert_fusion.4), channel_id=1, source_target_pairs={{0,2},{1,3},{2,0},{3,1},{4,6},{5,7},{6,4},{7,5},{8,10},{9,11},{10,... | collective-permute-start | bytes 786440 | tf_op jit(solution)/shard_map/ppermute | solution.py:843
  106.0 25.1 %collective-permute-start.32 = (bf16[128,1024]{1,0:T(8,128)(2,1)S(1)}, bf16[128,1024]{1,0:T(8,128)(2,1)S(1)}, u32[]{:S(2)}, u32[]{:S(2)}) collective-permute-start(bf16[128,1024]{1,0:T(8,128)(2,1)S(1)} %add_convert_fusion.1), channel_id=1, source_target_pairs={{0,4},{1,5},{2,6},{3,7},{4,0},{5,1},{6,2},{7,3},{8,12},{9,13},{10,... | collective-permute-start | bytes 786440 | tf_op jit(solution)/shard_map/ppermute | solution.py:846
  107.6 48.7 %collective-permute-start.38 = (bf16[3,128,1024]{2,1,0:T(8,128)(2,1)}, bf16[3,128,1024]{2,1,0:T(8,128)(2,1)}, u32[]{:S(2)}, u32[]{:S(2)}) collective-permute-start(bf16[3,128,1024]{2,1,0:T(8,128)(2,1)} %get-tuple-element.259.refs_1_), channel_id=1, source_target_pairs={{0,1},{1,0},{2,3},{3,2},{4,5},{5,4},{6,7},{7,6},{8,9},{9,8},{10,11... | collective-permute-start | bytes 2359304 | tf_op jit(solution)/shard_map/ppermute | solution.py:802
  119.4 30.4 %all-to-all-start = ((bf16[4,1040,256]{2,1,0:T(8,128)(2,1)}), bf16[4,1040,256]{2,1,0:T(8,128)(2,1)}, u32[]{:S(2)}, u32[]{:S(2)}) async-start(bf16[4,1040,256]{2,1,0:T(8,128)(2,1)} %mlp_grad.1), calls=%async_computation | async-start | bytes 4259840 | tf_op jit(solution)/shard_map/all_to_all | solution.py:705
  131.1 15.0 %collective-permute-start.33 = (bf16[128,1024]{1,0:T(8,128)(2,1)}, bf16[128,1024]{1,0:T(8,128)(2,1)}, u32[]{:S(2)}, u32[]{:S(2)}) collective-permute-start(bf16[128,1024]{1,0:T(8,128)(2,1)} %get-tuple-element.253), channel_id=1, source_target_pairs={{0,2},{1,3},{2,0},{3,1},{4,6},{5,7},{6,4},{7,5},{8,10},{9,11},{10,... | collective-permute-start | bytes 786440 | tf_op jit(solution)/shard_map/ppermute | solution.py:885
  131.6 14.5 %collective-permute-start.34 = (bf16[128,1024]{1,0:T(8,128)(2,1)}, bf16[128,1024]{1,0:T(8,128)(2,1)}, u32[]{:S(2)}, u32[]{:S(2)}) collective-permute-start(bf16[128,1024]{1,0:T(8,128)(2,1)} %get-tuple-element.254), channel_id=1, source_target_pairs={{0,4},{1,5},{2,6},{3,7},{4,0},{5,1},{6,2},{7,3},{8,12},{9,13},{10,... | collective-permute-start | bytes 786440 | tf_op jit(solution)/shard_map/ppermute | solution.py:885
  149.8 8.8 %collective-permute-start.39 = (bf16[3,128,1024]{2,1,0:T(8,128)(2,1)}, bf16[3,128,1024]{2,1,0:T(8,128)(2,1)S(1)}, u32[]{:S(2)}, u32[]{:S(2)}) collective-permute-start(bf16[3,128,1024]{2,1,0:T(8,128)(2,1)} %get-tuple-element.260.refs_3_), channel_id=1, source_target_pairs={{0,1},{1,0},{2,3},{3,2},{4,5},{5,4},{6,7},{7,6},{8,9},{9,8},{10,11... | collective-permute-start | bytes 2359304 | tf_op jit(solution)/shard_map/ppermute | solution.py:936
  154.1 13.8 %collective-permute-start.40 = (bf16[1024,256]{1,0:T(8,128)(2,1)}, bf16[1024,256]{1,0:T(8,128)(2,1)S(1)}, u32[]{:S(2)}, u32[]{:S(2)}) collective-permute-start(bf16[1024,256]{1,0:T(8,128)(2,1)} %sum_mlp.1.refs_1_), channel_id=1, source_target_pairs={{0,8},{8,0},{16,24},{24,16},{1,9},{9,1},{17,25},{25,17},{2,10},{10... | collective-permute-start | bytes 1572872 | tf_op jit(solution)/shard_map/ppermute | solution.py:924
  154.5 13.4 %collective-permute-start.41 = (bf16[1024,256]{1,0:T(8,128)(2,1)}, bf16[1024,256]{1,0:T(8,128)(2,1)S(1)}, u32[]{:S(2)}, u32[]{:S(2)}) collective-permute-start(bf16[1024,256]{1,0:T(8,128)(2,1)} %sum_mlp.1.refs_1_), channel_id=1, source_target_pairs={{0,16},{8,24},{16,0},{24,8},{1,17},{9,25},{17,1},{25,9},{2,18},{10... | collective-permute-start | bytes 1572872 | tf_op jit(solution)/shard_map/ppermute | solution.py:924
  156.2 8.7 %collective-permute-start.35 = (bf16[2,128,128]{2,1,0:T(8,128)(2,1)S(1)}, bf16[2,128,128]{2,1,0:T(8,128)(2,1)S(1)}, u32[]{:S(2)}, u32[]{:S(2)}) collective-permute-start(bf16[2,128,128]{2,1,0:T(8,128)(2,1)S(1)} %copy-done.53), channel_id=1, source_target_pairs={{0,2},{1,3},{2,0},{3,1},{4,6},{5,7},{6,4},{7,5},{8,10},{9,11},{10,... | collective-permute-start | bytes 196616 | tf_op jit(solution)/shard_map/ppermute | solution.py:927
  157.2 7.7 %collective-permute-start.36 = (bf16[2,128,128]{2,1,0:T(8,128)(2,1)S(1)}, bf16[2,128,128]{2,1,0:T(8,128)(2,1)S(1)}, u32[]{:S(2)}, u32[]{:S(2)}) collective-permute-start(bf16[2,128,128]{2,1,0:T(8,128)(2,1)S(1)} %copy-done.52), channel_id=1, source_target_pairs={{0,4},{1,5},{2,6},{3,7},{4,0},{5,1},{6,2},{7,3},{8,12},{9,13},{10,... | collective-permute-start | bytes 196616 | tf_op jit(solution)/shard_map/ppermute | solution.py:927
  158.6 6.7 %collective-permute-start.37 = (bf16[2,128,128]{2,1,0:T(8,128)(2,1)S(1)}, bf16[2,128,128]{2,1,0:T(8,128)(2,1)S(1)}, u32[]{:S(2)}, u32[]{:S(2)}) collective-permute-start(bf16[2,128,128]{2,1,0:T(8,128)(2,1)S(1)} %copy-done.50), channel_id=1, source_target_pairs={{0,6},{1,7},{2,4},{3,5},{4,2},{5,3},{6,0},{7,1},{8,14},{9,15},{10,... | collective-permute-start | bytes 196616 | tf_op jit(solution)/shard_map/ppermute | solution.py:927
  167.9 8.5 %collective-permute-start.42 = (bf16[2,128,128]{2,1,0:T(8,128)(2,1)S(1)}, bf16[2,128,128]{2,1,0:T(8,128)(2,1)S(1)}, u32[]{:S(2)}, u32[]{:S(2)}) collective-permute-start(bf16[2,128,128]{2,1,0:T(8,128)(2,1)S(1)} %copy-done.47), channel_id=1, source_target_pairs={{0,1},{1,0},{2,3},{3,2},{4,5},{5,4},{6,7},{7,6},{8,9},{9,8},{10,11... | collective-permute-start | bytes 196616 | tf_op jit(solution)/shard_map/ppermute | solution.py:945
  169.0 9.4 %collective-permute-start.43 = (bf16[2,128,128]{2,1,0:T(8,128)(2,1)S(1)}, bf16[2,128,128]{2,1,0:T(8,128)(2,1)S(1)}, u32[]{:S(2)}, u32[]{:S(2)}) collective-permute-start(bf16[2,128,128]{2,1,0:T(8,128)(2,1)S(1)} %collective-permute-done.35.refs_5_), channel_id=1, source_target_pairs={{0,1},{1,0},{2,3},{3,2},{4,5},{5,4},{6,7},{7,6},{8,9},{9,8},{10,11... | collective-permute-start | bytes 196616 | tf_op jit(solution)/shard_map/ppermute | solution.py:945
  169.1 9.6 %collective-permute-start.44 = (bf16[2,128,128]{2,1,0:T(8,128)(2,1)S(1)}, bf16[2,128,128]{2,1,0:T(8,128)(2,1)S(1)}, u32[]{:S(2)}, u32[]{:S(2)}) collective-permute-start(bf16[2,128,128]{2,1,0:T(8,128)(2,1)S(1)} %collective-permute-done.36.refs_6_), channel_id=1, source_target_pairs={{0,1},{1,0},{2,3},{3,2},{4,5},{5,4},{6,7},{7,6},{8,9},{9,8},{10,11... | collective-permute-start | bytes 196616 | tf_op jit(solution)/shard_map/ppermute | solution.py:945
  169.6 10.4 %collective-permute-start.45 = (bf16[2,128,128]{2,1,0:T(8,128)(2,1)S(1)}, bf16[2,128,128]{2,1,0:T(8,128)(2,1)S(1)}, u32[]{:S(2)}, u32[]{:S(2)}) collective-permute-start(bf16[2,128,128]{2,1,0:T(8,128)(2,1)S(1)} %collective-permute-done.37.refs_7_), channel_id=1, source_target_pairs={{0,1},{1,0},{2,3},{3,2},{4,5},{5,4},{6,7},{7,6},{8,9},{9,8},{10,11... | collective-permute-start | bytes 196616 | tf_op jit(solution)/shard_map/ppermute | solution.py:945
  170.3 24.9 %collective-permute-start.52 = (bf16[2,64,128]{2,1,0:T(8,128)(2,1)}, bf16[2,64,128]{2,1,0:T(8,128)(2,1)}, u32[]{:S(2)}, u32[]{:S(2)}) collective-permute-start(bf16[2,64,128]{2,1,0:T(8,128)(2,1)} %get-tuple-element.357), channel_id=1, source_target_pairs={{0,2},{1,3},{2,0},{3,1},{4,6},{5,7},{6,4},{7,5},{8,10},{9,11},{10,... | collective-permute-start | bytes 98312 | tf_op jit(solution)/shard_map/ppermute | solution.py:976
  170.7 53.0 %all-to-all-start.1 = ((bf16[4,1536,256]{2,1,0:T(8,128)(2,1)}), bf16[4,1536,256]{2,1,0:T(8,128)(2,1)}, u32[]{:S(2)}, u32[]{:S(2)}) async-start(bf16[4,1536,256]{2,1,0:T(8,128)(2,1)} %row_grad.1), calls=%async_computation.1 | async-start | bytes 6291456 | tf_op jit(solution)/shard_map/all_to_all | solution.py:705
  176.5 19.3 %collective-permute-start.53 = (bf16[2,64,128]{2,1,0:T(8,128)(2,1)}, bf16[2,64,128]{2,1,0:T(8,128)(2,1)}, u32[]{:S(2)}, u32[]{:S(2)}) collective-permute-start(bf16[2,64,128]{2,1,0:T(8,128)(2,1)} %get-tuple-element.359), channel_id=1, source_target_pairs={{0,4},{1,5},{2,6},{3,7},{4,0},{5,1},{6,2},{7,3},{8,12},{9,13},{10,... | collective-permute-start | bytes 98312 | tf_op jit(solution)/shard_map/ppermute | solution.py:976
  178.4 17.4 %collective-permute-start.54 = (bf16[2,64,128]{2,1,0:T(8,128)(2,1)}, bf16[2,64,128]{2,1,0:T(8,128)(2,1)}, u32[]{:S(2)}, u32[]{:S(2)}) collective-permute-start(bf16[2,64,128]{2,1,0:T(8,128)(2,1)} %get-tuple-element.358), channel_id=1, source_target_pairs={{0,6},{1,7},{2,4},{3,5},{4,2},{5,3},{6,0},{7,1},{8,14},{9,15},{10,... | collective-permute-start | bytes 98312 | tf_op jit(solution)/shard_map/ppermute | solution.py:976
  178.7 15.4 %collective-permute-start.46 = (bf16[128,1024]{1,0:T(8,128)(2,1)}, bf16[128,1024]{1,0:T(8,128)(2,1)}, u32[]{:S(2)}, u32[]{:S(2)}) collective-permute-start(bf16[128,1024]{1,0:T(8,128)(2,1)} %get-tuple-element.279), channel_id=1, source_target_pairs={{0,6},{1,7},{2,4},{3,5},{4,2},{5,3},{6,0},{7,1},{8,14},{9,15},{10,... | collective-permute-start | bytes 786440 | tf_op jit(solution)/shard_map/ppermute | solution.py:947
  194.1 4.3 %collective-permute-start.47 = (bf16[128,1024]{1,0:T(8,128)(2,1)}, bf16[128,1024]{1,0:T(8,128)(2,1)S(1)}, u32[]{:S(2)}, u32[]{:S(2)}) collective-permute-start(bf16[128,1024]{1,0:T(8,128)(2,1)} %get-tuple-element.280.refs_11_), channel_id=1, source_target_pairs={{0,1},{1,0},{2,3},{3,2},{4,5},{5,4},{6,7},{7,6},{8,9},{9,8},{10,11... | collective-permute-start | bytes 786440 | tf_op jit(solution)/shard_map/ppermute | solution.py:973
  195.2 3.3 %collective-permute-start.48 = (bf16[128,1024]{1,0:T(8,128)(2,1)}, bf16[128,1024]{1,0:T(8,128)(2,1)S(1)}, u32[]{:S(2)}, u32[]{:S(2)}) collective-permute-start(bf16[128,1024]{1,0:T(8,128)(2,1)} %get-tuple-element.281.refs_12_), channel_id=1, source_target_pairs={{0,1},{1,0},{2,3},{3,2},{4,5},{5,4},{6,7},{7,6},{8,9},{9,8},{10,11... | collective-permute-start | bytes 786440 | tf_op jit(solution)/shard_map/ppermute | solution.py:973
  195.2 3.3 %collective-permute-start.49 = (bf16[128,1024]{1,0:T(8,128)(2,1)}, bf16[128,1024]{1,0:T(8,128)(2,1)S(1)}, u32[]{:S(2)}, u32[]{:S(2)}) collective-permute-start(bf16[128,1024]{1,0:T(8,128)(2,1)} %get-tuple-element.282.refs_13_), channel_id=1, source_target_pairs={{0,1},{1,0},{2,3},{3,2},{4,5},{5,4},{6,7},{7,6},{8,9},{9,8},{10,11... | collective-permute-start | bytes 786440 | tf_op jit(solution)/shard_map/ppermute | solution.py:973
  195.8 27.1 %collective-permute-start.55 = (bf16[1024,256]{1,0:T(8,128)(2,1)S(1)}, bf16[1024,256]{1,0:T(8,128)(2,1)S(1)}, u32[]{:S(2)}, u32[]{:S(2)}) collective-permute-start(bf16[1024,256]{1,0:T(8,128)(2,1)S(1)} %copy-done.12), channel_id=1, source_target_pairs={{0,24},{8,16},{16,8},{24,0},{1,25},{9,17},{17,9},{25,1},{2,26},{10... | collective-permute-start | bytes 1572872 | tf_op jit(solution)/shard_map/ppermute | solution.py:944
  203.5 20.1 %collective-permute-start.56 = (bf16[128,1024]{1,0:T(8,128)(2,1)}, bf16[128,1024]{1,0:T(8,128)(2,1)S(1)}, u32[]{:S(2)}, u32[]{:S(2)}) collective-permute-start(bf16[128,1024]{1,0:T(8,128)(2,1)} %get-tuple-element.304), channel_id=1, source_target_pairs={{0,2},{1,3},{2,0},{3,1},{4,6},{5,7},{6,4},{7,5},{8,10},{9,11},{10,... | collective-permute-start | bytes 786440 | tf_op jit(solution)/shard_map/ppermute | solution.py:980
  204.8 18.8 %collective-permute-start.57 = (bf16[128,1024]{1,0:T(8,128)(2,1)}, bf16[128,1024]{1,0:T(8,128)(2,1)}, u32[]{:S(2)}, u32[]{:S(2)}) collective-permute-start(bf16[128,1024]{1,0:T(8,128)(2,1)} %get-tuple-element.305), channel_id=1, source_target_pairs={{0,4},{1,5},{2,6},{3,7},{4,0},{5,1},{6,2},{7,3},{8,12},{9,13},{10,... | collective-permute-start | bytes 786440 | tf_op jit(solution)/shard_map/ppermute | solution.py:980
  223.7 26.8 %all-to-all-start.2 = ((bf16[4,704,256]{2,1,0:T(8,128)(2,1)}), bf16[4,704,256]{2,1,0:T(8,128)(2,1)S(1)}, u32[]{:S(2)}, u32[]{:S(2)}) async-start(bf16[4,704,256]{2,1,0:T(8,128)(2,1)} %self_grad.1), calls=%async_computation.2 | async-start | bytes 2883584 | tf_op jit(solution)/shard_map/all_to_all | solution.py:705
  231.4 6.7 %collective-permute-start.58 = (bf16[384,256]{1,0:T(8,128)(2,1)S(1)}, bf16[384,256]{1,0:T(8,128)(2,1)S(1)}, u32[]{:S(2)}, u32[]{:S(2)}) collective-permute-start(bf16[384,256]{1,0:T(8,128)(2,1)S(1)} %get-tuple-element.344), channel_id=1, source_target_pairs={{0,2},{1,3},{2,0},{3,1},{4,6},{5,7},{6,4},{7,5},{8,10},{9,11},{10,... | collective-permute-start | bytes 589832 | tf_op jit(solution)/shard_map/ppermute | solution.py:1008
  232.6 8.3 %collective-permute-start.59 = (bf16[384,256]{1,0:T(8,128)(2,1)S(1)}, bf16[384,256]{1,0:T(8,128)(2,1)S(1)}, u32[]{:S(2)}, u32[]{:S(2)}) collective-permute-start(bf16[384,256]{1,0:T(8,128)(2,1)S(1)} %get-tuple-element.343), channel_id=1, source_target_pairs={{0,4},{1,5},{2,6},{3,7},{4,0},{5,1},{6,2},{7,3},{8,12},{9,13},{10,... | collective-permute-start | bytes 589832 | tf_op jit(solution)/shard_map/ppermute | solution.py:1008
  233.6 16.9 %collective-permute-start.60 = (bf16[384,256]{1,0:T(8,128)(2,1)S(1)}, bf16[384,256]{1,0:T(8,128)(2,1)S(1)}, u32[]{:S(2)}, u32[]{:S(2)}) collective-permute-start(bf16[384,256]{1,0:T(8,128)(2,1)S(1)} %get-tuple-element.342), channel_id=1, source_target_pairs={{0,6},{1,7},{2,4},{3,5},{4,2},{5,3},{6,0},{7,1},{8,14},{9,15},{10,... | collective-permute-start | bytes 589832 | tf_op jit(solution)/shard_map/ppermute | solution.py:1008
  251.6 24.3 %collective-permute-start.65 = (bf16[128,1024]{1,0:T(8,128)(2,1)}, bf16[128,1024]{1,0:T(8,128)(2,1)S(1)}, u32[]{:S(2)}, u32[]{:S(2)}) collective-permute-start(bf16[128,1024]{1,0:T(8,128)(2,1)} %get-tuple-element.322), channel_id=1, source_target_pairs={{0,6},{1,7},{2,4},{3,5},{4,2},{5,3},{6,0},{7,1},{8,14},{9,15},{10,... | collective-permute-start | bytes 786440 | tf_op jit(solution)/shard_map/ppermute | solution.py:1010
  253.3 12.2 %collective-permute-start.61 = (bf16[80,512]{1,0:T(8,128)(2,1)}, bf16[80,512]{1,0:T(8,128)(2,1)}, u32[]{:S(2)}, u32[]{:S(2)}) collective-permute-start(bf16[80,512]{1,0:T(8,128)(2,1)} %constant_dynamic-slice_fusion), channel_id=1, source_target_pairs={{0,1},{1,0},{2,3},{3,2},{4,5},{5,4},{6,7},{7,6},{8,9},{9,8},{10,11... | collective-permute-start | bytes 245768 | tf_op jit(solution)/shard_map/ppermute | solution.py:1034
  261.5 28.7 %all-to-all-start.3 = ((bf16[4,1024,256]{2,1,0:T(8,128)(2,1)}), bf16[4,1024,256]{2,1,0:T(8,128)(2,1)S(1)}, u32[]{:S(2)}, u32[]{:S(2)}) async-start(bf16[4,1024,256]{2,1,0:T(8,128)(2,1)} %broadcast_in_dim.23), calls=%async_computation.3 | async-start | bytes 4194304 | tf_op jit(solution)/shard_map/all_to_all | solution.py:690
  266.4 14.5 %collective-permute-start.62 = (bf16[80,512]{1,0:T(8,128)(2,1)S(1)}, bf16[80,512]{1,0:T(8,128)(2,1)S(1)}, u32[]{:S(2)}, u32[]{:S(2)}) collective-permute-start(bf16[80,512]{1,0:T(8,128)(2,1)S(1)} %add_convert_fusion.8), channel_id=1, source_target_pairs={{0,2},{1,3},{2,0},{3,1},{4,6},{5,7},{6,4},{7,5},{8,10},{9,11},{10,... | collective-permute-start | bytes 245768 | tf_op jit(solution)/shard_map/ppermute | solution.py:1035
  266.5 14.4 %collective-permute-start.63 = (bf16[80,512]{1,0:T(8,128)(2,1)S(1)}, bf16[80,512]{1,0:T(8,128)(2,1)S(1)}, u32[]{:S(2)}, u32[]{:S(2)}) collective-permute-start(bf16[80,512]{1,0:T(8,128)(2,1)S(1)} %add_convert_fusion.8), channel_id=1, source_target_pairs={{0,4},{1,5},{2,6},{3,7},{4,0},{5,1},{6,2},{7,3},{8,12},{9,13},{10,... | collective-permute-start | bytes 245768 | tf_op jit(solution)/shard_map/ppermute | solution.py:1035
  268.4 12.5 %collective-permute-start.64 = (bf16[80,512]{1,0:T(8,128)(2,1)S(1)}, bf16[80,512]{1,0:T(8,128)(2,1)S(1)}, u32[]{:S(2)}, u32[]{:S(2)}) collective-permute-start(bf16[80,512]{1,0:T(8,128)(2,1)S(1)} %add_convert_fusion.8), channel_id=1, source_target_pairs={{0,6},{1,7},{2,4},{3,5},{4,2},{5,3},{6,0},{7,1},{8,14},{9,15},{10,... | collective-permute-start | bytes 245768 | tf_op jit(solution)/shard_map/ppermute | solution.py:1035
  (65 other events, 539.1 us)

commit v2 on v1

--- a/solution.py
+++ b/solution.py
@@ -842,8 +842,7 @@
                 n3s[2] = to_z[1](n3s[3])
     backs = sent[:1] + [to_z[k](sent[k]) for k in range(1, 2 if relay else chips)]
     if relay:
-        sent[2] = total(sent[2], to_z[1](sent[3])).astype(BF16)
-        backs.append(to_z[2](sent[2]))
+        relayed = to_z[1](sent[3])
     (mlp_grad,) = call(
         functools.partial(mlp_grad_kernel, chips),
         [((dps, 2 * hid + PAD, cut), BF16)],
@@ -857,10 +856,14 @@
             pltpu.VMEM((rows, hid), BF16),
             pltpu.VMEM((rows, dim), BF16),
         ],
-        after=sent,
+        after=[x for k, x in enumerate(sent) if k != 2],
+        cost=10**12,
         stage=True,
         name="mlp_grad",
     )
+    if relay:
+        mlp_grad, relayed = lax.optimization_barrier((mlp_grad, relayed))
+        backs.append(to_z[2](total(sent[2], relayed).astype(BF16)))
     mlp_grad, backs[1] = lax.optimization_barrier((mlp_grad, backs[1]))
     mlp_swap = swap_dp(mlp_grad)
     mlp_part = call(
@@ -1006,7 +1009,10 @@
     self_swap = swap_dp(self_part)
     row_piece = sum_dp(row_swap).reshape(chips, 3 * width, cut)
     row_parts = [row_piece[0]] + [to_z[k](row_piece[k]) for k in far]
-    row_parts, self_swap, sent = lax.optimization_barrier((row_parts, self_swap, sent))
+    block_output = (second + total(*mlp_parts) + output_bias.astype(F32)).astype(BF16)
+    row_parts, self_swap, sent, block_output = lax.optimization_barrier(
+        (row_parts, self_swap, sent, block_output)
+    )
     parts += [to_z[k](sent[k]) for k in far[2:]]
     row_piece = total(*row_parts).astype(BF16)
     self_sum = sum_dp(self_swap)
@@ -1044,7 +1050,6 @@
             **kept,
         )
 
-    block_output = (second + total(*mlp_parts) + output_bias.astype(F32)).astype(BF16)
     grad_output_weight, grad_hidden_weight = place(
         mlp_all, ((hid, None, False), (hid, None, True)), ((hid, dim), (dim, hid)), "place_mlp"
     )

time: 295 us -> 289 us (0.980)
  starting transfers between devices: 94.1 us -> 88.9 us
  local copies, waits for them, and re-layouts: 17.7 us -> 14.6 us
    ppermute x1, waiting for transfers between devices: 0.01 us -> 8.36 us  [body(): parts += [to_z[k](sent[k]) for k in far[2:]]]
    ppermute x2, waiting for transfers between devices: 5.73 us -> 0.01 us  [the longest x1 0.01 us: body(): relayed = to_z[1](sent[3])]
    ppermute x1, starting transfers between devices: 5.63 us -> 2.47 us  [body(): state_half = total(half_of(core), to_core(half_of(1 - core))).astype(BF16)]
    unnamed x118 -> x110, local copies, waits for them, and re-layouts: 9.18 us -> 6.71 us
  transfers between devices with their start and end apart: 71 -> 71, of which waited for: 22 -> 22; matrix products, arithmetic and copies ran while one was open for 8% -> 8% of each run, Pallas kernels for 33% -> 34%
where the time goes in v2:
time: 289 us; the launch traced here: 287 us
  Pallas kernels  112 us (39%)
  starting transfers between devices  88.9 us (31%)
  waiting for transfers between devices  53.6 us (19%)
  local copies, waits for them, and re-layouts  14.6 us (5%)
  other arithmetic  14.5 us (5%)
  between operations  3.64 us (1%)
    pallas_call x19, Pallas kernels, call(): pl.pallas_call(kernel, out_shape=out_shape, in_specs=[pl.BlockSpec(memory...  112 us
    ppermute x3, waiting for transfers between devices, body(): row_parts = [row_piece[0]] + [to_z[k](row_piece[k]) for k in far]  16.1 us
    all_to_all x3, starting transfers between devices, swap_dp(): return lax.all_to_all(pieces, 'dp', 0, 0)  16 us
    ppermute x4, starting transfers between devices, body(): att2 = [to_core(x) for x in att]  9.27 us
    ppermute x1, waiting for transfers between devices, body(): parts += [to_z[k](sent[k]) for k in far[2:]]  8.36 us
    ppermute x1, waiting for transfers between devices, body(): mlp_all += [to_dp[q](mlp_all[0]) for q in range(3, dps)]  7.76 us
    ppermute x1, starting transfers between devices, body(): n3s[2] = to_z[1](n3s[3])  6.97 us
    unnamed x110, local copies, waits for them, and re-layouts  6.71 us
  transfers between devices with their start and end apart: 71, of which 22 were waited for; matrix products, arithmetic and copies ran while one was open for 8% of the time, Pallas kernels for 34%

profile of v2, /device:TPU:11, one launch (start us, length us, event | category | flops | bytes accessed | tf_op | source)
XLA Modules:
  0.0 287.2 jit_solution(12458294988415866556)
XLA Ops:
  3.9 2.3 collective-permute-start.1
  8.3 13.3 %self_fwd.1 = (bf16[1024,1024]{1,0:T(8,128)(2,1)}, bf16[3,1024,128]{2,1,0:T(8,128)(2,1)}, bf16[2,1024,1024]{2,1,0:T(8,128)(2,1)}, bf16[384,128]{1,0:T(8,128)(2,1...) custom-call(s32[4]{0:T(128)} %pad_add_fusion.refs_0_.idx, ...), custom_call_target="tpu_custom_call" | custom-call | flops 1 | bytes 1 | tf_op jit(solution)/shard_map/self_fwd/pallas_call | solution.py:111
  21.6 2.1 collective-permute-done.2.refs_2_
  24.7 1.2 collective-permute-start.5
  25.9 1.2 collective-permute-start.6
  27.1 2.5 collective-permute-start.13
  29.5 1.6 collective-permute-done.12.refs_16_.refs_21_
  31.1 1.3 collective-permute-start.14
  33.0 4.2 %collective-permute-start.7 = (bf16[384,1024]{1,0:T(8,128)(2,1)S(1)}, bf16[384,1024]{1,0:T(8,128)(2,1)}, u32[]{:S(2)}, u32[]{:S(2)}) collective-permute-start(bf16[384,1024]{1,0:T(8,128)(2,1)S(1)} %pad_maximum_fusion.refs_5_.refs_7_), channel_id=1, source_target_pairs={{0,1},{1,0},{2,3},{3,2},{4,5},{5,4},{6,7},{7,6},{8,9},{9,8},{10,11... | collective-permute-start | bytes 2359304 | tf_op jit(solution)/shard_map/ppermute | solution.py:767
  37.2 6.0 %grad_active.1 = (f32[256,512]{1,0:T(8,128)}, f32[256,512]{1,0:T(8,128)}, f32[256,512]{1,0:T(8,128)}, f32[256,512]{1,0:T(8,128)}) custom-call(s32[4]{0:T(128)} %pad_add_fusion.refs_0_.idx, bf16[1024,1024]{1,0:T(8,128)(2,1)} %refs_1_.13, bf16[512,1024]{1,0:T(8,128)(2,1)} %refs_1_.12), custom_call_target="tpu_custom_call" | custom-call | flops 1 | bytes 1 | tf_op jit(solution)/shard_map/grad_active/pallas_call | solution.py:111
  45.1 7.0 %collective-permute-start.17 = (bf16[384,128]{1,0:T(8,128)(2,1)}, bf16[384,128]{1,0:T(8,128)(2,1)}, u32[]{:S(2)}, u32[]{:S(2)}) collective-permute-start(bf16[384,128]{1,0:T(8,128)(2,1)} %collective-permute-done.13.refs_17_.refs_22_), channel_id=1, source_target_pairs={{0,1},{1,0},{2,3},{3,2},{4,5},{5,4},{6,7},{7,6},{8,9},{9,8},{10,11... | collective-permute-start | bytes 294920 | tf_op jit(solution)/shard_map/ppermute | solution.py:751
  52.1 1.7 collective-permute-start.18
  55.7 1.2 collective-permute-done.10.refs_13_.refs_15_
  59.5 10.6 %cross_fwd.1 = (f32[128,1024]{1,0:T(8,128)}, bf16[3,128,1024]{2,1,0:T(8,128)(2,1)}, bf16[128,1024]{1,0:T(8,128)(2,1)}, bf16[8,128,128]{2,1,0:T(8,128)(2,1)}, f32...) custom-call(s32[4]{0:T(128)} %pad_add_fusion.refs_0_.idx, bf16[1024,1024]{1,0:T(8,128)(2,1)} %refs_1_.15, ...), custom_call_target="tpu_custom_call" | custom-call | flops 1 | bytes 1 | tf_op jit(solution)/shard_map/cross_fwd/pallas_call | solution.py:111
  70.3 1.4 collective-permute-start.22
  72.9 2.1 hidden.4
  75.0 3.0 %collective-permute-done.21.same = bf16[128,1024]{1,0:T(8,128)(2,1)S(1)} collective-permute-done((bf16[128,1024]{1,0:T(8,128)(2,1)}, bf16[128,1024]{1,0:T(8,128)(2,1)S(1)}, u32[]{:S(2)}, u32[]{:S(2)}) %collective-permute-start.21) | collective-permute-done | bytes 262176 | tf_op jit(solution)/shard_map/ppermute | solution.py:801
  78.1 2.0 collective-permute-start.23
  80.6 7.0 %collective-permute-start.27 = (bf16[128,1024]{1,0:T(8,128)(2,1)S(1)}, bf16[128,1024]{1,0:T(8,128)(2,1)S(1)}, u32[]{:S(2)}, u32[]{:S(2)}) collective-permute-start(bf16[128,1024]{1,0:T(8,128)(2,1)S(1)} %collective-permute-done.22.same), channel_id=1, source_target_pairs={{0,2},{1,3},{2,0},{3,1},{4,6},{5,7},{6,4},{7,5},{8,10},{9,11},{10,... | collective-permute-start | bytes 786440 | tf_op jit(solution)/shard_map/ppermute | solution.py:842
  87.6 2.1 hidden.5
  89.7 2.2 hidden.6
  92.3 2.0 collective-permute-done.27.same
  96.0 2.9 hidden.7
  100.2 1.5 collective-permute-start.29
  102.5 8.4 %mlp_grad.1 = bf16[4,1040,256]{2,1,0:T(8,128)(2,1)} custom-call(s32[4]{0:T(128)} %pad_add_fusion.refs_0_.idx, bf16[1024,1024]{1,0:T(8,128)(2,1)} %refs_1_.13, bf16[256,512]{1,0:T(8,128)(2,1)} %get-tuple-element.208.refs_2_.refs_3_, bf16[256,512]{1,0:T(8,128)(2,1)} %get-tuple-element.214.refs_3_.refs_4_, bf16[256,512]{1,0:T(8,128)(2,1)} %get-tuple-element.224.refs_4_.refs_5_, ...), custom_call_target="tpu_custom_call" | custom-call | flops 999999995904 | bytes 1 | tf_op jit(solution)/shard_map/mlp_grad/pallas_call | solution.py:111
  111.0 1.2 add_convert_fusion.1
  112.1 1.5 collective-permute-start.32
  114.6 5.3 %all-to-all-start = ((bf16[4,1040,256]{2,1,0:T(8,128)(2,1)}), bf16[4,1040,256]{2,1,0:T(8,128)(2,1)}, u32[]{:S(2)}, u32[]{:S(2)}) async-start(bf16[4,1040,256]{2,1,0:T(8,128)(2,1)} %mlp_grad.1), calls=%async_computation | async-start | bytes 4259840 | tf_op jit(solution)/shard_map/all_to_all | solution.py:705
  119.9 6.4 %mlp_out.1 = (bf16[128,1024]{1,0:T(8,128)(2,1)}, bf16[128,1024]{1,0:T(8,128)(2,1)}, bf16[128,1024]{1,0:T(8,128)(2,1)}, bf16[128,1024]{1,0:T(8,128)(2,1)}) custom-call(s32[4]{0:T(128)} %pad_add_fusion.refs_0_.idx, bf16[512,1024]{1,0:T(8,128)(2,1)} %refs_1_.12, bf16[512,1024]{1,0:T(8,128)(2,1)} %copy-done.16, ...), custom_call_target="tpu_custom_call" | custom-call | flops 1 | bytes 1 | tf_op jit(solution)/shard_map/mlp_out/pallas_call | solution.py:111
  126.4 1.8 collective-permute-start.33
  128.8 12.5 %cross_bwd.1 = (bf16[3,128,1024]{2,1,0:T(8,128)(2,1)}, f32[128,1024]{1,0:T(8,128)}, f32[8,1024]{1,0:T(8,128)}, bf16[4,2,64,128]{3,2,1,0:T(8,128)(2,1)}, bf16[4,2...) custom-call(s32[4]{0:T(128)} %pad_add_fusion.refs_0_.idx, ...), custom_call_target="tpu_custom_call" | custom-call | flops 999999995904 | bytes 1 | tf_op jit(solution)/shard_map/cross_bwd/pallas_call | solution.py:111
  141.4 3.4 %all-to-all-done.refs_1_ = bf16[4,1040,256]{2,1,0:T(8,128)(2,1)} async-done(((bf16[4,1040,256]{2,1,0:T(8,128)(2,1)}), bf16[4,1040,256]{2,1,0:T(8,128)(2,1)}, u32[]{:S(2)}, u32[]{:S(2)}) %all-to-all-start) | async-done | bytes 2129952 | tf_op jit(solution)/shard_map/all_to_all | solution.py:705
  145.9 3.4 %sum_mlp.1.refs_1_ = bf16[1024,256]{1,0:T(8,128)(2,1)} custom-call(s32[4]{0:T(128)} %pad_add_fusion.refs_0_.idx, bf16[4,1040,256]{2,1,0:T(8,128)(2,1)} %all-to-all-done.refs_1_), custom_call_target="tpu_custom_call" | custom-call | flops 1 | bytes 1 | tf_op jit(solution)/shard_map/sum_mlp/pallas_call | solution.py:111
  149.7 1.2 collective-permute-start.41
  152.4 1.4 collective-permute-start.36
  154.7 5.4 %row_grad.1 = bf16[4,1536,256]{2,1,0:T(8,128)(2,1)} custom-call(s32[4]{0:T(128)} %pad_add_fusion.refs_0_.idx, bf16[3,128,1024]{2,1,0:T(8,128)(2,1)} %get-tuple-element.264.refs_1_, bf16[3,128,1024]{2,1,0:T(8,128)(2,1)} %collective-permute-done.38.refs_2_, bf16[3,128,1024]{2,1,0:T(8,128)(2,1)} %get-tuple-element.265.refs_3_, bf16[3,128,1024]{2,1,0:T(8,128)(2,1)} %copy-done.17), custom_call_target="tpu_custom_call" | custom-call | flops 1 | bytes 1 | tf_op jit(solution)/shard_map/row_grad/pallas_call | solution.py:111
  160.6 2.5 collective-permute-done.40.refs_2_
  166.2 5.8 %all-to-all-start.1 = ((bf16[4,1536,256]{2,1,0:T(8,128)(2,1)}), bf16[4,1536,256]{2,1,0:T(8,128)(2,1)}, u32[]{:S(2)}, u32[]{:S(2)}) async-start(bf16[4,1536,256]{2,1,0:T(8,128)(2,1)} %row_grad.1), calls=%async_computation.1 | async-start | bytes 6291456 | tf_op jit(solution)/shard_map/all_to_all | solution.py:705
  172.1 1.6 collective-permute-start.53
  174.0 1.2 collective-permute-start.46
  175.8 12.1 %self_bwd.1 = (bf16[1024,384]{1,0:T(8,128)(2,1)}, bf16[128,1024]{1,0:T(8,128)(2,1)}, bf16[128,1024]{1,0:T(8,128)(2,1)}, bf16[128,1024]{1,0:T(8,128)(2,1)}, bf16[...) custom-call(s32[4]{0:T(128)} %pad_add_fusion.refs_0_.idx, ...), custom_call_target="tpu_custom_call" | custom-call | flops 999999995904 | bytes 1 | tf_op jit(solution)/shard_map/self_bwd/pallas_call | solution.py:111
  187.9 1.5 collective-permute-done.46
  191.1 1.2 collective-permute-start.55
  192.3 1.4 fusion.3.refs_5_
  195.3 3.5 %self_add.1 = (bf16[128,1024]{1,0:T(8,128)(2,1)}, bf16[128,1024]{1,0:T(8,128)(2,1)}, bf16[128,1024]{1,0:T(8,128)(2,1)}, bf16[128,1024]{1,0:T(8,128)(2,1)}) custom-call(s32[4]{0:T(128)} %pad_add_fusion.refs_0_.idx, bf16[128,1024]{1,0:T(8,128)(2,1)} %get-tuple-element.292.refs_1_.refs_7_, bf16[128,1024]{1,0:T(8,128)(2,1)} %get-tuple-element.293.refs_2_.refs_8_, ...), custom_call_target="tpu_custom_call" | custom-call | flops 1 | bytes 1 | tf_op jit(solution)/shard_map/self_add/pallas_call | solution.py:111
  198.7 1.2 collective-permute-start.56
  200.8 1.6 dynamic-slice_bitcast_fusion.refs_4_
  202.4 8.3 %self_grad.1 = bf16[4,704,256]{2,1,0:T(8,128)(2,1)} custom-call(s32[4]{0:T(128)} %pad_add_fusion.refs_0_.idx, bf16[1024,1024]{1,0:T(8,128)(2,1)} %refs_1_.15, bf16[1024,1024]{1,0:T(8,128)(2,1)} %get-tuple-element.302.refs_2_, bf16[1024,384]{1,0:T(8,128)(2,1)} %get-tuple-element.303.refs_3_, bf16[64,1024]{1,0:T(8,128)(2,1)} %dynamic-slice_bitcast_fusion.refs_4_, ...), custom_call_target="tpu_custom_call" | custom-call | flops 1 | bytes 1 | tf_op jit(solution)/shard_map/self_grad/pallas_call | solution.py:111
  210.7 7.8 %collective-permute-done.55.refs_4_ = bf16[1024,256]{1,0:T(8,128)(2,1)S(1)} collective-permute-done((bf16[1024,256]{1,0:T(8,128)(2,1)S(1)}, bf16[1024,256]{1,0:T(8,128)(2,1)S(1)}, u32[]{:S(2)}, u32[]{:S(2)}) %collective-permute-start.55) | collective-permute-done | bytes 524320 | tf_op jit(solution)/shard_map/ppermute | solution.py:947
  218.5 4.8 %all-to-all-start.2 = ((bf16[4,704,256]{2,1,0:T(8,128)(2,1)}), bf16[4,704,256]{2,1,0:T(8,128)(2,1)S(1)}, u32[]{:S(2)}, u32[]{:S(2)}) async-start(bf16[4,704,256]{2,1,0:T(8,128)(2,1)} %self_grad.1), calls=%async_computation.2 | async-start | bytes 2883584 | tf_op jit(solution)/shard_map/all_to_all | solution.py:705
  223.3 2.0 add_convert_fusion
  225.3 2.9 %reduce_sum.43 = bf16[1536,256]{1,0:T(8,128)(2,1)S(1)} reduce(bf16[4,1536,256]{2,1,0:T(8,128)(2,1)} %all-to-all-done.1, bf16[]{:T(256)} %constant.45.clone.1), dimensions={0}, to_apply=%region_1.2 | reduce | flops 1179648 | bytes 3932162 | tf_op jit(solution)/shard_map/reduce_sum | solution.py:708
  231.3 2.0 collective-permute-done.58
  233.2 4.2 %collective-permute-done.59 = bf16[384,256]{1,0:T(8,128)(2,1)S(1)} collective-permute-done((bf16[384,256]{1,0:T(8,128)(2,1)S(1)}, bf16[384,256]{1,0:T(8,128)(2,1)S(1)}, u32[]{:S(2)}, u32[]{:S(2)}) %collective-permute-start.59) | collective-permute-done | bytes 196640 | tf_op jit(solution)/shard_map/ppermute | solution.py:1011
  237.4 10.0 %collective-permute-done.60 = bf16[384,256]{1,0:T(8,128)(2,1)S(1)} collective-permute-done((bf16[384,256]{1,0:T(8,128)(2,1)S(1)}, bf16[384,256]{1,0:T(8,128)(2,1)S(1)}, u32[]{:S(2)}, u32[]{:S(2)}) %collective-permute-start.60) | collective-permute-done | bytes 196640 | tf_op jit(solution)/shard_map/ppermute | solution.py:1011
  248.0 1.5 broadcast_in_dim.23
  249.6 4.0 %all-to-all-start.3 = ((bf16[4,1024,256]{2,1,0:T(8,128)(2,1)}), bf16[4,1024,256]{2,1,0:T(8,128)(2,1)S(1)}, u32[]{:S(2)}, u32[]{:S(2)}) async-start(bf16[4,1024,256]{2,1,0:T(8,128)(2,1)} %broadcast_in_dim.23), calls=%async_computation.3 | async-start | bytes 4194304 | tf_op jit(solution)/shard_map/all_to_all | solution.py:690
  253.6 2.5 collective-permute-start.61
  257.1 1.7 collective-permute-start.63
  259.8 4.7 %place_mlp.1 = (f32[512,1024]{1,0:T(8,128)}, f32[1024,512]{1,0:T(8,128)}) custom-call(s32[4]{0:T(128)} %pad_add_fusion.refs_0_.idx, bf16[1024,256]{1,0:T(8,128)(2,1)} %sum_mlp.1.refs_1_, bf16[1024,256]{1,0:T(8,128)(2,1)} %copy-done.23, bf16[1024,256]{1,0:T(8,128)(2,1)} %copy-done.24, bf16[1024,256]{1,0:T(8,128)(2,1)} %copy-done.25), custom_call_target="tpu_custom_call" | custom-call | flops 1 | bytes 1 | tf_op jit(solution)/shard_map/place_mlp/pallas_call | solution.py:111
  264.4 8.4 %collective-permute-done.65.refs_7_ = bf16[128,1024]{1,0:T(8,128)(2,1)S(1)} collective-permute-done((bf16[128,1024]{1,0:T(8,128)(2,1)S(1)}, bf16[128,1024]{1,0:T(8,128)(2,1)S(1)}, u32[]{:S(2)}, u32[]{:S(2)}) %collective-permute-start.65) | collective-permute-done | bytes 262176 | tf_op jit(solution)/shard_map/ppermute | solution.py:1016
  273.5 4.3 %tokens.1 = f32[128,1024]{1,0:T(8,128)} custom-call(s32[4]{0:T(128)} %pad_add_fusion.refs_0_.idx, bf16[1024,1024]{1,0:T(8,128)(2,1)} %refs_1_.15, bf16[3,1024]{1,0:T(4,128)(2,1)} %refs_2_.9, f32[128,1024]{1,0:T(8,128)} %get-tuple-element.325.refs_3_, bf16[128,1024]{1,0:T(8,128)(2,1)} %get-tuple-element.300.refs_4_, bf16[128,1024]{1,0:T(8,128)(2,1)} %copy-done.29, ...), custom_call_target="tpu_custom_call" | custom-call | flops 1 | bytes 1 | tf_op jit(solution)/shard_map/tokens/pallas_call | solution.py:111
  281.0 1.7 dynamic_update_slice.11
  284.0 3.0 %place.1 = (f32[128,1024]{1,0:T(8,128)}, f32[1024,128]{1,0:T(8,128)}, f32[128,1024]{1,0:T(8,128)}, f32[3,1024,128]{2,1,0:T(8,128)}, f32[2,1024,128]{2,1,0:T(8,128)}) custom-call(s32[4]{0:T(128)S(1)} %copy-done.9, bf16[4,1024,256]{2,1,0:T(8,128)(2,1)S(1)} %all-to-all-done.3.refs_1_), custom_call_target="tpu_custom_call" | custom-call | flops 1 | bytes 1 | tf_op jit(solution)/shard_map/place/pallas_call | solution.py:111
  (246 shorter events, 42.2 us)
Async XLA Ops:
  0.6 23.1 %collective-permute-start.3 = (bf16[512,1024]{1,0:T(8,128)(2,1)}, bf16[512,1024]{1,0:T(8,128)(2,1)S(1)}, u32[]{:S(2)}, u32[]{:S(2)}) collective-permute-start(bf16[512,1024]{1,0:T(8,128)(2,1)} %refs_1_.12), channel_id=1, source_target_pairs={{0,1},{1,0},{2,3},{3,2},{4,5},{5,4},{6,7},{7,6},{8,9},{9,8},{10,11... | collective-permute-start | bytes 3145736 | tf_op jit(solution)/shard_map/ppermute | solution.py:719
  3.6 17.9 %collective-permute-start = (bf16[384,256]{1,0:T(8,128)(2,1)S(1)}, bf16[384,256]{1,0:T(8,128)(2,1)S(1)}, u32[]{:S(2)}, u32[]{:S(2)}) collective-permute-start(bf16[384,256]{1,0:T(8,128)(2,1)S(1)} %constant_dynamic-slice_fusion.2), channel_id=1, source_target_pairs={{0,2},{1,3},{2,0},{3,1},{4,6},{5,7},{6,4},{7,5},{8,10},{9,11},{10,... | collective-permute-start | bytes 589832 | tf_op jit(solution)/shard_map/ppermute | solution.py:718
  3.9 17.7 %collective-permute-start.1 = (bf16[384,256]{1,0:T(8,128)(2,1)S(1)}, bf16[384,256]{1,0:T(8,128)(2,1)S(1)}, u32[]{:S(2)}, u32[]{:S(2)}) collective-permute-start(bf16[384,256]{1,0:T(8,128)(2,1)S(1)} %constant_dynamic-slice_fusion.2), channel_id=1, source_target_pairs={{0,4},{1,5},{2,6},{3,7},{4,0},{5,1},{6,2},{7,3},{8,12},{9,13},{10,... | collective-permute-start | bytes 589832 | tf_op jit(solution)/shard_map/ppermute | solution.py:718
  6.2 17.6 %collective-permute-start.2 = (bf16[384,256]{1,0:T(8,128)(2,1)S(1)}, bf16[384,256]{1,0:T(8,128)(2,1)S(1)}, u32[]{:S(2)}, u32[]{:S(2)}) collective-permute-start(bf16[384,256]{1,0:T(8,128)(2,1)S(1)} %constant_dynamic-slice_fusion.2), channel_id=1, source_target_pairs={{0,6},{1,7},{2,4},{3,5},{4,2},{5,3},{6,0},{7,1},{8,14},{9,15},{10,... | collective-permute-start | bytes 589832 | tf_op jit(solution)/shard_map/ppermute | solution.py:718
  24.3 20.3 %collective-permute-start.4 = (bf16[1152,256]{1,0:T(8,128)(2,1)S(1)}, bf16[1152,256]{1,0:T(8,128)(2,1)S(1)}, u32[]{:S(2)}, u32[]{:S(2)}) collective-permute-start(bf16[1152,256]{1,0:T(8,128)(2,1)S(1)} %pack.1.refs_6_.refs_8_), channel_id=1, source_target_pairs={{0,8},{8,0},{16,24},{24,16},{1,9},{9,1},{17,25},{25,17},{2,10},{10... | collective-permute-start | bytes 1769480 | tf_op jit(solution)/shard_map/ppermute | solution.py:765
  24.7 20.5 %collective-permute-start.5 = (bf16[1152,256]{1,0:T(8,128)(2,1)S(1)}, bf16[1152,256]{1,0:T(8,128)(2,1)}, u32[]{:S(2)}, u32[]{:S(2)}) collective-permute-start(bf16[1152,256]{1,0:T(8,128)(2,1)S(1)} %pack.1.refs_6_.refs_8_), channel_id=1, source_target_pairs={{0,16},{8,24},{16,0},{24,8},{1,17},{9,25},{17,1},{25,9},{2,18},{10... | collective-permute-start | bytes 1769480 | tf_op jit(solution)/shard_map/ppermute | solution.py:765
  25.9 26.2 %collective-permute-start.6 = (bf16[1152,256]{1,0:T(8,128)(2,1)S(1)}, bf16[1152,256]{1,0:T(8,128)(2,1)}, u32[]{:S(2)}, u32[]{:S(2)}) collective-permute-start(bf16[1152,256]{1,0:T(8,128)(2,1)S(1)} %pack.1.refs_6_.refs_8_), channel_id=1, source_target_pairs={{0,24},{8,16},{16,8},{24,0},{1,25},{9,17},{17,9},{25,1},{2,26},{10... | collective-permute-start | bytes 1769480 | tf_op jit(solution)/shard_map/ppermute | solution.py:765
  27.1 4.1 %collective-permute-start.12 = (bf16[384,128]{1,0:T(8,128)(2,1)}, bf16[384,128]{1,0:T(8,128)(2,1)}, u32[]{:S(2)}, u32[]{:S(2)}) collective-permute-start(bf16[384,128]{1,0:T(8,128)(2,1)} %get-tuple-element.197), channel_id=1, source_target_pairs={{0,2},{1,3},{2,0},{3,1},{4,6},{5,7},{6,4},{7,5},{8,10},{9,11},{10,... | collective-permute-start | bytes 294920 | tf_op jit(solution)/shard_map/ppermute | solution.py:750
  27.1 5.9 %collective-permute-start.13 = (bf16[384,128]{1,0:T(8,128)(2,1)}, bf16[384,128]{1,0:T(8,128)(2,1)}, u32[]{:S(2)}, u32[]{:S(2)}) collective-permute-start(bf16[384,128]{1,0:T(8,128)(2,1)} %get-tuple-element.198), channel_id=1, source_target_pairs={{0,4},{1,5},{2,6},{3,7},{4,0},{5,1},{6,2},{7,3},{8,12},{9,13},{10,... | collective-permute-start | bytes 294920 | tf_op jit(solution)/shard_map/ppermute | solution.py:750
  31.1 13.4 %collective-permute-start.14 = (bf16[384,128]{1,0:T(8,128)(2,1)}, bf16[384,128]{1,0:T(8,128)(2,1)}, u32[]{:S(2)}, u32[]{:S(2)}) collective-permute-start(bf16[384,128]{1,0:T(8,128)(2,1)} %get-tuple-element.199), channel_id=1, source_target_pairs={{0,6},{1,7},{2,4},{3,5},{4,2},{5,3},{6,0},{7,1},{8,14},{9,15},{10,... | collective-permute-start | bytes 294920 | tf_op jit(solution)/shard_map/ppermute | solution.py:750
  33.0 22.7 %collective-permute-start.7 = (bf16[384,1024]{1,0:T(8,128)(2,1)S(1)}, bf16[384,1024]{1,0:T(8,128)(2,1)}, u32[]{:S(2)}, u32[]{:S(2)}) collective-permute-start(bf16[384,1024]{1,0:T(8,128)(2,1)S(1)} %pad_maximum_fusion.refs_5_.refs_7_), channel_id=1, source_target_pairs={{0,1},{1,0},{2,3},{3,2},{4,5},{5,4},{6,7},{7,6},{8,9},{9,8},{10,11... | collective-permute-start | bytes 2359304 | tf_op jit(solution)/shard_map/ppermute | solution.py:767
  44.6 10.0 %collective-permute-start.15 = (bf16[384,128]{1,0:T(8,128)(2,1)S(1)}, bf16[384,128]{1,0:T(8,128)(2,1)}, u32[]{:S(2)}, u32[]{:S(2)}) collective-permute-start(bf16[384,128]{1,0:T(8,128)(2,1)S(1)} %copy-done.36), channel_id=1, source_target_pairs={{0,1},{1,0},{2,3},{3,2},{4,5},{5,4},{6,7},{7,6},{8,9},{9,8},{10,11... | collective-permute-start | bytes 294920 | tf_op jit(solution)/shard_map/ppermute | solution.py:751
  44.7 10.0 %collective-permute-start.16 = (bf16[384,128]{1,0:T(8,128)(2,1)}, bf16[384,128]{1,0:T(8,128)(2,1)}, u32[]{:S(2)}, u32[]{:S(2)}) collective-permute-start(bf16[384,128]{1,0:T(8,128)(2,1)} %collective-permute-done.12.refs_16_.refs_21_), channel_id=1, source_target_pairs={{0,1},{1,0},{2,3},{3,2},{4,5},{5,4},{6,7},{7,6},{8,9},{9,8},{10,11... | collective-permute-start | bytes 294920 | tf_op jit(solution)/shard_map/ppermute | solution.py:751
  45.1 10.0 %collective-permute-start.17 = (bf16[384,128]{1,0:T(8,128)(2,1)}, bf16[384,128]{1,0:T(8,128)(2,1)}, u32[]{:S(2)}, u32[]{:S(2)}) collective-permute-start(bf16[384,128]{1,0:T(8,128)(2,1)} %collective-permute-done.13.refs_17_.refs_22_), channel_id=1, source_target_pairs={{0,1},{1,0},{2,3},{3,2},{4,5},{5,4},{6,7},{7,6},{8,9},{9,8},{10,11... | collective-permute-start | bytes 294920 | tf_op jit(solution)/shard_map/ppermute | solution.py:751
  52.1 3.1 %collective-permute-start.18 = (bf16[384,128]{1,0:T(8,128)(2,1)}, bf16[384,128]{1,0:T(8,128)(2,1)}, u32[]{:S(2)}, u32[]{:S(2)}) collective-permute-start(bf16[384,128]{1,0:T(8,128)(2,1)} %collective-permute-done.14.refs_18_.refs_23_), channel_id=1, source_target_pairs={{0,1},{1,0},{2,3},{3,2},{4,5},{5,4},{6,7},{7,6},{8,9},{9,8},{10,11... | collective-permute-start | bytes 294920 | tf_op jit(solution)/shard_map/ppermute | solution.py:751
  55.1 3.4 %collective-permute-start.8 = (bf16[1152,256]{1,0:T(8,128)(2,1)S(1)}, bf16[1152,256]{1,0:T(8,128)(2,1)S(1)}, u32[]{:S(2)}, u32[]{:S(2)}) collective-permute-start(bf16[1152,256]{1,0:T(8,128)(2,1)S(1)} %pack.1.refs_6_.refs_8_), channel_id=1, source_target_pairs={{0,1},{1,0},{2,3},{3,2},{4,5},{5,4},{6,7},{7,6},{8,9},{9,8},{10,11... | collective-permute-start | bytes 1769480 | tf_op jit(solution)/shard_map/ppermute | solution.py:767
  55.2 4.3 %collective-permute-start.9 = (bf16[1152,256]{1,0:T(8,128)(2,1)}, bf16[1152,256]{1,0:T(8,128)(2,1)}, u32[]{:S(2)}, u32[]{:S(2)}) collective-permute-start(bf16[1152,256]{1,0:T(8,128)(2,1)} %copy-done.18), channel_id=1, source_target_pairs={{0,1},{1,0},{2,3},{3,2},{4,5},{5,4},{6,7},{7,6},{8,9},{9,8},{10,11... | collective-permute-start | bytes 1769480 | tf_op jit(solution)/shard_map/ppermute | solution.py:767
  70.3 7.7 %collective-permute-start.21 = (bf16[128,1024]{1,0:T(8,128)(2,1)}, bf16[128,1024]{1,0:T(8,128)(2,1)S(1)}, u32[]{:S(2)}, u32[]{:S(2)}) collective-permute-start(bf16[128,1024]{1,0:T(8,128)(2,1)} %get-tuple-element.204.same), channel_id=1, source_target_pairs={{0,2},{1,3},{2,0},{3,1},{4,6},{5,7},{6,4},{7,5},{8,10},{9,11},{10,... | collective-permute-start | bytes 786440 | tf_op jit(solution)/shard_map/ppermute | solution.py:801
  70.3 7.7 %collective-permute-start.22 = (bf16[128,1024]{1,0:T(8,128)(2,1)}, bf16[128,1024]{1,0:T(8,128)(2,1)S(1)}, u32[]{:S(2)}, u32[]{:S(2)}) collective-permute-start(bf16[128,1024]{1,0:T(8,128)(2,1)} %get-tuple-element.204.same), channel_id=1, source_target_pairs={{0,6},{1,7},{2,4},{3,5},{4,2},{5,3},{6,0},{7,1},{8,14},{9,15},{10,... | collective-permute-start | bytes 786440 | tf_op jit(solution)/shard_map/ppermute | solution.py:801
  78.1 9.5 %collective-permute-start.23 = (bf16[128,1024]{1,0:T(8,128)(2,1)S(1)}, bf16[128,1024]{1,0:T(8,128)(2,1)S(1)}, u32[]{:S(2)}, u32[]{:S(2)}) collective-permute-start(bf16[128,1024]{1,0:T(8,128)(2,1)S(1)} %collective-permute-done.21.same), channel_id=1, source_target_pairs={{0,1},{1,0},{2,3},{3,2},{4,5},{5,4},{6,7},{7,6},{8,9},{9,8},{10,11... | collective-permute-start | bytes 786440 | tf_op jit(solution)/shard_map/ppermute | solution.py:819
  80.1 9.6 %collective-permute-start.25 = (bf16[128,1024]{1,0:T(8,128)(2,1)S(1)}, bf16[128,1024]{1,0:T(8,128)(2,1)S(1)}, u32[]{:S(2)}, u32[]{:S(2)}) collective-permute-start(bf16[128,1024]{1,0:T(8,128)(2,1)S(1)} %collective-permute-done.22.same), channel_id=1, source_target_pairs={{0,1},{1,0},{2,3},{3,2},{4,5},{5,4},{6,7},{7,6},{8,9},{9,8},{10,11... | collective-permute-start | bytes 786440 | tf_op jit(solution)/shard_map/ppermute | solution.py:819
  80.1 14.7 %collective-permute-start.20 = (bf16[128,1536]{1,0:T(8,128)(2,1)S(1)}, bf16[128,1536]{1,0:T(8,128)(2,1)S(1)}, u32[]{:S(2)}, u32[]{:S(2)}) collective-permute-start(bf16[128,1536]{1,0:T(8,128)(2,1)S(1)} %get-tuple-element.207), channel_id=1, source_target_pairs={{0,1},{1,0},{2,3},{3,2},{4,5},{5,4},{6,7},{7,6},{8,9},{9,8},{10,11... | collective-permute-start | bytes 1179656 | tf_op jit(solution)/shard_map/ppermute | solution.py:837
  80.6 13.7 %collective-permute-start.27 = (bf16[128,1024]{1,0:T(8,128)(2,1)S(1)}, bf16[128,1024]{1,0:T(8,128)(2,1)S(1)}, u32[]{:S(2)}, u32[]{:S(2)}) collective-permute-start(bf16[128,1024]{1,0:T(8,128)(2,1)S(1)} %collective-permute-done.22.same), channel_id=1, source_target_pairs={{0,2},{1,3},{2,0},{3,1},{4,6},{5,7},{6,4},{7,5},{8,10},{9,11},{10,... | collective-permute-start | bytes 786440 | tf_op jit(solution)/shard_map/ppermute | solution.py:842
  91.9 7.4 %collective-permute-start.26 = (bf16[128,1536]{1,0:T(8,128)(2,1)S(1)}, bf16[128,1536]{1,0:T(8,128)(2,1)S(1)}, u32[]{:S(2)}, u32[]{:S(2)}) collective-permute-start(bf16[128,1536]{1,0:T(8,128)(2,1)S(1)} %get-tuple-element.219), channel_id=1, source_target_pairs={{0,1},{1,0},{2,3},{3,2},{4,5},{5,4},{6,7},{7,6},{8,9},{9,8},{10,11... | collective-permute-start | bytes 1179656 | tf_op jit(solution)/shard_map/ppermute | solution.py:837
  94.8 6.8 %collective-permute-start.24 = (bf16[128,1536]{1,0:T(8,128)(2,1)S(1)}, bf16[128,1536]{1,0:T(8,128)(2,1)S(1)}, u32[]{:S(2)}, u32[]{:S(2)}) collective-permute-start(bf16[128,1536]{1,0:T(8,128)(2,1)S(1)} %get-tuple-element.213), channel_id=1, source_target_pairs={{0,1},{1,0},{2,3},{3,2},{4,5},{5,4},{6,7},{7,6},{8,9},{9,8},{10,11... | collective-permute-start | bytes 1179656 | tf_op jit(solution)/shard_map/ppermute | solution.py:837
  98.9 12.1 %collective-permute-start.31 = (bf16[128,1536]{1,0:T(8,128)(2,1)}, bf16[128,1536]{1,0:T(8,128)(2,1)}, u32[]{:S(2)}, u32[]{:S(2)}) collective-permute-start(bf16[128,1536]{1,0:T(8,128)(2,1)} %get-tuple-element.236), channel_id=1, source_target_pairs={{0,1},{1,0},{2,3},{3,2},{4,5},{5,4},{6,7},{7,6},{8,9},{9,8},{10,11... | collective-permute-start | bytes 1179656 | tf_op jit(solution)/shard_map/ppermute | solution.py:837
  100.2 10.8 %collective-permute-start.29 = (bf16[128,1024]{1,0:T(8,128)(2,1)}, bf16[128,1024]{1,0:T(8,128)(2,1)}, u32[]{:S(2)}, u32[]{:S(2)}) collective-permute-start(bf16[128,1024]{1,0:T(8,128)(2,1)} %add_convert_fusion.3), channel_id=1, source_target_pairs={{0,2},{1,3},{2,0},{3,1},{4,6},{5,7},{6,4},{7,5},{8,10},{9,11},{10,... | collective-permute-start | bytes 786440 | tf_op jit(solution)/shard_map/ppermute | solution.py:845
  102.5 12.1 %collective-permute-start.30 = (bf16[128,1024]{1,0:T(8,128)(2,1)}, bf16[128,1024]{1,0:T(8,128)(2,1)}, u32[]{:S(2)}, u32[]{:S(2)}) collective-permute-start(bf16[128,1024]{1,0:T(8,128)(2,1)} %add_convert_fusion.4), channel_id=1, source_target_pairs={{0,2},{1,3},{2,0},{3,1},{4,6},{5,7},{6,4},{7,5},{8,10},{9,11},{10,... | collective-permute-start | bytes 786440 | tf_op jit(solution)/shard_map/ppermute | solution.py:843
  112.1 14.2 %collective-permute-start.32 = (bf16[128,1024]{1,0:T(8,128)(2,1)S(1)}, bf16[128,1024]{1,0:T(8,128)(2,1)S(1)}, u32[]{:S(2)}, u32[]{:S(2)}) collective-permute-start(bf16[128,1024]{1,0:T(8,128)(2,1)S(1)} %add_convert_fusion.1), channel_id=1, source_target_pairs={{0,4},{1,5},{2,6},{3,7},{4,0},{5,1},{6,2},{7,3},{8,12},{9,13},{10,... | collective-permute-start | bytes 786440 | tf_op jit(solution)/shard_map/ppermute | solution.py:866
  113.6 37.8 %collective-permute-start.38 = (bf16[3,128,1024]{2,1,0:T(8,128)(2,1)}, bf16[3,128,1024]{2,1,0:T(8,128)(2,1)}, u32[]{:S(2)}, u32[]{:S(2)}) collective-permute-start(bf16[3,128,1024]{2,1,0:T(8,128)(2,1)} %get-tuple-element.264.refs_1_), channel_id=1, source_target_pairs={{0,1},{1,0},{2,3},{3,2},{4,5},{5,4},{6,7},{7,6},{8,9},{9,8},{10,11... | collective-permute-start | bytes 2359304 | tf_op jit(solution)/shard_map/ppermute | solution.py:802
  114.6 30.2 %all-to-all-start = ((bf16[4,1040,256]{2,1,0:T(8,128)(2,1)}), bf16[4,1040,256]{2,1,0:T(8,128)(2,1)}, u32[]{:S(2)}, u32[]{:S(2)}) async-start(bf16[4,1040,256]{2,1,0:T(8,128)(2,1)} %mlp_grad.1), calls=%async_computation | async-start | bytes 4259840 | tf_op jit(solution)/shard_map/all_to_all | solution.py:705
  126.4 15.0 %collective-permute-start.33 = (bf16[128,1024]{1,0:T(8,128)(2,1)}, bf16[128,1024]{1,0:T(8,128)(2,1)}, u32[]{:S(2)}, u32[]{:S(2)}) collective-permute-start(bf16[128,1024]{1,0:T(8,128)(2,1)} %get-tuple-element.258), channel_id=1, source_target_pairs={{0,2},{1,3},{2,0},{3,1},{4,6},{5,7},{6,4},{7,5},{8,10},{9,11},{10,... | collective-permute-start | bytes 786440 | tf_op jit(solution)/shard_map/ppermute | solution.py:888
  128.1 13.2 %collective-permute-start.34 = (bf16[128,1024]{1,0:T(8,128)(2,1)}, bf16[128,1024]{1,0:T(8,128)(2,1)}, u32[]{:S(2)}, u32[]{:S(2)}) collective-permute-start(bf16[128,1024]{1,0:T(8,128)(2,1)} %get-tuple-element.259), channel_id=1, source_target_pairs={{0,4},{1,5},{2,6},{3,7},{4,0},{5,1},{6,2},{7,3},{8,12},{9,13},{10,... | collective-permute-start | bytes 786440 | tf_op jit(solution)/shard_map/ppermute | solution.py:888
  144.8 9.1 %collective-permute-start.39 = (bf16[3,128,1024]{2,1,0:T(8,128)(2,1)}, bf16[3,128,1024]{2,1,0:T(8,128)(2,1)S(1)}, u32[]{:S(2)}, u32[]{:S(2)}) collective-permute-start(bf16[3,128,1024]{2,1,0:T(8,128)(2,1)} %get-tuple-element.265.refs_3_), channel_id=1, source_target_pairs={{0,1},{1,0},{2,3},{3,2},{4,5},{5,4},{6,7},{7,6},{8,9},{9,8},{10,11... | collective-permute-start | bytes 2359304 | tf_op jit(solution)/shard_map/ppermute | solution.py:939
  149.3 13.8 %collective-permute-start.40 = (bf16[1024,256]{1,0:T(8,128)(2,1)}, bf16[1024,256]{1,0:T(8,128)(2,1)S(1)}, u32[]{:S(2)}, u32[]{:S(2)}) collective-permute-start(bf16[1024,256]{1,0:T(8,128)(2,1)} %sum_mlp.1.refs_1_), channel_id=1, source_target_pairs={{0,8},{8,0},{16,24},{24,16},{1,9},{9,1},{17,25},{25,17},{2,10},{10... | collective-permute-start | bytes 1572872 | tf_op jit(solution)/shard_map/ppermute | solution.py:927
  149.7 13.4 %collective-permute-start.41 = (bf16[1024,256]{1,0:T(8,128)(2,1)}, bf16[1024,256]{1,0:T(8,128)(2,1)S(1)}, u32[]{:S(2)}, u32[]{:S(2)}) collective-permute-start(bf16[1024,256]{1,0:T(8,128)(2,1)} %sum_mlp.1.refs_1_), channel_id=1, source_target_pairs={{0,16},{8,24},{16,0},{24,8},{1,17},{9,25},{17,1},{25,9},{2,18},{10... | collective-permute-start | bytes 1572872 | tf_op jit(solution)/shard_map/ppermute | solution.py:927
  151.5 8.7 %collective-permute-start.35 = (bf16[2,128,128]{2,1,0:T(8,128)(2,1)S(1)}, bf16[2,128,128]{2,1,0:T(8,128)(2,1)S(1)}, u32[]{:S(2)}, u32[]{:S(2)}) collective-permute-start(bf16[2,128,128]{2,1,0:T(8,128)(2,1)S(1)} %copy-done.49), channel_id=1, source_target_pairs={{0,2},{1,3},{2,0},{3,1},{4,6},{5,7},{6,4},{7,5},{8,10},{9,11},{10,... | collective-permute-start | bytes 196616 | tf_op jit(solution)/shard_map/ppermute | solution.py:930
  152.4 7.7 %collective-permute-start.36 = (bf16[2,128,128]{2,1,0:T(8,128)(2,1)S(1)}, bf16[2,128,128]{2,1,0:T(8,128)(2,1)S(1)}, u32[]{:S(2)}, u32[]{:S(2)}) collective-permute-start(bf16[2,128,128]{2,1,0:T(8,128)(2,1)S(1)} %copy-done.48), channel_id=1, source_target_pairs={{0,4},{1,5},{2,6},{3,7},{4,0},{5,1},{6,2},{7,3},{8,12},{9,13},{10,... | collective-permute-start | bytes 196616 | tf_op jit(solution)/shard_map/ppermute | solution.py:930
  153.9 6.8 %collective-permute-start.37 = (bf16[2,128,128]{2,1,0:T(8,128)(2,1)S(1)}, bf16[2,128,128]{2,1,0:T(8,128)(2,1)S(1)}, u32[]{:S(2)}, u32[]{:S(2)}) collective-permute-start(bf16[2,128,128]{2,1,0:T(8,128)(2,1)S(1)} %copy-done.46), channel_id=1, source_target_pairs={{0,6},{1,7},{2,4},{3,5},{4,2},{5,3},{6,0},{7,1},{8,14},{9,15},{10,... | collective-permute-start | bytes 196616 | tf_op jit(solution)/shard_map/ppermute | solution.py:930
  163.1 9.0 %collective-permute-start.42 = (bf16[2,128,128]{2,1,0:T(8,128)(2,1)S(1)}, bf16[2,128,128]{2,1,0:T(8,128)(2,1)S(1)}, u32[]{:S(2)}, u32[]{:S(2)}) collective-permute-start(bf16[2,128,128]{2,1,0:T(8,128)(2,1)S(1)} %copy-done.43), channel_id=1, source_target_pairs={{0,1},{1,0},{2,3},{3,2},{4,5},{5,4},{6,7},{7,6},{8,9},{9,8},{10,11... | collective-permute-start | bytes 196616 | tf_op jit(solution)/shard_map/ppermute | solution.py:948
  164.3 9.5 %collective-permute-start.43 = (bf16[2,128,128]{2,1,0:T(8,128)(2,1)S(1)}, bf16[2,128,128]{2,1,0:T(8,128)(2,1)S(1)}, u32[]{:S(2)}, u32[]{:S(2)}) collective-permute-start(bf16[2,128,128]{2,1,0:T(8,128)(2,1)S(1)} %collective-permute-done.35.refs_5_), channel_id=1, source_target_pairs={{0,1},{1,0},{2,3},{3,2},{4,5},{5,4},{6,7},{7,6},{8,9},{9,8},{10,11... | collective-permute-start | bytes 196616 | tf_op jit(solution)/shard_map/ppermute | solution.py:948
  164.3 9.7 %collective-permute-start.44 = (bf16[2,128,128]{2,1,0:T(8,128)(2,1)S(1)}, bf16[2,128,128]{2,1,0:T(8,128)(2,1)S(1)}, u32[]{:S(2)}, u32[]{:S(2)}) collective-permute-start(bf16[2,128,128]{2,1,0:T(8,128)(2,1)S(1)} %collective-permute-done.36.refs_6_), channel_id=1, source_target_pairs={{0,1},{1,0},{2,3},{3,2},{4,5},{5,4},{6,7},{7,6},{8,9},{9,8},{10,11... | collective-permute-start | bytes 196616 | tf_op jit(solution)/shard_map/ppermute | solution.py:948
  164.8 10.4 %collective-permute-start.45 = (bf16[2,128,128]{2,1,0:T(8,128)(2,1)S(1)}, bf16[2,128,128]{2,1,0:T(8,128)(2,1)S(1)}, u32[]{:S(2)}, u32[]{:S(2)}) collective-permute-start(bf16[2,128,128]{2,1,0:T(8,128)(2,1)S(1)} %collective-permute-done.37.refs_7_), channel_id=1, source_target_pairs={{0,1},{1,0},{2,3},{3,2},{4,5},{5,4},{6,7},{7,6},{8,9},{9,8},{10,11... | collective-permute-start | bytes 196616 | tf_op jit(solution)/shard_map/ppermute | solution.py:948
  165.5 25.0 %collective-permute-start.52 = (bf16[2,64,128]{2,1,0:T(8,128)(2,1)}, bf16[2,64,128]{2,1,0:T(8,128)(2,1)}, u32[]{:S(2)}, u32[]{:S(2)}) collective-permute-start(bf16[2,64,128]{2,1,0:T(8,128)(2,1)} %get-tuple-element.363), channel_id=1, source_target_pairs={{0,2},{1,3},{2,0},{3,1},{4,6},{5,7},{6,4},{7,5},{8,10},{9,11},{10,... | collective-permute-start | bytes 98312 | tf_op jit(solution)/shard_map/ppermute | solution.py:979
  166.2 52.2 %all-to-all-start.1 = ((bf16[4,1536,256]{2,1,0:T(8,128)(2,1)}), bf16[4,1536,256]{2,1,0:T(8,128)(2,1)}, u32[]{:S(2)}, u32[]{:S(2)}) async-start(bf16[4,1536,256]{2,1,0:T(8,128)(2,1)} %row_grad.1), calls=%async_computation.1 | async-start | bytes 6291456 | tf_op jit(solution)/shard_map/all_to_all | solution.py:705
  172.1 18.9 %collective-permute-start.53 = (bf16[2,64,128]{2,1,0:T(8,128)(2,1)}, bf16[2,64,128]{2,1,0:T(8,128)(2,1)}, u32[]{:S(2)}, u32[]{:S(2)}) collective-permute-start(bf16[2,64,128]{2,1,0:T(8,128)(2,1)} %get-tuple-element.365), channel_id=1, source_target_pairs={{0,4},{1,5},{2,6},{3,7},{4,0},{5,1},{6,2},{7,3},{8,12},{9,13},{10,... | collective-permute-start | bytes 98312 | tf_op jit(solution)/shard_map/ppermute | solution.py:979
  173.7 17.4 %collective-permute-start.54 = (bf16[2,64,128]{2,1,0:T(8,128)(2,1)}, bf16[2,64,128]{2,1,0:T(8,128)(2,1)}, u32[]{:S(2)}, u32[]{:S(2)}) collective-permute-start(bf16[2,64,128]{2,1,0:T(8,128)(2,1)} %get-tuple-element.364), channel_id=1, source_target_pairs={{0,6},{1,7},{2,4},{3,5},{4,2},{5,3},{6,0},{7,1},{8,14},{9,15},{10,... | collective-permute-start | bytes 98312 | tf_op jit(solution)/shard_map/ppermute | solution.py:979
  174.0 15.4 %collective-permute-start.46 = (bf16[128,1024]{1,0:T(8,128)(2,1)}, bf16[128,1024]{1,0:T(8,128)(2,1)}, u32[]{:S(2)}, u32[]{:S(2)}) collective-permute-start(bf16[128,1024]{1,0:T(8,128)(2,1)} %get-tuple-element.284), channel_id=1, source_target_pairs={{0,6},{1,7},{2,4},{3,5},{4,2},{5,3},{6,0},{7,1},{8,14},{9,15},{10,... | collective-permute-start | bytes 786440 | tf_op jit(solution)/shard_map/ppermute | solution.py:950
  189.4 4.3 %collective-permute-start.47 = (bf16[128,1024]{1,0:T(8,128)(2,1)}, bf16[128,1024]{1,0:T(8,128)(2,1)S(1)}, u32[]{:S(2)}, u32[]{:S(2)}) collective-permute-start(bf16[128,1024]{1,0:T(8,128)(2,1)} %get-tuple-element.285.refs_11_), channel_id=1, source_target_pairs={{0,1},{1,0},{2,3},{3,2},{4,5},{5,4},{6,7},{7,6},{8,9},{9,8},{10,11... | collective-permute-start | bytes 786440 | tf_op jit(solution)/shard_map/ppermute | solution.py:976
  190.5 3.2 %collective-permute-start.48 = (bf16[128,1024]{1,0:T(8,128)(2,1)}, bf16[128,1024]{1,0:T(8,128)(2,1)S(1)}, u32[]{:S(2)}, u32[]{:S(2)}) collective-permute-start(bf16[128,1024]{1,0:T(8,128)(2,1)} %get-tuple-element.286.refs_12_), channel_id=1, source_target_pairs={{0,1},{1,0},{2,3},{3,2},{4,5},{5,4},{6,7},{7,6},{8,9},{9,8},{10,11... | collective-permute-start | bytes 786440 | tf_op jit(solution)/shard_map/ppermute | solution.py:976
  190.5 3.2 %collective-permute-start.49 = (bf16[128,1024]{1,0:T(8,128)(2,1)}, bf16[128,1024]{1,0:T(8,128)(2,1)S(1)}, u32[]{:S(2)}, u32[]{:S(2)}) collective-permute-start(bf16[128,1024]{1,0:T(8,128)(2,1)} %get-tuple-element.287.refs_13_), channel_id=1, source_target_pairs={{0,1},{1,0},{2,3},{3,2},{4,5},{5,4},{6,7},{7,6},{8,9},{9,8},{10,11... | collective-permute-start | bytes 786440 | tf_op jit(solution)/shard_map/ppermute | solution.py:976
  191.1 27.4 %collective-permute-start.55 = (bf16[1024,256]{1,0:T(8,128)(2,1)S(1)}, bf16[1024,256]{1,0:T(8,128)(2,1)S(1)}, u32[]{:S(2)}, u32[]{:S(2)}) collective-permute-start(bf16[1024,256]{1,0:T(8,128)(2,1)S(1)} %copy-done.12), channel_id=1, source_target_pairs={{0,24},{8,16},{16,8},{24,0},{1,25},{9,17},{17,9},{25,1},{2,26},{10... | collective-permute-start | bytes 1572872 | tf_op jit(solution)/shard_map/ppermute | solution.py:947
  198.7 19.8 %collective-permute-start.56 = (bf16[128,1024]{1,0:T(8,128)(2,1)}, bf16[128,1024]{1,0:T(8,128)(2,1)S(1)}, u32[]{:S(2)}, u32[]{:S(2)}) collective-permute-start(bf16[128,1024]{1,0:T(8,128)(2,1)} %get-tuple-element.309), channel_id=1, source_target_pairs={{0,2},{1,3},{2,0},{3,1},{4,6},{5,7},{6,4},{7,5},{8,10},{9,11},{10,... | collective-permute-start | bytes 786440 | tf_op jit(solution)/shard_map/ppermute | solution.py:983
  200.0 18.5 %collective-permute-start.57 = (bf16[128,1024]{1,0:T(8,128)(2,1)}, bf16[128,1024]{1,0:T(8,128)(2,1)}, u32[]{:S(2)}, u32[]{:S(2)}) collective-permute-start(bf16[128,1024]{1,0:T(8,128)(2,1)} %get-tuple-element.310), channel_id=1, source_target_pairs={{0,4},{1,5},{2,6},{3,7},{4,0},{5,1},{6,2},{7,3},{8,12},{9,13},{10,... | collective-permute-start | bytes 786440 | tf_op jit(solution)/shard_map/ppermute | solution.py:983
  218.5 28.9 %all-to-all-start.2 = ((bf16[4,704,256]{2,1,0:T(8,128)(2,1)}), bf16[4,704,256]{2,1,0:T(8,128)(2,1)S(1)}, u32[]{:S(2)}, u32[]{:S(2)}) async-start(bf16[4,704,256]{2,1,0:T(8,128)(2,1)} %self_grad.1), calls=%async_computation.2 | async-start | bytes 2883584 | tf_op jit(solution)/shard_map/all_to_all | solution.py:705
  228.3 5.0 %collective-permute-start.58 = (bf16[384,256]{1,0:T(8,128)(2,1)S(1)}, bf16[384,256]{1,0:T(8,128)(2,1)S(1)}, u32[]{:S(2)}, u32[]{:S(2)}) collective-permute-start(bf16[384,256]{1,0:T(8,128)(2,1)S(1)} %get-tuple-element.350), channel_id=1, source_target_pairs={{0,2},{1,3},{2,0},{3,1},{4,6},{5,7},{6,4},{7,5},{8,10},{9,11},{10,... | collective-permute-start | bytes 589832 | tf_op jit(solution)/shard_map/ppermute | solution.py:1011
  229.1 8.4 %collective-permute-start.59 = (bf16[384,256]{1,0:T(8,128)(2,1)S(1)}, bf16[384,256]{1,0:T(8,128)(2,1)S(1)}, u32[]{:S(2)}, u32[]{:S(2)}) collective-permute-start(bf16[384,256]{1,0:T(8,128)(2,1)S(1)} %get-tuple-element.349), channel_id=1, source_target_pairs={{0,4},{1,5},{2,6},{3,7},{4,0},{5,1},{6,2},{7,3},{8,12},{9,13},{10,... | collective-permute-start | bytes 589832 | tf_op jit(solution)/shard_map/ppermute | solution.py:1011
  230.1 17.4 %collective-permute-start.60 = (bf16[384,256]{1,0:T(8,128)(2,1)S(1)}, bf16[384,256]{1,0:T(8,128)(2,1)S(1)}, u32[]{:S(2)}, u32[]{:S(2)}) collective-permute-start(bf16[384,256]{1,0:T(8,128)(2,1)S(1)} %get-tuple-element.348), channel_id=1, source_target_pairs={{0,6},{1,7},{2,4},{3,5},{4,2},{5,3},{6,0},{7,1},{8,14},{9,15},{10,... | collective-permute-start | bytes 589832 | tf_op jit(solution)/shard_map/ppermute | solution.py:1011
  249.6 34.4 %all-to-all-start.3 = ((bf16[4,1024,256]{2,1,0:T(8,128)(2,1)}), bf16[4,1024,256]{2,1,0:T(8,128)(2,1)S(1)}, u32[]{:S(2)}, u32[]{:S(2)}) async-start(bf16[4,1024,256]{2,1,0:T(8,128)(2,1)} %broadcast_in_dim.23), calls=%async_computation.3 | async-start | bytes 4194304 | tf_op jit(solution)/shard_map/all_to_all | solution.py:690
  253.6 3.4 %collective-permute-start.61 = (bf16[80,512]{1,0:T(8,128)(2,1)S(1)}, bf16[80,512]{1,0:T(8,128)(2,1)S(1)}, u32[]{:S(2)}, u32[]{:S(2)}) collective-permute-start(bf16[80,512]{1,0:T(8,128)(2,1)S(1)} %constant_dynamic-slice_fusion), channel_id=1, source_target_pairs={{0,1},{1,0},{2,3},{3,2},{4,5},{5,4},{6,7},{7,6},{8,9},{9,8},{10,11... | collective-permute-start | bytes 245768 | tf_op jit(solution)/shard_map/ppermute | solution.py:1040
  256.1 16.7 %collective-permute-start.65 = (bf16[128,1024]{1,0:T(8,128)(2,1)S(1)}, bf16[128,1024]{1,0:T(8,128)(2,1)S(1)}, u32[]{:S(2)}, u32[]{:S(2)}) collective-permute-start(bf16[128,1024]{1,0:T(8,128)(2,1)S(1)} %copy-done.40), channel_id=1, source_target_pairs={{0,6},{1,7},{2,4},{3,5},{4,2},{5,3},{6,0},{7,1},{8,14},{9,15},{10,... | collective-permute-start | bytes 786440 | tf_op jit(solution)/shard_map/ppermute | solution.py:1016
  257.1 20.8 %collective-permute-start.62 = (bf16[80,512]{1,0:T(8,128)(2,1)S(1)}, bf16[80,512]{1,0:T(8,128)(2,1)S(1)}, u32[]{:S(2)}, u32[]{:S(2)}) collective-permute-start(bf16[80,512]{1,0:T(8,128)(2,1)S(1)} %add_convert_fusion.8), channel_id=1, source_target_pairs={{0,2},{1,3},{2,0},{3,1},{4,6},{5,7},{6,4},{7,5},{8,10},{9,11},{10,... | collective-permute-start | bytes 245768 | tf_op jit(solution)/shard_map/ppermute | solution.py:1041
  257.1 20.7 %collective-permute-start.63 = (bf16[80,512]{1,0:T(8,128)(2,1)S(1)}, bf16[80,512]{1,0:T(8,128)(2,1)S(1)}, u32[]{:S(2)}, u32[]{:S(2)}) collective-permute-start(bf16[80,512]{1,0:T(8,128)(2,1)S(1)} %add_convert_fusion.8), channel_id=1, source_target_pairs={{0,4},{1,5},{2,6},{3,7},{4,0},{5,1},{6,2},{7,3},{8,12},{9,13},{10,... | collective-permute-start | bytes 245768 | tf_op jit(solution)/shard_map/ppermute | solution.py:1041
  258.9 19.0 %collective-permute-start.64 = (bf16[80,512]{1,0:T(8,128)(2,1)S(1)}, bf16[80,512]{1,0:T(8,128)(2,1)S(1)}, u32[]{:S(2)}, u32[]{:S(2)}) collective-permute-start(bf16[80,512]{1,0:T(8,128)(2,1)S(1)} %add_convert_fusion.8), channel_id=1, source_target_pairs={{0,6},{1,7},{2,4},{3,5},{4,2},{5,3},{6,0},{7,1},{8,14},{9,15},{10,... | collective-permute-start | bytes 245768 | tf_op jit(solution)/shard_map/ppermute | solution.py:1041
  (61 other events, 504.1 us)

commit v3 on v2

--- a/solution.py
+++ b/solution.py
@@ -1010,8 +1010,22 @@
     row_piece = sum_dp(row_swap).reshape(chips, 3 * width, cut)
     row_parts = [row_piece[0]] + [to_z[k](row_piece[k]) for k in far]
     block_output = (second + total(*mlp_parts) + output_bias.astype(F32)).astype(BF16)
-    row_parts, self_swap, sent, block_output = lax.optimization_barrier(
-        (row_parts, self_swap, sent, block_output)
+    def place(pieces, plan, shapes, name, **kept):
+        return call(
+            functools.partial(place_kernel, plan),
+            [(s, F32) for s in shapes],
+            idx,
+            *pieces,
+            stage=True,
+            name=name,
+            **kept,
+        )
+
+    grad_output_weight, grad_hidden_weight = place(
+        mlp_all, ((hid, None, False), (hid, None, True)), ((hid, dim), (dim, hid)), "place_mlp"
+    )
+    row_parts, self_swap, sent, block_output, grad_output_weight = lax.optimization_barrier(
+        (row_parts, self_swap, sent, block_output, grad_output_weight)
     )
     parts += [to_z[k](sent[k]) for k in far[2:]]
     row_piece = total(*row_parts).astype(BF16)
@@ -1039,20 +1053,6 @@
     half_of = lambda c: lax.dynamic_slice_in_dim(state_part, c * (dim // 2), dim // 2, 1)
     state_half = total(half_of(core), to_core(half_of(1 - core))).astype(BF16)
     state_got = [to_z[k](state_half) for k in far]
-    def place(pieces, plan, shapes, name, **kept):
-        return call(
-            functools.partial(place_kernel, plan),
-            [(s, F32) for s in shapes],
-            idx,
-            *pieces,
-            stage=True,
-            name=name,
-            **kept,
-        )
-
-    grad_output_weight, grad_hidden_weight = place(
-        mlp_all, ((hid, None, False), (hid, None, True)), ((hid, dim), (dim, hid)), "place_mlp"
-    )
     state_got, block_output, grad_output_weight, grad_tokens = lax.optimization_barrier(
         (state_got, block_output, grad_output_weight, grad_tokens)
     )

time: 289 us -> 289 us (level)
    ppermute x3, waiting for transfers between devices: 16.1 us -> 11.4 us  [body(): row_parts = [row_piece[0]] + [to_z[k](row_piece[k]) for k in far]]
    ppermute x1, waiting for transfers between devices: 8.36 us -> 13 us  [body(): parts += [to_z[k](sent[k]) for k in far[2:]]]
  transfers between devices with their start and end apart: 71 -> 71, of which waited for: 22 -> 21; matrix products, arithmetic and copies ran while one was open for 8% -> 8% of each run, Pallas kernels for 34% -> 34%
where the time goes in v3:
time: 289 us; the launch traced here: 287 us
  Pallas kernels  112 us (39%)
  starting transfers between devices  88.9 us (31%)
  waiting for transfers between devices  53.6 us (19%)
  local copies, waits for them, and re-layouts  14.6 us (5%)
  other arithmetic  14.5 us (5%)
  between operations  3.65 us (1%)
    pallas_call x19, Pallas kernels, call(): pl.pallas_call(kernel, out_shape=out_shape, in_specs=[pl.BlockSpec(memory...  112 us
    all_to_all x3, starting transfers between devices, swap_dp(): return lax.all_to_all(pieces, 'dp', 0, 0)  16 us
    ppermute x1, waiting for transfers between devices, body(): parts += [to_z[k](sent[k]) for k in far[2:]]  13 us
    ppermute x3, waiting for transfers between devices, body(): row_parts = [row_piece[0]] + [to_z[k](row_piece[k]) for k in far]  11.4 us
    ppermute x4, starting transfers between devices, body(): att2 = [to_core(x) for x in att]  9.27 us
    ppermute x1, waiting for transfers between devices, body(): mlp_all += [to_dp[q](mlp_all[0]) for q in range(3, dps)]  7.76 us
    ppermute x1, starting transfers between devices, body(): n3s[2] = to_z[1](n3s[3])  6.97 us
    unnamed x110, local copies, waits for them, and re-layouts  6.71 us
  transfers between devices with their start and end apart: 71, of which 21 were waited for; matrix products, arithmetic and copies ran while one was open for 8% of the time, Pallas kernels for 34%

profile of v3, /device:TPU:11, one launch (start us, length us, event | category | flops | bytes accessed | tf_op | source)
XLA Modules:
  0.0 287.2 jit_solution(9480609605440763923)
XLA Ops:
  3.9 2.3 collective-permute-start.1
  8.3 13.3 %self_fwd.1 = (bf16[1024,1024]{1,0:T(8,128)(2,1)}, bf16[3,1024,128]{2,1,0:T(8,128)(2,1)}, bf16[2,1024,1024]{2,1,0:T(8,128)(2,1)}, bf16[384,128]{1,0:T(8,128)(2,1...) custom-call(s32[4]{0:T(128)} %pad_add_fusion.refs_0_.idx, ...), custom_call_target="tpu_custom_call" | custom-call | flops 1 | bytes 1 | tf_op jit(solution)/shard_map/self_fwd/pallas_call | solution.py:111
  21.6 2.1 collective-permute-done.2.refs_2_
  24.7 1.2 collective-permute-start.5
  25.9 1.2 collective-permute-start.6
  27.1 2.5 collective-permute-start.13
  29.5 1.6 collective-permute-done.12.refs_16_.refs_21_
  31.1 1.3 collective-permute-start.14
  33.0 4.2 %collective-permute-start.7 = (bf16[384,1024]{1,0:T(8,128)(2,1)S(1)}, bf16[384,1024]{1,0:T(8,128)(2,1)}, u32[]{:S(2)}, u32[]{:S(2)}) collective-permute-start(bf16[384,1024]{1,0:T(8,128)(2,1)S(1)} %pad_maximum_fusion.refs_5_.refs_7_), channel_id=1, source_target_pairs={{0,1},{1,0},{2,3},{3,2},{4,5},{5,4},{6,7},{7,6},{8,9},{9,8},{10,11... | collective-permute-start | bytes 2359304 | tf_op jit(solution)/shard_map/ppermute | solution.py:767
  37.2 6.0 %grad_active.1 = (f32[256,512]{1,0:T(8,128)}, f32[256,512]{1,0:T(8,128)}, f32[256,512]{1,0:T(8,128)}, f32[256,512]{1,0:T(8,128)}) custom-call(s32[4]{0:T(128)} %pad_add_fusion.refs_0_.idx, bf16[1024,1024]{1,0:T(8,128)(2,1)} %refs_1_.13, bf16[512,1024]{1,0:T(8,128)(2,1)} %refs_1_.12), custom_call_target="tpu_custom_call" | custom-call | flops 1 | bytes 1 | tf_op jit(solution)/shard_map/grad_active/pallas_call | solution.py:111
  45.1 7.0 %collective-permute-start.17 = (bf16[384,128]{1,0:T(8,128)(2,1)}, bf16[384,128]{1,0:T(8,128)(2,1)}, u32[]{:S(2)}, u32[]{:S(2)}) collective-permute-start(bf16[384,128]{1,0:T(8,128)(2,1)} %collective-permute-done.13.refs_17_.refs_22_), channel_id=1, source_target_pairs={{0,1},{1,0},{2,3},{3,2},{4,5},{5,4},{6,7},{7,6},{8,9},{9,8},{10,11... | collective-permute-start | bytes 294920 | tf_op jit(solution)/shard_map/ppermute | solution.py:751
  52.1 1.7 collective-permute-start.18
  55.7 1.2 collective-permute-done.10.refs_13_.refs_15_
  59.5 10.6 %cross_fwd.1 = (f32[128,1024]{1,0:T(8,128)}, bf16[3,128,1024]{2,1,0:T(8,128)(2,1)}, bf16[128,1024]{1,0:T(8,128)(2,1)}, bf16[8,128,128]{2,1,0:T(8,128)(2,1)}, f32...) custom-call(s32[4]{0:T(128)} %pad_add_fusion.refs_0_.idx, bf16[1024,1024]{1,0:T(8,128)(2,1)} %refs_1_.15, ...), custom_call_target="tpu_custom_call" | custom-call | flops 1 | bytes 1 | tf_op jit(solution)/shard_map/cross_fwd/pallas_call | solution.py:111
  70.3 1.4 collective-permute-start.22
  72.9 2.1 hidden.4
  75.0 3.0 %collective-permute-done.21.same = bf16[128,1024]{1,0:T(8,128)(2,1)S(1)} collective-permute-done((bf16[128,1024]{1,0:T(8,128)(2,1)}, bf16[128,1024]{1,0:T(8,128)(2,1)S(1)}, u32[]{:S(2)}, u32[]{:S(2)}) %collective-permute-start.21) | collective-permute-done | bytes 262176 | tf_op jit(solution)/shard_map/ppermute | solution.py:801
  78.1 2.0 collective-permute-start.23
  80.6 7.0 %collective-permute-start.27 = (bf16[128,1024]{1,0:T(8,128)(2,1)S(1)}, bf16[128,1024]{1,0:T(8,128)(2,1)S(1)}, u32[]{:S(2)}, u32[]{:S(2)}) collective-permute-start(bf16[128,1024]{1,0:T(8,128)(2,1)S(1)} %collective-permute-done.22.same), channel_id=1, source_target_pairs={{0,2},{1,3},{2,0},{3,1},{4,6},{5,7},{6,4},{7,5},{8,10},{9,11},{10,... | collective-permute-start | bytes 786440 | tf_op jit(solution)/shard_map/ppermute | solution.py:842
  87.6 2.1 hidden.5
  89.7 2.2 hidden.6
  92.3 2.0 collective-permute-done.27.same
  96.0 2.9 hidden.7
  100.2 1.5 collective-permute-start.29
  102.5 8.4 %mlp_grad.1 = bf16[4,1040,256]{2,1,0:T(8,128)(2,1)} custom-call(s32[4]{0:T(128)} %pad_add_fusion.refs_0_.idx, bf16[1024,1024]{1,0:T(8,128)(2,1)} %refs_1_.13, bf16[256,512]{1,0:T(8,128)(2,1)} %get-tuple-element.209.refs_2_.refs_3_, bf16[256,512]{1,0:T(8,128)(2,1)} %get-tuple-element.215.refs_3_.refs_4_, bf16[256,512]{1,0:T(8,128)(2,1)} %get-tuple-element.225.refs_4_.refs_5_, ...), custom_call_target="tpu_custom_call" | custom-call | flops 999999995904 | bytes 1 | tf_op jit(solution)/shard_map/mlp_grad/pallas_call | solution.py:111
  111.0 1.2 add_convert_fusion.1
  112.1 1.5 collective-permute-start.32
  114.6 5.3 %all-to-all-start = ((bf16[4,1040,256]{2,1,0:T(8,128)(2,1)}), bf16[4,1040,256]{2,1,0:T(8,128)(2,1)}, u32[]{:S(2)}, u32[]{:S(2)}) async-start(bf16[4,1040,256]{2,1,0:T(8,128)(2,1)} %mlp_grad.1), calls=%async_computation | async-start | bytes 4259840 | tf_op jit(solution)/shard_map/all_to_all | solution.py:705
  119.9 6.4 %mlp_out.1 = (bf16[128,1024]{1,0:T(8,128)(2,1)}, bf16[128,1024]{1,0:T(8,128)(2,1)}, bf16[128,1024]{1,0:T(8,128)(2,1)}, bf16[128,1024]{1,0:T(8,128)(2,1)}) custom-call(s32[4]{0:T(128)} %pad_add_fusion.refs_0_.idx, bf16[512,1024]{1,0:T(8,128)(2,1)} %refs_1_.12, bf16[512,1024]{1,0:T(8,128)(2,1)} %copy-done.16, ...), custom_call_target="tpu_custom_call" | custom-call | flops 1 | bytes 1 | tf_op jit(solution)/shard_map/mlp_out/pallas_call | solution.py:111
  126.4 1.8 collective-permute-start.33
  128.8 12.5 %cross_bwd.1 = (bf16[3,128,1024]{2,1,0:T(8,128)(2,1)}, f32[128,1024]{1,0:T(8,128)}, f32[8,1024]{1,0:T(8,128)}, bf16[4,2,64,128]{3,2,1,0:T(8,128)(2,1)}, bf16[4,2...) custom-call(s32[4]{0:T(128)} %pad_add_fusion.refs_0_.idx, ...), custom_call_target="tpu_custom_call" | custom-call | flops 999999995904 | bytes 1 | tf_op jit(solution)/shard_map/cross_bwd/pallas_call | solution.py:111
  141.4 3.4 %all-to-all-done.refs_1_ = bf16[4,1040,256]{2,1,0:T(8,128)(2,1)} async-done(((bf16[4,1040,256]{2,1,0:T(8,128)(2,1)}), bf16[4,1040,256]{2,1,0:T(8,128)(2,1)}, u32[]{:S(2)}, u32[]{:S(2)}) %all-to-all-start) | async-done | bytes 2129952 | tf_op jit(solution)/shard_map/all_to_all | solution.py:705
  145.9 3.4 %sum_mlp.1.refs_1_ = bf16[1024,256]{1,0:T(8,128)(2,1)} custom-call(s32[4]{0:T(128)} %pad_add_fusion.refs_0_.idx, bf16[4,1040,256]{2,1,0:T(8,128)(2,1)} %all-to-all-done.refs_1_), custom_call_target="tpu_custom_call" | custom-call | flops 1 | bytes 1 | tf_op jit(solution)/shard_map/sum_mlp/pallas_call | solution.py:111
  149.7 1.2 collective-permute-start.41
  152.4 1.4 collective-permute-start.36
  154.7 5.4 %row_grad.1 = bf16[4,1536,256]{2,1,0:T(8,128)(2,1)} custom-call(s32[4]{0:T(128)} %pad_add_fusion.refs_0_.idx, bf16[3,128,1024]{2,1,0:T(8,128)(2,1)} %get-tuple-element.265.refs_1_, bf16[3,128,1024]{2,1,0:T(8,128)(2,1)} %collective-permute-done.38.refs_2_, bf16[3,128,1024]{2,1,0:T(8,128)(2,1)} %get-tuple-element.266.refs_3_, bf16[3,128,1024]{2,1,0:T(8,128)(2,1)} %copy-done.17), custom_call_target="tpu_custom_call" | custom-call | flops 1 | bytes 1 | tf_op jit(solution)/shard_map/row_grad/pallas_call | solution.py:111
  160.6 2.5 collective-permute-done.40.refs_2_
  163.1 1.1 collective-permute-start.42
  166.2 5.8 %all-to-all-start.1 = ((bf16[4,1536,256]{2,1,0:T(8,128)(2,1)}), bf16[4,1536,256]{2,1,0:T(8,128)(2,1)}, u32[]{:S(2)}, u32[]{:S(2)}) async-start(bf16[4,1536,256]{2,1,0:T(8,128)(2,1)} %row_grad.1), calls=%async_computation.1 | async-start | bytes 6291456 | tf_op jit(solution)/shard_map/all_to_all | solution.py:705
  172.1 1.6 collective-permute-start.53
  174.0 1.2 collective-permute-start.46
  175.8 12.1 %self_bwd.1 = (bf16[1024,384]{1,0:T(8,128)(2,1)}, bf16[128,1024]{1,0:T(8,128)(2,1)}, bf16[128,1024]{1,0:T(8,128)(2,1)}, bf16[128,1024]{1,0:T(8,128)(2,1)}, bf16[...) custom-call(s32[4]{0:T(128)} %pad_add_fusion.refs_0_.idx, ...), custom_call_target="tpu_custom_call" | custom-call | flops 999999995904 | bytes 1 | tf_op jit(solution)/shard_map/self_bwd/pallas_call | solution.py:111
  187.9 1.5 collective-permute-done.46
  191.1 1.2 collective-permute-start.55
  192.3 1.4 fusion.3.refs_5_
  195.3 3.5 %self_add.1 = (bf16[128,1024]{1,0:T(8,128)(2,1)}, bf16[128,1024]{1,0:T(8,128)(2,1)}, bf16[128,1024]{1,0:T(8,128)(2,1)}, bf16[128,1024]{1,0:T(8,128)(2,1)}) custom-call(s32[4]{0:T(128)} %pad_add_fusion.refs_0_.idx, bf16[128,1024]{1,0:T(8,128)(2,1)} %get-tuple-element.293.refs_1_.refs_7_, bf16[128,1024]{1,0:T(8,128)(2,1)} %get-tuple-element.294.refs_2_.refs_8_, ...), custom_call_target="tpu_custom_call" | custom-call | flops 1 | bytes 1 | tf_op jit(solution)/shard_map/self_add/pallas_call | solution.py:111
  198.7 1.2 collective-permute-start.56
  200.8 1.6 dynamic-slice_bitcast_fusion.refs_4_
  202.4 8.3 %self_grad.1 = bf16[4,704,256]{2,1,0:T(8,128)(2,1)} custom-call(s32[4]{0:T(128)} %pad_add_fusion.refs_0_.idx, bf16[1024,1024]{1,0:T(8,128)(2,1)} %refs_1_.15, bf16[1024,1024]{1,0:T(8,128)(2,1)} %get-tuple-element.303.refs_2_, bf16[1024,384]{1,0:T(8,128)(2,1)} %get-tuple-element.304.refs_3_, bf16[64,1024]{1,0:T(8,128)(2,1)} %dynamic-slice_bitcast_fusion.refs_4_, ...), custom_call_target="tpu_custom_call" | custom-call | flops 1 | bytes 1 | tf_op jit(solution)/shard_map/self_grad/pallas_call | solution.py:111
  210.7 7.8 %collective-permute-done.55.refs_4_ = bf16[1024,256]{1,0:T(8,128)(2,1)S(1)} collective-permute-done((bf16[1024,256]{1,0:T(8,128)(2,1)S(1)}, bf16[1024,256]{1,0:T(8,128)(2,1)S(1)}, u32[]{:S(2)}, u32[]{:S(2)}) %collective-permute-start.55) | collective-permute-done | bytes 524320 | tf_op jit(solution)/shard_map/ppermute | solution.py:947
  218.5 4.8 %all-to-all-start.2 = ((bf16[4,704,256]{2,1,0:T(8,128)(2,1)}), bf16[4,704,256]{2,1,0:T(8,128)(2,1)S(1)}, u32[]{:S(2)}, u32[]{:S(2)}) async-start(bf16[4,704,256]{2,1,0:T(8,128)(2,1)} %self_grad.1), calls=%async_computation.2 | async-start | bytes 2883584 | tf_op jit(solution)/shard_map/all_to_all | solution.py:705
  223.3 2.0 add_convert_fusion
  225.3 2.9 %reduce_sum.43 = bf16[1536,256]{1,0:T(8,128)(2,1)S(1)} reduce(bf16[4,1536,256]{2,1,0:T(8,128)(2,1)} %all-to-all-done.1, bf16[]{:T(256)} %constant.45.clone.1), dimensions={0}, to_apply=%region_1.2 | reduce | flops 1179648 | bytes 3932162 | tf_op jit(solution)/shard_map/reduce_sum | solution.py:708
  231.3 4.7 %place_mlp.1 = (f32[512,1024]{1,0:T(8,128)}, f32[1024,512]{1,0:T(8,128)}) custom-call(s32[4]{0:T(128)} %pad_add_fusion.refs_0_.idx, bf16[1024,256]{1,0:T(8,128)(2,1)} %sum_mlp.1.refs_1_, bf16[1024,256]{1,0:T(8,128)(2,1)} %copy-done.23, bf16[1024,256]{1,0:T(8,128)(2,1)} %copy-done.24, bf16[1024,256]{1,0:T(8,128)(2,1)} %copy-done.25), custom_call_target="tpu_custom_call" | custom-call | flops 1 | bytes 1 | tf_op jit(solution)/shard_map/place_mlp/pallas_call | solution.py:111
  236.0 1.4 collective-permute-done.59
  237.4 10.0 %collective-permute-done.60 = bf16[384,256]{1,0:T(8,128)(2,1)S(1)} collective-permute-done((bf16[384,256]{1,0:T(8,128)(2,1)S(1)}, bf16[384,256]{1,0:T(8,128)(2,1)S(1)}, u32[]{:S(2)}, u32[]{:S(2)}) %collective-permute-start.60) | collective-permute-done | bytes 196640 | tf_op jit(solution)/shard_map/ppermute | solution.py:1011
  248.0 1.5 broadcast_in_dim.23
  249.6 4.0 %all-to-all-start.3 = ((bf16[4,1024,256]{2,1,0:T(8,128)(2,1)}), bf16[4,1024,256]{2,1,0:T(8,128)(2,1)S(1)}, u32[]{:S(2)}, u32[]{:S(2)}) async-start(bf16[4,1024,256]{2,1,0:T(8,128)(2,1)} %broadcast_in_dim.23), calls=%async_computation.3 | async-start | bytes 4194304 | tf_op jit(solution)/shard_map/all_to_all | solution.py:690
  253.6 2.5 collective-permute-start.61
  257.1 1.7 collective-permute-start.63
  259.8 13.0 %collective-permute-done.65.refs_7_ = bf16[128,1024]{1,0:T(8,128)(2,1)S(1)} collective-permute-done((bf16[128,1024]{1,0:T(8,128)(2,1)S(1)}, bf16[128,1024]{1,0:T(8,128)(2,1)S(1)}, u32[]{:S(2)}, u32[]{:S(2)}) %collective-permute-start.65) | collective-permute-done | bytes 262176 | tf_op jit(solution)/shard_map/ppermute | solution.py:1030
  273.5 4.3 %tokens.1 = f32[128,1024]{1,0:T(8,128)} custom-call(s32[4]{0:T(128)} %pad_add_fusion.refs_0_.idx, bf16[1024,1024]{1,0:T(8,128)(2,1)} %refs_1_.15, bf16[3,1024]{1,0:T(4,128)(2,1)} %refs_2_.9, f32[128,1024]{1,0:T(8,128)} %get-tuple-element.327.refs_3_, bf16[128,1024]{1,0:T(8,128)(2,1)} %get-tuple-element.301.refs_4_, bf16[128,1024]{1,0:T(8,128)(2,1)} %copy-done.29, ...), custom_call_target="tpu_custom_call" | custom-call | flops 1 | bytes 1 | tf_op jit(solution)/shard_map/tokens/pallas_call | solution.py:111
  281.0 1.7 dynamic_update_slice.11
  284.0 3.0 %place.1 = (f32[128,1024]{1,0:T(8,128)}, f32[1024,128]{1,0:T(8,128)}, f32[128,1024]{1,0:T(8,128)}, f32[3,1024,128]{2,1,0:T(8,128)}, f32[2,1024,128]{2,1,0:T(8,128)}) custom-call(s32[4]{0:T(128)S(1)} %copy-done.9, bf16[4,1024,256]{2,1,0:T(8,128)(2,1)S(1)} %all-to-all-done.3.refs_1_), custom_call_target="tpu_custom_call" | custom-call | flops 1 | bytes 1 | tf_op jit(solution)/shard_map/place/pallas_call | solution.py:111
  (246 shorter events, 41.1 us)
Async XLA Ops:
  0.6 23.1 %collective-permute-start.3 = (bf16[512,1024]{1,0:T(8,128)(2,1)}, bf16[512,1024]{1,0:T(8,128)(2,1)S(1)}, u32[]{:S(2)}, u32[]{:S(2)}) collective-permute-start(bf16[512,1024]{1,0:T(8,128)(2,1)} %refs_1_.12), channel_id=1, source_target_pairs={{0,1},{1,0},{2,3},{3,2},{4,5},{5,4},{6,7},{7,6},{8,9},{9,8},{10,11... | collective-permute-start | bytes 3145736 | tf_op jit(solution)/shard_map/ppermute | solution.py:719
  3.6 17.9 %collective-permute-start = (bf16[384,256]{1,0:T(8,128)(2,1)S(1)}, bf16[384,256]{1,0:T(8,128)(2,1)S(1)}, u32[]{:S(2)}, u32[]{:S(2)}) collective-permute-start(bf16[384,256]{1,0:T(8,128)(2,1)S(1)} %constant_dynamic-slice_fusion.2), channel_id=1, source_target_pairs={{0,2},{1,3},{2,0},{3,1},{4,6},{5,7},{6,4},{7,5},{8,10},{9,11},{10,... | collective-permute-start | bytes 589832 | tf_op jit(solution)/shard_map/ppermute | solution.py:718
  3.9 17.7 %collective-permute-start.1 = (bf16[384,256]{1,0:T(8,128)(2,1)S(1)}, bf16[384,256]{1,0:T(8,128)(2,1)S(1)}, u32[]{:S(2)}, u32[]{:S(2)}) collective-permute-start(bf16[384,256]{1,0:T(8,128)(2,1)S(1)} %constant_dynamic-slice_fusion.2), channel_id=1, source_target_pairs={{0,4},{1,5},{2,6},{3,7},{4,0},{5,1},{6,2},{7,3},{8,12},{9,13},{10,... | collective-permute-start | bytes 589832 | tf_op jit(solution)/shard_map/ppermute | solution.py:718
  6.2 17.6 %collective-permute-start.2 = (bf16[384,256]{1,0:T(8,128)(2,1)S(1)}, bf16[384,256]{1,0:T(8,128)(2,1)S(1)}, u32[]{:S(2)}, u32[]{:S(2)}) collective-permute-start(bf16[384,256]{1,0:T(8,128)(2,1)S(1)} %constant_dynamic-slice_fusion.2), channel_id=1, source_target_pairs={{0,6},{1,7},{2,4},{3,5},{4,2},{5,3},{6,0},{7,1},{8,14},{9,15},{10,... | collective-permute-start | bytes 589832 | tf_op jit(solution)/shard_map/ppermute | solution.py:718
  24.3 20.3 %collective-permute-start.4 = (bf16[1152,256]{1,0:T(8,128)(2,1)S(1)}, bf16[1152,256]{1,0:T(8,128)(2,1)S(1)}, u32[]{:S(2)}, u32[]{:S(2)}) collective-permute-start(bf16[1152,256]{1,0:T(8,128)(2,1)S(1)} %pack.1.refs_6_.refs_8_), channel_id=1, source_target_pairs={{0,8},{8,0},{16,24},{24,16},{1,9},{9,1},{17,25},{25,17},{2,10},{10... | collective-permute-start | bytes 1769480 | tf_op jit(solution)/shard_map/ppermute | solution.py:765
  24.7 20.5 %collective-permute-start.5 = (bf16[1152,256]{1,0:T(8,128)(2,1)S(1)}, bf16[1152,256]{1,0:T(8,128)(2,1)}, u32[]{:S(2)}, u32[]{:S(2)}) collective-permute-start(bf16[1152,256]{1,0:T(8,128)(2,1)S(1)} %pack.1.refs_6_.refs_8_), channel_id=1, source_target_pairs={{0,16},{8,24},{16,0},{24,8},{1,17},{9,25},{17,1},{25,9},{2,18},{10... | collective-permute-start | bytes 1769480 | tf_op jit(solution)/shard_map/ppermute | solution.py:765
  25.9 26.2 %collective-permute-start.6 = (bf16[1152,256]{1,0:T(8,128)(2,1)S(1)}, bf16[1152,256]{1,0:T(8,128)(2,1)}, u32[]{:S(2)}, u32[]{:S(2)}) collective-permute-start(bf16[1152,256]{1,0:T(8,128)(2,1)S(1)} %pack.1.refs_6_.refs_8_), channel_id=1, source_target_pairs={{0,24},{8,16},{16,8},{24,0},{1,25},{9,17},{17,9},{25,1},{2,26},{10... | collective-permute-start | bytes 1769480 | tf_op jit(solution)/shard_map/ppermute | solution.py:765
  27.1 4.1 %collective-permute-start.12 = (bf16[384,128]{1,0:T(8,128)(2,1)}, bf16[384,128]{1,0:T(8,128)(2,1)}, u32[]{:S(2)}, u32[]{:S(2)}) collective-permute-start(bf16[384,128]{1,0:T(8,128)(2,1)} %get-tuple-element.198), channel_id=1, source_target_pairs={{0,2},{1,3},{2,0},{3,1},{4,6},{5,7},{6,4},{7,5},{8,10},{9,11},{10,... | collective-permute-start | bytes 294920 | tf_op jit(solution)/shard_map/ppermute | solution.py:750
  27.1 5.9 %collective-permute-start.13 = (bf16[384,128]{1,0:T(8,128)(2,1)}, bf16[384,128]{1,0:T(8,128)(2,1)}, u32[]{:S(2)}, u32[]{:S(2)}) collective-permute-start(bf16[384,128]{1,0:T(8,128)(2,1)} %get-tuple-element.199), channel_id=1, source_target_pairs={{0,4},{1,5},{2,6},{3,7},{4,0},{5,1},{6,2},{7,3},{8,12},{9,13},{10,... | collective-permute-start | bytes 294920 | tf_op jit(solution)/shard_map/ppermute | solution.py:750
  31.1 13.4 %collective-permute-start.14 = (bf16[384,128]{1,0:T(8,128)(2,1)}, bf16[384,128]{1,0:T(8,128)(2,1)}, u32[]{:S(2)}, u32[]{:S(2)}) collective-permute-start(bf16[384,128]{1,0:T(8,128)(2,1)} %get-tuple-element.200), channel_id=1, source_target_pairs={{0,6},{1,7},{2,4},{3,5},{4,2},{5,3},{6,0},{7,1},{8,14},{9,15},{10,... | collective-permute-start | bytes 294920 | tf_op jit(solution)/shard_map/ppermute | solution.py:750
  33.0 22.7 %collective-permute-start.7 = (bf16[384,1024]{1,0:T(8,128)(2,1)S(1)}, bf16[384,1024]{1,0:T(8,128)(2,1)}, u32[]{:S(2)}, u32[]{:S(2)}) collective-permute-start(bf16[384,1024]{1,0:T(8,128)(2,1)S(1)} %pad_maximum_fusion.refs_5_.refs_7_), channel_id=1, source_target_pairs={{0,1},{1,0},{2,3},{3,2},{4,5},{5,4},{6,7},{7,6},{8,9},{9,8},{10,11... | collective-permute-start | bytes 2359304 | tf_op jit(solution)/shard_map/ppermute | solution.py:767
  44.6 10.0 %collective-permute-start.15 = (bf16[384,128]{1,0:T(8,128)(2,1)S(1)}, bf16[384,128]{1,0:T(8,128)(2,1)}, u32[]{:S(2)}, u32[]{:S(2)}) collective-permute-start(bf16[384,128]{1,0:T(8,128)(2,1)S(1)} %copy-done.36), channel_id=1, source_target_pairs={{0,1},{1,0},{2,3},{3,2},{4,5},{5,4},{6,7},{7,6},{8,9},{9,8},{10,11... | collective-permute-start | bytes 294920 | tf_op jit(solution)/shard_map/ppermute | solution.py:751
  44.7 10.0 %collective-permute-start.16 = (bf16[384,128]{1,0:T(8,128)(2,1)}, bf16[384,128]{1,0:T(8,128)(2,1)}, u32[]{:S(2)}, u32[]{:S(2)}) collective-permute-start(bf16[384,128]{1,0:T(8,128)(2,1)} %collective-permute-done.12.refs_16_.refs_21_), channel_id=1, source_target_pairs={{0,1},{1,0},{2,3},{3,2},{4,5},{5,4},{6,7},{7,6},{8,9},{9,8},{10,11... | collective-permute-start | bytes 294920 | tf_op jit(solution)/shard_map/ppermute | solution.py:751
  45.1 10.0 %collective-permute-start.17 = (bf16[384,128]{1,0:T(8,128)(2,1)}, bf16[384,128]{1,0:T(8,128)(2,1)}, u32[]{:S(2)}, u32[]{:S(2)}) collective-permute-start(bf16[384,128]{1,0:T(8,128)(2,1)} %collective-permute-done.13.refs_17_.refs_22_), channel_id=1, source_target_pairs={{0,1},{1,0},{2,3},{3,2},{4,5},{5,4},{6,7},{7,6},{8,9},{9,8},{10,11... | collective-permute-start | bytes 294920 | tf_op jit(solution)/shard_map/ppermute | solution.py:751
  52.1 3.1 %collective-permute-start.18 = (bf16[384,128]{1,0:T(8,128)(2,1)}, bf16[384,128]{1,0:T(8,128)(2,1)}, u32[]{:S(2)}, u32[]{:S(2)}) collective-permute-start(bf16[384,128]{1,0:T(8,128)(2,1)} %collective-permute-done.14.refs_18_.refs_23_), channel_id=1, source_target_pairs={{0,1},{1,0},{2,3},{3,2},{4,5},{5,4},{6,7},{7,6},{8,9},{9,8},{10,11... | collective-permute-start | bytes 294920 | tf_op jit(solution)/shard_map/ppermute | solution.py:751
  55.1 3.4 %collective-permute-start.8 = (bf16[1152,256]{1,0:T(8,128)(2,1)S(1)}, bf16[1152,256]{1,0:T(8,128)(2,1)S(1)}, u32[]{:S(2)}, u32[]{:S(2)}) collective-permute-start(bf16[1152,256]{1,0:T(8,128)(2,1)S(1)} %pack.1.refs_6_.refs_8_), channel_id=1, source_target_pairs={{0,1},{1,0},{2,3},{3,2},{4,5},{5,4},{6,7},{7,6},{8,9},{9,8},{10,11... | collective-permute-start | bytes 1769480 | tf_op jit(solution)/shard_map/ppermute | solution.py:767
  55.2 4.3 %collective-permute-start.9 = (bf16[1152,256]{1,0:T(8,128)(2,1)}, bf16[1152,256]{1,0:T(8,128)(2,1)}, u32[]{:S(2)}, u32[]{:S(2)}) collective-permute-start(bf16[1152,256]{1,0:T(8,128)(2,1)} %copy-done.18), channel_id=1, source_target_pairs={{0,1},{1,0},{2,3},{3,2},{4,5},{5,4},{6,7},{7,6},{8,9},{9,8},{10,11... | collective-permute-start | bytes 1769480 | tf_op jit(solution)/shard_map/ppermute | solution.py:767
  70.3 7.7 %collective-permute-start.21 = (bf16[128,1024]{1,0:T(8,128)(2,1)}, bf16[128,1024]{1,0:T(8,128)(2,1)S(1)}, u32[]{:S(2)}, u32[]{:S(2)}) collective-permute-start(bf16[128,1024]{1,0:T(8,128)(2,1)} %get-tuple-element.205.same), channel_id=1, source_target_pairs={{0,2},{1,3},{2,0},{3,1},{4,6},{5,7},{6,4},{7,5},{8,10},{9,11},{10,... | collective-permute-start | bytes 786440 | tf_op jit(solution)/shard_map/ppermute | solution.py:801
  70.3 7.7 %collective-permute-start.22 = (bf16[128,1024]{1,0:T(8,128)(2,1)}, bf16[128,1024]{1,0:T(8,128)(2,1)S(1)}, u32[]{:S(2)}, u32[]{:S(2)}) collective-permute-start(bf16[128,1024]{1,0:T(8,128)(2,1)} %get-tuple-element.205.same), channel_id=1, source_target_pairs={{0,6},{1,7},{2,4},{3,5},{4,2},{5,3},{6,0},{7,1},{8,14},{9,15},{10,... | collective-permute-start | bytes 786440 | tf_op jit(solution)/shard_map/ppermute | solution.py:801
  78.1 9.5 %collective-permute-start.23 = (bf16[128,1024]{1,0:T(8,128)(2,1)S(1)}, bf16[128,1024]{1,0:T(8,128)(2,1)S(1)}, u32[]{:S(2)}, u32[]{:S(2)}) collective-permute-start(bf16[128,1024]{1,0:T(8,128)(2,1)S(1)} %collective-permute-done.21.same), channel_id=1, source_target_pairs={{0,1},{1,0},{2,3},{3,2},{4,5},{5,4},{6,7},{7,6},{8,9},{9,8},{10,11... | collective-permute-start | bytes 786440 | tf_op jit(solution)/shard_map/ppermute | solution.py:819
  80.1 9.6 %collective-permute-start.25 = (bf16[128,1024]{1,0:T(8,128)(2,1)S(1)}, bf16[128,1024]{1,0:T(8,128)(2,1)S(1)}, u32[]{:S(2)}, u32[]{:S(2)}) collective-permute-start(bf16[128,1024]{1,0:T(8,128)(2,1)S(1)} %collective-permute-done.22.same), channel_id=1, source_target_pairs={{0,1},{1,0},{2,3},{3,2},{4,5},{5,4},{6,7},{7,6},{8,9},{9,8},{10,11... | collective-permute-start | bytes 786440 | tf_op jit(solution)/shard_map/ppermute | solution.py:819
  80.1 14.7 %collective-permute-start.20 = (bf16[128,1536]{1,0:T(8,128)(2,1)S(1)}, bf16[128,1536]{1,0:T(8,128)(2,1)S(1)}, u32[]{:S(2)}, u32[]{:S(2)}) collective-permute-start(bf16[128,1536]{1,0:T(8,128)(2,1)S(1)} %get-tuple-element.208), channel_id=1, source_target_pairs={{0,1},{1,0},{2,3},{3,2},{4,5},{5,4},{6,7},{7,6},{8,9},{9,8},{10,11... | collective-permute-start | bytes 1179656 | tf_op jit(solution)/shard_map/ppermute | solution.py:837
  80.6 13.7 %collective-permute-start.27 = (bf16[128,1024]{1,0:T(8,128)(2,1)S(1)}, bf16[128,1024]{1,0:T(8,128)(2,1)S(1)}, u32[]{:S(2)}, u32[]{:S(2)}) collective-permute-start(bf16[128,1024]{1,0:T(8,128)(2,1)S(1)} %collective-permute-done.22.same), channel_id=1, source_target_pairs={{0,2},{1,3},{2,0},{3,1},{4,6},{5,7},{6,4},{7,5},{8,10},{9,11},{10,... | collective-permute-start | bytes 786440 | tf_op jit(solution)/shard_map/ppermute | solution.py:842
  91.9 7.4 %collective-permute-start.26 = (bf16[128,1536]{1,0:T(8,128)(2,1)S(1)}, bf16[128,1536]{1,0:T(8,128)(2,1)S(1)}, u32[]{:S(2)}, u32[]{:S(2)}) collective-permute-start(bf16[128,1536]{1,0:T(8,128)(2,1)S(1)} %get-tuple-element.220), channel_id=1, source_target_pairs={{0,1},{1,0},{2,3},{3,2},{4,5},{5,4},{6,7},{7,6},{8,9},{9,8},{10,11... | collective-permute-start | bytes 1179656 | tf_op jit(solution)/shard_map/ppermute | solution.py:837
  94.8 6.8 %collective-permute-start.24 = (bf16[128,1536]{1,0:T(8,128)(2,1)S(1)}, bf16[128,1536]{1,0:T(8,128)(2,1)S(1)}, u32[]{:S(2)}, u32[]{:S(2)}) collective-permute-start(bf16[128,1536]{1,0:T(8,128)(2,1)S(1)} %get-tuple-element.214), channel_id=1, source_target_pairs={{0,1},{1,0},{2,3},{3,2},{4,5},{5,4},{6,7},{7,6},{8,9},{9,8},{10,11... | collective-permute-start | bytes 1179656 | tf_op jit(solution)/shard_map/ppermute | solution.py:837
  98.9 12.1 %collective-permute-start.31 = (bf16[128,1536]{1,0:T(8,128)(2,1)}, bf16[128,1536]{1,0:T(8,128)(2,1)}, u32[]{:S(2)}, u32[]{:S(2)}) collective-permute-start(bf16[128,1536]{1,0:T(8,128)(2,1)} %get-tuple-element.237), channel_id=1, source_target_pairs={{0,1},{1,0},{2,3},{3,2},{4,5},{5,4},{6,7},{7,6},{8,9},{9,8},{10,11... | collective-permute-start | bytes 1179656 | tf_op jit(solution)/shard_map/ppermute | solution.py:837
  100.2 10.8 %collective-permute-start.29 = (bf16[128,1024]{1,0:T(8,128)(2,1)}, bf16[128,1024]{1,0:T(8,128)(2,1)}, u32[]{:S(2)}, u32[]{:S(2)}) collective-permute-start(bf16[128,1024]{1,0:T(8,128)(2,1)} %add_convert_fusion.3), channel_id=1, source_target_pairs={{0,2},{1,3},{2,0},{3,1},{4,6},{5,7},{6,4},{7,5},{8,10},{9,11},{10,... | collective-permute-start | bytes 786440 | tf_op jit(solution)/shard_map/ppermute | solution.py:845
  102.5 12.1 %collective-permute-start.30 = (bf16[128,1024]{1,0:T(8,128)(2,1)}, bf16[128,1024]{1,0:T(8,128)(2,1)}, u32[]{:S(2)}, u32[]{:S(2)}) collective-permute-start(bf16[128,1024]{1,0:T(8,128)(2,1)} %add_convert_fusion.4), channel_id=1, source_target_pairs={{0,2},{1,3},{2,0},{3,1},{4,6},{5,7},{6,4},{7,5},{8,10},{9,11},{10,... | collective-permute-start | bytes 786440 | tf_op jit(solution)/shard_map/ppermute | solution.py:843
  112.1 14.2 %collective-permute-start.32 = (bf16[128,1024]{1,0:T(8,128)(2,1)S(1)}, bf16[128,1024]{1,0:T(8,128)(2,1)S(1)}, u32[]{:S(2)}, u32[]{:S(2)}) collective-permute-start(bf16[128,1024]{1,0:T(8,128)(2,1)S(1)} %add_convert_fusion.1), channel_id=1, source_target_pairs={{0,4},{1,5},{2,6},{3,7},{4,0},{5,1},{6,2},{7,3},{8,12},{9,13},{10,... | collective-permute-start | bytes 786440 | tf_op jit(solution)/shard_map/ppermute | solution.py:866
  113.6 37.8 %collective-permute-start.38 = (bf16[3,128,1024]{2,1,0:T(8,128)(2,1)}, bf16[3,128,1024]{2,1,0:T(8,128)(2,1)}, u32[]{:S(2)}, u32[]{:S(2)}) collective-permute-start(bf16[3,128,1024]{2,1,0:T(8,128)(2,1)} %get-tuple-element.265.refs_1_), channel_id=1, source_target_pairs={{0,1},{1,0},{2,3},{3,2},{4,5},{5,4},{6,7},{7,6},{8,9},{9,8},{10,11... | collective-permute-start | bytes 2359304 | tf_op jit(solution)/shard_map/ppermute | solution.py:802
  114.6 30.2 %all-to-all-start = ((bf16[4,1040,256]{2,1,0:T(8,128)(2,1)}), bf16[4,1040,256]{2,1,0:T(8,128)(2,1)}, u32[]{:S(2)}, u32[]{:S(2)}) async-start(bf16[4,1040,256]{2,1,0:T(8,128)(2,1)} %mlp_grad.1), calls=%async_computation | async-start | bytes 4259840 | tf_op jit(solution)/shard_map/all_to_all | solution.py:705
  126.4 15.0 %collective-permute-start.33 = (bf16[128,1024]{1,0:T(8,128)(2,1)}, bf16[128,1024]{1,0:T(8,128)(2,1)}, u32[]{:S(2)}, u32[]{:S(2)}) collective-permute-start(bf16[128,1024]{1,0:T(8,128)(2,1)} %get-tuple-element.259), channel_id=1, source_target_pairs={{0,2},{1,3},{2,0},{3,1},{4,6},{5,7},{6,4},{7,5},{8,10},{9,11},{10,... | collective-permute-start | bytes 786440 | tf_op jit(solution)/shard_map/ppermute | solution.py:888
  128.1 13.2 %collective-permute-start.34 = (bf16[128,1024]{1,0:T(8,128)(2,1)}, bf16[128,1024]{1,0:T(8,128)(2,1)}, u32[]{:S(2)}, u32[]{:S(2)}) collective-permute-start(bf16[128,1024]{1,0:T(8,128)(2,1)} %get-tuple-element.260), channel_id=1, source_target_pairs={{0,4},{1,5},{2,6},{3,7},{4,0},{5,1},{6,2},{7,3},{8,12},{9,13},{10,... | collective-permute-start | bytes 786440 | tf_op jit(solution)/shard_map/ppermute | solution.py:888
  144.8 9.1 %collective-permute-start.39 = (bf16[3,128,1024]{2,1,0:T(8,128)(2,1)}, bf16[3,128,1024]{2,1,0:T(8,128)(2,1)S(1)}, u32[]{:S(2)}, u32[]{:S(2)}) collective-permute-start(bf16[3,128,1024]{2,1,0:T(8,128)(2,1)} %get-tuple-element.266.refs_3_), channel_id=1, source_target_pairs={{0,1},{1,0},{2,3},{3,2},{4,5},{5,4},{6,7},{7,6},{8,9},{9,8},{10,11... | collective-permute-start | bytes 2359304 | tf_op jit(solution)/shard_map/ppermute | solution.py:939
  149.3 13.8 %collective-permute-start.40 = (bf16[1024,256]{1,0:T(8,128)(2,1)}, bf16[1024,256]{1,0:T(8,128)(2,1)S(1)}, u32[]{:S(2)}, u32[]{:S(2)}) collective-permute-start(bf16[1024,256]{1,0:T(8,128)(2,1)} %sum_mlp.1.refs_1_), channel_id=1, source_target_pairs={{0,8},{8,0},{16,24},{24,16},{1,9},{9,1},{17,25},{25,17},{2,10},{10... | collective-permute-start | bytes 1572872 | tf_op jit(solution)/shard_map/ppermute | solution.py:927
  149.7 13.4 %collective-permute-start.41 = (bf16[1024,256]{1,0:T(8,128)(2,1)}, bf16[1024,256]{1,0:T(8,128)(2,1)S(1)}, u32[]{:S(2)}, u32[]{:S(2)}) collective-permute-start(bf16[1024,256]{1,0:T(8,128)(2,1)} %sum_mlp.1.refs_1_), channel_id=1, source_target_pairs={{0,16},{8,24},{16,0},{24,8},{1,17},{9,25},{17,1},{25,9},{2,18},{10... | collective-permute-start | bytes 1572872 | tf_op jit(solution)/shard_map/ppermute | solution.py:927
  151.5 8.7 %collective-permute-start.35 = (bf16[2,128,128]{2,1,0:T(8,128)(2,1)S(1)}, bf16[2,128,128]{2,1,0:T(8,128)(2,1)S(1)}, u32[]{:S(2)}, u32[]{:S(2)}) collective-permute-start(bf16[2,128,128]{2,1,0:T(8,128)(2,1)S(1)} %copy-done.49), channel_id=1, source_target_pairs={{0,2},{1,3},{2,0},{3,1},{4,6},{5,7},{6,4},{7,5},{8,10},{9,11},{10,... | collective-permute-start | bytes 196616 | tf_op jit(solution)/shard_map/ppermute | solution.py:930
  152.4 7.7 %collective-permute-start.36 = (bf16[2,128,128]{2,1,0:T(8,128)(2,1)S(1)}, bf16[2,128,128]{2,1,0:T(8,128)(2,1)S(1)}, u32[]{:S(2)}, u32[]{:S(2)}) collective-permute-start(bf16[2,128,128]{2,1,0:T(8,128)(2,1)S(1)} %copy-done.48), channel_id=1, source_target_pairs={{0,4},{1,5},{2,6},{3,7},{4,0},{5,1},{6,2},{7,3},{8,12},{9,13},{10,... | collective-permute-start | bytes 196616 | tf_op jit(solution)/shard_map/ppermute | solution.py:930
  153.9 6.8 %collective-permute-start.37 = (bf16[2,128,128]{2,1,0:T(8,128)(2,1)S(1)}, bf16[2,128,128]{2,1,0:T(8,128)(2,1)S(1)}, u32[]{:S(2)}, u32[]{:S(2)}) collective-permute-start(bf16[2,128,128]{2,1,0:T(8,128)(2,1)S(1)} %copy-done.46), channel_id=1, source_target_pairs={{0,6},{1,7},{2,4},{3,5},{4,2},{5,3},{6,0},{7,1},{8,14},{9,15},{10,... | collective-permute-start | bytes 196616 | tf_op jit(solution)/shard_map/ppermute | solution.py:930
  163.1 9.0 %collective-permute-start.42 = (bf16[2,128,128]{2,1,0:T(8,128)(2,1)S(1)}, bf16[2,128,128]{2,1,0:T(8,128)(2,1)S(1)}, u32[]{:S(2)}, u32[]{:S(2)}) collective-permute-start(bf16[2,128,128]{2,1,0:T(8,128)(2,1)S(1)} %copy-done.43), channel_id=1, source_target_pairs={{0,1},{1,0},{2,3},{3,2},{4,5},{5,4},{6,7},{7,6},{8,9},{9,8},{10,11... | collective-permute-start | bytes 196616 | tf_op jit(solution)/shard_map/ppermute | solution.py:948
  164.3 9.5 %collective-permute-start.43 = (bf16[2,128,128]{2,1,0:T(8,128)(2,1)S(1)}, bf16[2,128,128]{2,1,0:T(8,128)(2,1)S(1)}, u32[]{:S(2)}, u32[]{:S(2)}) collective-permute-start(bf16[2,128,128]{2,1,0:T(8,128)(2,1)S(1)} %collective-permute-done.35.refs_5_), channel_id=1, source_target_pairs={{0,1},{1,0},{2,3},{3,2},{4,5},{5,4},{6,7},{7,6},{8,9},{9,8},{10,11... | collective-permute-start | bytes 196616 | tf_op jit(solution)/shard_map/ppermute | solution.py:948
  164.3 9.7 %collective-permute-start.44 = (bf16[2,128,128]{2,1,0:T(8,128)(2,1)S(1)}, bf16[2,128,128]{2,1,0:T(8,128)(2,1)S(1)}, u32[]{:S(2)}, u32[]{:S(2)}) collective-permute-start(bf16[2,128,128]{2,1,0:T(8,128)(2,1)S(1)} %collective-permute-done.36.refs_6_), channel_id=1, source_target_pairs={{0,1},{1,0},{2,3},{3,2},{4,5},{5,4},{6,7},{7,6},{8,9},{9,8},{10,11... | collective-permute-start | bytes 196616 | tf_op jit(solution)/shard_map/ppermute | solution.py:948
  164.8 10.4 %collective-permute-start.45 = (bf16[2,128,128]{2,1,0:T(8,128)(2,1)S(1)}, bf16[2,128,128]{2,1,0:T(8,128)(2,1)S(1)}, u32[]{:S(2)}, u32[]{:S(2)}) collective-permute-start(bf16[2,128,128]{2,1,0:T(8,128)(2,1)S(1)} %collective-permute-done.37.refs_7_), channel_id=1, source_target_pairs={{0,1},{1,0},{2,3},{3,2},{4,5},{5,4},{6,7},{7,6},{8,9},{9,8},{10,11... | collective-permute-start | bytes 196616 | tf_op jit(solution)/shard_map/ppermute | solution.py:948
  165.5 25.0 %collective-permute-start.52 = (bf16[2,64,128]{2,1,0:T(8,128)(2,1)}, bf16[2,64,128]{2,1,0:T(8,128)(2,1)}, u32[]{:S(2)}, u32[]{:S(2)}) collective-permute-start(bf16[2,64,128]{2,1,0:T(8,128)(2,1)} %get-tuple-element.365), channel_id=1, source_target_pairs={{0,2},{1,3},{2,0},{3,1},{4,6},{5,7},{6,4},{7,5},{8,10},{9,11},{10,... | collective-permute-start | bytes 98312 | tf_op jit(solution)/shard_map/ppermute | solution.py:979
  166.2 52.2 %all-to-all-start.1 = ((bf16[4,1536,256]{2,1,0:T(8,128)(2,1)}), bf16[4,1536,256]{2,1,0:T(8,128)(2,1)}, u32[]{:S(2)}, u32[]{:S(2)}) async-start(bf16[4,1536,256]{2,1,0:T(8,128)(2,1)} %row_grad.1), calls=%async_computation.1 | async-start | bytes 6291456 | tf_op jit(solution)/shard_map/all_to_all | solution.py:705
  172.1 18.9 %collective-permute-start.53 = (bf16[2,64,128]{2,1,0:T(8,128)(2,1)}, bf16[2,64,128]{2,1,0:T(8,128)(2,1)}, u32[]{:S(2)}, u32[]{:S(2)}) collective-permute-start(bf16[2,64,128]{2,1,0:T(8,128)(2,1)} %get-tuple-element.367), channel_id=1, source_target_pairs={{0,4},{1,5},{2,6},{3,7},{4,0},{5,1},{6,2},{7,3},{8,12},{9,13},{10,... | collective-permute-start | bytes 98312 | tf_op jit(solution)/shard_map/ppermute | solution.py:979
  173.7 17.4 %collective-permute-start.54 = (bf16[2,64,128]{2,1,0:T(8,128)(2,1)}, bf16[2,64,128]{2,1,0:T(8,128)(2,1)}, u32[]{:S(2)}, u32[]{:S(2)}) collective-permute-start(bf16[2,64,128]{2,1,0:T(8,128)(2,1)} %get-tuple-element.366), channel_id=1, source_target_pairs={{0,6},{1,7},{2,4},{3,5},{4,2},{5,3},{6,0},{7,1},{8,14},{9,15},{10,... | collective-permute-start | bytes 98312 | tf_op jit(solution)/shard_map/ppermute | solution.py:979
  174.0 15.4 %collective-permute-start.46 = (bf16[128,1024]{1,0:T(8,128)(2,1)}, bf16[128,1024]{1,0:T(8,128)(2,1)}, u32[]{:S(2)}, u32[]{:S(2)}) collective-permute-start(bf16[128,1024]{1,0:T(8,128)(2,1)} %get-tuple-element.285), channel_id=1, source_target_pairs={{0,6},{1,7},{2,4},{3,5},{4,2},{5,3},{6,0},{7,1},{8,14},{9,15},{10,... | collective-permute-start | bytes 786440 | tf_op jit(solution)/shard_map/ppermute | solution.py:950
  189.4 4.3 %collective-permute-start.47 = (bf16[128,1024]{1,0:T(8,128)(2,1)}, bf16[128,1024]{1,0:T(8,128)(2,1)S(1)}, u32[]{:S(2)}, u32[]{:S(2)}) collective-permute-start(bf16[128,1024]{1,0:T(8,128)(2,1)} %get-tuple-element.286.refs_11_), channel_id=1, source_target_pairs={{0,1},{1,0},{2,3},{3,2},{4,5},{5,4},{6,7},{7,6},{8,9},{9,8},{10,11... | collective-permute-start | bytes 786440 | tf_op jit(solution)/shard_map/ppermute | solution.py:976
  190.5 3.2 %collective-permute-start.48 = (bf16[128,1024]{1,0:T(8,128)(2,1)}, bf16[128,1024]{1,0:T(8,128)(2,1)S(1)}, u32[]{:S(2)}, u32[]{:S(2)}) collective-permute-start(bf16[128,1024]{1,0:T(8,128)(2,1)} %get-tuple-element.287.refs_12_), channel_id=1, source_target_pairs={{0,1},{1,0},{2,3},{3,2},{4,5},{5,4},{6,7},{7,6},{8,9},{9,8},{10,11... | collective-permute-start | bytes 786440 | tf_op jit(solution)/shard_map/ppermute | solution.py:976
  190.5 3.2 %collective-permute-start.49 = (bf16[128,1024]{1,0:T(8,128)(2,1)}, bf16[128,1024]{1,0:T(8,128)(2,1)S(1)}, u32[]{:S(2)}, u32[]{:S(2)}) collective-permute-start(bf16[128,1024]{1,0:T(8,128)(2,1)} %get-tuple-element.288.refs_13_), channel_id=1, source_target_pairs={{0,1},{1,0},{2,3},{3,2},{4,5},{5,4},{6,7},{7,6},{8,9},{9,8},{10,11... | collective-permute-start | bytes 786440 | tf_op jit(solution)/shard_map/ppermute | solution.py:976
  191.1 27.4 %collective-permute-start.55 = (bf16[1024,256]{1,0:T(8,128)(2,1)S(1)}, bf16[1024,256]{1,0:T(8,128)(2,1)S(1)}, u32[]{:S(2)}, u32[]{:S(2)}) collective-permute-start(bf16[1024,256]{1,0:T(8,128)(2,1)S(1)} %copy-done.12), channel_id=1, source_target_pairs={{0,24},{8,16},{16,8},{24,0},{1,25},{9,17},{17,9},{25,1},{2,26},{10... | collective-permute-start | bytes 1572872 | tf_op jit(solution)/shard_map/ppermute | solution.py:947
  198.7 19.8 %collective-permute-start.56 = (bf16[128,1024]{1,0:T(8,128)(2,1)}, bf16[128,1024]{1,0:T(8,128)(2,1)S(1)}, u32[]{:S(2)}, u32[]{:S(2)}) collective-permute-start(bf16[128,1024]{1,0:T(8,128)(2,1)} %get-tuple-element.310), channel_id=1, source_target_pairs={{0,2},{1,3},{2,0},{3,1},{4,6},{5,7},{6,4},{7,5},{8,10},{9,11},{10,... | collective-permute-start | bytes 786440 | tf_op jit(solution)/shard_map/ppermute | solution.py:983
  200.0 18.5 %collective-permute-start.57 = (bf16[128,1024]{1,0:T(8,128)(2,1)}, bf16[128,1024]{1,0:T(8,128)(2,1)}, u32[]{:S(2)}, u32[]{:S(2)}) collective-permute-start(bf16[128,1024]{1,0:T(8,128)(2,1)} %get-tuple-element.311), channel_id=1, source_target_pairs={{0,4},{1,5},{2,6},{3,7},{4,0},{5,1},{6,2},{7,3},{8,12},{9,13},{10,... | collective-permute-start | bytes 786440 | tf_op jit(solution)/shard_map/ppermute | solution.py:983
  218.5 28.9 %all-to-all-start.2 = ((bf16[4,704,256]{2,1,0:T(8,128)(2,1)}), bf16[4,704,256]{2,1,0:T(8,128)(2,1)S(1)}, u32[]{:S(2)}, u32[]{:S(2)}) async-start(bf16[4,704,256]{2,1,0:T(8,128)(2,1)} %self_grad.1), calls=%async_computation.2 | async-start | bytes 2883584 | tf_op jit(solution)/shard_map/all_to_all | solution.py:705
  228.3 7.7 %collective-permute-start.58 = (bf16[384,256]{1,0:T(8,128)(2,1)S(1)}, bf16[384,256]{1,0:T(8,128)(2,1)S(1)}, u32[]{:S(2)}, u32[]{:S(2)}) collective-permute-start(bf16[384,256]{1,0:T(8,128)(2,1)S(1)} %get-tuple-element.352), channel_id=1, source_target_pairs={{0,2},{1,3},{2,0},{3,1},{4,6},{5,7},{6,4},{7,5},{8,10},{9,11},{10,... | collective-permute-start | bytes 589832 | tf_op jit(solution)/shard_map/ppermute | solution.py:1011
  229.1 8.4 %collective-permute-start.59 = (bf16[384,256]{1,0:T(8,128)(2,1)S(1)}, bf16[384,256]{1,0:T(8,128)(2,1)S(1)}, u32[]{:S(2)}, u32[]{:S(2)}) collective-permute-start(bf16[384,256]{1,0:T(8,128)(2,1)S(1)} %get-tuple-element.351), channel_id=1, source_target_pairs={{0,4},{1,5},{2,6},{3,7},{4,0},{5,1},{6,2},{7,3},{8,12},{9,13},{10,... | collective-permute-start | bytes 589832 | tf_op jit(solution)/shard_map/ppermute | solution.py:1011
  230.1 17.4 %collective-permute-start.60 = (bf16[384,256]{1,0:T(8,128)(2,1)S(1)}, bf16[384,256]{1,0:T(8,128)(2,1)S(1)}, u32[]{:S(2)}, u32[]{:S(2)}) collective-permute-start(bf16[384,256]{1,0:T(8,128)(2,1)S(1)} %get-tuple-element.350), channel_id=1, source_target_pairs={{0,6},{1,7},{2,4},{3,5},{4,2},{5,3},{6,0},{7,1},{8,14},{9,15},{10,... | collective-permute-start | bytes 589832 | tf_op jit(solution)/shard_map/ppermute | solution.py:1011
  249.6 34.4 %all-to-all-start.3 = ((bf16[4,1024,256]{2,1,0:T(8,128)(2,1)}), bf16[4,1024,256]{2,1,0:T(8,128)(2,1)S(1)}, u32[]{:S(2)}, u32[]{:S(2)}) async-start(bf16[4,1024,256]{2,1,0:T(8,128)(2,1)} %broadcast_in_dim.23), calls=%async_computation.3 | async-start | bytes 4194304 | tf_op jit(solution)/shard_map/all_to_all | solution.py:690
  253.6 3.4 %collective-permute-start.61 = (bf16[80,512]{1,0:T(8,128)(2,1)S(1)}, bf16[80,512]{1,0:T(8,128)(2,1)S(1)}, u32[]{:S(2)}, u32[]{:S(2)}) collective-permute-start(bf16[80,512]{1,0:T(8,128)(2,1)S(1)} %constant_dynamic-slice_fusion), channel_id=1, source_target_pairs={{0,1},{1,0},{2,3},{3,2},{4,5},{5,4},{6,7},{7,6},{8,9},{9,8},{10,11... | collective-permute-start | bytes 245768 | tf_op jit(solution)/shard_map/ppermute | solution.py:1054
  256.1 16.7 %collective-permute-start.65 = (bf16[128,1024]{1,0:T(8,128)(2,1)S(1)}, bf16[128,1024]{1,0:T(8,128)(2,1)S(1)}, u32[]{:S(2)}, u32[]{:S(2)}) collective-permute-start(bf16[128,1024]{1,0:T(8,128)(2,1)S(1)} %copy-done.40), channel_id=1, source_target_pairs={{0,6},{1,7},{2,4},{3,5},{4,2},{5,3},{6,0},{7,1},{8,14},{9,15},{10,... | collective-permute-start | bytes 786440 | tf_op jit(solution)/shard_map/ppermute | solution.py:1030
  257.1 20.8 %collective-permute-start.62 = (bf16[80,512]{1,0:T(8,128)(2,1)S(1)}, bf16[80,512]{1,0:T(8,128)(2,1)S(1)}, u32[]{:S(2)}, u32[]{:S(2)}) collective-permute-start(bf16[80,512]{1,0:T(8,128)(2,1)S(1)} %add_convert_fusion.8), channel_id=1, source_target_pairs={{0,2},{1,3},{2,0},{3,1},{4,6},{5,7},{6,4},{7,5},{8,10},{9,11},{10,... | collective-permute-start | bytes 245768 | tf_op jit(solution)/shard_map/ppermute | solution.py:1055
  257.1 20.7 %collective-permute-start.63 = (bf16[80,512]{1,0:T(8,128)(2,1)S(1)}, bf16[80,512]{1,0:T(8,128)(2,1)S(1)}, u32[]{:S(2)}, u32[]{:S(2)}) collective-permute-start(bf16[80,512]{1,0:T(8,128)(2,1)S(1)} %add_convert_fusion.8), channel_id=1, source_target_pairs={{0,4},{1,5},{2,6},{3,7},{4,0},{5,1},{6,2},{7,3},{8,12},{9,13},{10,... | collective-permute-start | bytes 245768 | tf_op jit(solution)/shard_map/ppermute | solution.py:1055
  258.9 19.0 %collective-permute-start.64 = (bf16[80,512]{1,0:T(8,128)(2,1)S(1)}, bf16[80,512]{1,0:T(8,128)(2,1)S(1)}, u32[]{:S(2)}, u32[]{:S(2)}) collective-permute-start(bf16[80,512]{1,0:T(8,128)(2,1)S(1)} %add_convert_fusion.8), channel_id=1, source_target_pairs={{0,6},{1,7},{2,4},{3,5},{4,2},{5,3},{6,0},{7,1},{8,14},{9,15},{10,... | collective-permute-start | bytes 245768 | tf_op jit(solution)/shard_map/ppermute | solution.py:1055
  (61 other events, 504.1 us)
